TPU v7x, 32 devices: a whole 2x2x4 slice. The times are simulated.
32 devices in a mesh: dp: 16 (over z, x, core), mp: 2 (over y).
Axes of the slice: x: 2, y: 2, z: 4, core: 2. Of those that a mesh axis runs over, the one named last changes fastest.
Arguments:
- tokens_in: bfloat16 [32768, 1024], P('dp'), may hold values from -6 to 6
- cotangent: bfloat16 [32768, 1024], P(('dp', 'mp')), may hold values from -6 to 6
- segment_ids: int32 [64, 512], P('dp'), may hold values from 0 to 3, never falling along the last dimension, each value on 1 to 256 neighbouring positions
- project_weight: float32 [3, 1024, 1024], P(None, 'dp', 'mp'), may hold values from -0.25 to 0.25
- project_momentum: float32 [3, 1024, 1024], P(None, 'dp', 'mp'), may hold values from -1536 to 1536
- project_squares: float32 [3, 1024, 1024], P(None, 'dp', 'mp'), may hold values from 32768 to 524288
- output_weight: float32 [1024, 1024], P('dp', 'mp'), may hold values from -0.75 to 0.75
- output_momentum: float32 [1024, 1024], P('dp', 'mp'), may hold values from -256 to 256
- output_squares: float32 [1024, 1024], P('dp', 'mp'), may hold values from 983.04 to 16384
- up_weight: float32 [1024, 4096], P('dp', 'mp'), may hold values from -0.1875 to 0.1875
- up_momentum: float32 [1024, 4096], P('dp', 'mp'), may hold values from -320 to 320
- up_squares: float32 [1024, 4096], P('dp', 'mp'), may hold values from 1638.4 to 26214.4
- down_weight: float32 [1024, 4096], P('dp', 'mp'), may hold values from -0.09375 to 0.09375
- down_momentum: float32 [1024, 4096], P('dp', 'mp'), may hold values from -640 to 640
- down_squares: float32 [1024, 4096], P('dp', 'mp'), may hold values from 6553.6 to 98304
- norm_params: float32 [4, 1024], P(None, ('dp', 'mp')), as said below
- norm_momentum: float32 [4, 1024], P(None, ('dp', 'mp')), may hold values from -1024 to 1024
- norm_squares: float32 [4, 1024], P(None, ('dp', 'mp')), may hold values from 16384 to 262144
Outputs:
- layer_out: bfloat16 [32768, 1024], P(('dp', 'mp'))
- input_grad: float32 [32768, 1024], P(('dp', 'mp'))
- project_grad: float32 [3, 1024, 1024], P(None, 'dp', 'mp')
- project_moment: float32 [3, 1024, 1024], P(None, 'dp', 'mp')
- project_square: float32 [3, 1024, 1024], P(None, 'dp', 'mp')
- project_updated: float32 [3, 1024, 1024], P(None, 'dp', 'mp')
- output_grad: float32 [1024, 1024], P('dp', 'mp')
- output_moment: float32 [1024, 1024], P('dp', 'mp')
- output_square: float32 [1024, 1024], P('dp', 'mp')
- output_updated: float32 [1024, 1024], P('dp', 'mp')
- up_grad: float32 [1024, 4096], P('dp', 'mp')
- up_moment: float32 [1024, 4096], P('dp', 'mp')
- up_square: float32 [1024, 4096], P('dp', 'mp')
- up_updated: float32 [1024, 4096], P('dp', 'mp')
- down_grad: float32 [1024, 4096], P('dp', 'mp')
- down_moment: float32 [1024, 4096], P('dp', 'mp')
- down_square: float32 [1024, 4096], P('dp', 'mp')
- down_updated: float32 [1024, 4096], P('dp', 'mp')
- norm_grad: float32 [4, 1024], P(None, ('dp', 'mp'))
- norm_moment: float32 [4, 1024], P(None, ('dp', 'mp'))
- norm_square: float32 [4, 1024], P(None, ('dp', 'mp'))
- norm_updated: float32 [4, 1024], P(None, ('dp', 'mp'))
Inputs may be any that keep to these rules, and one draw needn't show every extreme that they name: `segment_ids`: along each row the segment number never falls; a segment holds 1 to 256 tokens, and in every row one holds exactly that many. `norm_params`: gains lie in 0.6 to 1.4 and shifts in -0.3 to 0.3.
All inputs are finite; a program needn't handle non-finite values.
Results may differ from a plain program's by a relative error of at most 0.02.
The roundings to bfloat16 on the way count: a program that leaves them out, or rounds other values in their place, can miss the bound.
Values may be sent and summed in bfloat16 or wider, within the bound.
A program may use at most 256 MiB of HBM per device.

v0:
```python
import jax
import jax.numpy as jnp
from jax import lax
from jax.sharding import PartitionSpec as P

D = 1024
HEAD_DIM = 64
FF = 4096
STEP = 3


EPS_NORM = 1e-12
NEG_FILL = -1e30
BETA_ONE = 0.5
BETA_TWO = 0.5
ADAM_EPS = 1e-08
DECAY_RATE = 0.01


def layer_norm(values, norm_gain, norm_shift):
    center = values - jnp.mean(values, axis=-1, keepdims=True)
    spread = jnp.mean(center * center, axis=-1, keepdims=True)
    return center * lax.rsqrt(spread + EPS_NORM) * norm_gain + norm_shift


def exact_gelu(values):
    return jax.nn.gelu(values, approximate=False)


def adam_step(gradient, weight, first_old, second, step_rate):
    correct_one = 1.0 - BETA_ONE**STEP
    correct_two = 1.0 - BETA_TWO**STEP
    moment = BETA_ONE * first_old + (1.0 - BETA_ONE) * gradient
    square = BETA_TWO * second + (1.0 - BETA_TWO) * gradient * gradient
    normed = moment / correct_one / (jnp.sqrt(square / correct_two) + ADAM_EPS)
    updated = weight - step_rate * (normed + DECAY_RATE * weight)
    return (gradient, moment, square, updated)


def local(
    tokens_in,
    cotangent,
    segment_ids,
    project_weight,
    project_momentum,
    project_squares,
    output_weight,
    output_momentum,
    output_squares,
    up_weight,
    up_momentum,
    up_squares,
    down_weight,
    down_momentum,
    down_squares,
    norm_params,
    norm_momentum,
    norm_squares,
):
    gathered = (
        lax.all_gather(project_weight.astype(jnp.bfloat16), "dp", axis=1, tiled=True),
        lax.all_gather(output_weight.astype(jnp.bfloat16), "dp", axis=0, tiled=True),
        lax.all_gather(up_weight.astype(jnp.bfloat16), "dp", axis=0, tiled=True),
        lax.all_gather(down_weight.astype(jnp.bfloat16), "dp", axis=0, tiled=True),
    )
    proj_copy, out_copy, up_copy, down_copy = gathered
    norm_full = lax.all_gather(
        norm_params.astype(jnp.bfloat16), ("dp", "mp"), axis=1, tiled=True
    ).astype(jnp.float32)
    rows_here = segment_ids.shape[0]
    seq_len = segment_ids.shape[1]
    local_width = proj_copy.shape[2]
    heads_here = local_width // HEAD_DIM
    score_scale = HEAD_DIM ** (-0.5)
    projected = jnp.einsum(
        "tc,scn->stn", tokens_in, proj_copy, preferred_element_type=jnp.float32
    ).astype(jnp.bfloat16)
    heads_split = projected.reshape(3, rows_here, seq_len, heads_here, HEAD_DIM)

    def masked_scores(query_rows, key_rows, row_segments):
        scores = (
            jnp.einsum("qhd,khd->hqk", query_rows, key_rows, preferred_element_type=jnp.float32)
            * score_scale
        )
        same_doc = row_segments[:, None] == row_segments[None, :]
        return jnp.where(same_doc[None], scores, NEG_FILL)

    def row_forward(packed):
        query_rows, key_rows, value_rows, row_segments = packed
        scores = masked_scores(query_rows, key_rows, row_segments)
        row_max = jnp.max(scores, axis=-1, keepdims=True)
        row_exp = jnp.exp(scores - row_max)
        row_total = jnp.sum(row_exp, axis=-1, keepdims=True)
        row_probs = (row_exp / row_total).astype(jnp.bfloat16)
        mixed = jnp.einsum(
            "hqk,khd->qhd", row_probs, value_rows, preferred_element_type=jnp.float32
        )
        row_lse = (row_max + jnp.log(row_total))[..., 0]
        return (mixed.astype(jnp.bfloat16).reshape(seq_len, local_width), row_lse)

    context_rows, lse_rows = lax.map(
        row_forward, (heads_split[0], heads_split[1], heads_split[2], segment_ids)
    )
    context = context_rows.reshape(rows_here * seq_len, local_width)
    attn_part = jnp.einsum("tn,dn->td", context, out_copy, preferred_element_type=jnp.float32)
    attn_share = lax.psum_scatter(
        attn_part.astype(jnp.bfloat16), "mp", scatter_dimension=0, tiled=True
    ).astype(jnp.float32)
    share_rows = attn_share.shape[0]
    share_start = lax.axis_index("mp") * share_rows
    token_share = lax.dynamic_slice_in_dim(tokens_in, share_start, share_rows, 0).astype(
        jnp.float32
    )
    hidden_one, norm_one_back = jax.vjp(
        layer_norm, token_share + attn_share, norm_full[0], norm_full[1]
    )
    hidden_low = lax.all_gather(hidden_one.astype(jnp.bfloat16), "mp", axis=0, tiled=True)
    pre_act = jnp.dot(hidden_low, up_copy, preferred_element_type=jnp.float32)
    act_full, gelu_back = jax.vjp(exact_gelu, pre_act)
    act_low = act_full.astype(jnp.bfloat16)
    ffn_part = jnp.einsum("tf,df->td", act_low, down_copy, preferred_element_type=jnp.float32)
    ffn_share = lax.psum_scatter(
        ffn_part.astype(jnp.bfloat16), "mp", scatter_dimension=0, tiled=True
    ).astype(jnp.float32)
    result, norm_two_back = jax.vjp(layer_norm, hidden_one + ffn_share, norm_full[2], norm_full[3])
    layer_out = result.astype(jnp.bfloat16)
    regathered = (
        lax.all_gather(project_weight.astype(jnp.bfloat16), "dp", axis=1, tiled=True),
        lax.all_gather(output_weight.astype(jnp.bfloat16), "dp", axis=0, tiled=True),
        lax.all_gather(up_weight.astype(jnp.bfloat16), "dp", axis=0, tiled=True),
        lax.all_gather(down_weight.astype(jnp.bfloat16), "dp", axis=0, tiled=True),
    )
    proj_copy, out_copy, up_copy, down_copy = regathered
    d_resid_two, d_gain_two, d_shift_two = norm_two_back(cotangent.astype(jnp.float32))
    d_ffn = lax.all_gather(d_resid_two.astype(jnp.bfloat16), "mp", axis=0, tiled=True)
    down_grad = jnp.einsum("td,tf->df", d_ffn, act_low, preferred_element_type=jnp.float32)
    d_act = jnp.dot(d_ffn, down_copy, preferred_element_type=jnp.float32)
    d_pre = gelu_back(d_act)[0].astype(jnp.bfloat16)
    up_grad = jnp.einsum("tc,tf->cf", hidden_low, d_pre, preferred_element_type=jnp.float32)
    d_hidden_part = jnp.einsum("tf,cf->tc", d_pre, up_copy, preferred_element_type=jnp.float32)
    d_hidden = d_resid_two + lax.psum_scatter(
        d_hidden_part.astype(jnp.bfloat16), "mp", scatter_dimension=0, tiled=True
    ).astype(jnp.float32)
    d_resid_one, d_gain_one, d_shift_one = norm_one_back(d_hidden)
    d_attn = lax.all_gather(d_resid_one.astype(jnp.bfloat16), "mp", axis=0, tiled=True)
    output_grad = jnp.einsum("td,tn->dn", d_attn, context, preferred_element_type=jnp.float32)
    d_context = jnp.dot(d_attn, out_copy, preferred_element_type=jnp.float32).astype(jnp.bfloat16)

    def row_backward(packed):
        query_rows, key_rows, value_rows, row_segments, row_lse, row_grad = packed
        scores = masked_scores(query_rows, key_rows, row_segments)
        row_probs = jnp.exp(scores - row_lse[..., None])
        grad_heads = row_grad.reshape(seq_len, heads_here, HEAD_DIM)
        d_probs = jnp.einsum(
            "qhd,khd->hqk", grad_heads, value_rows, preferred_element_type=jnp.float32
        )
        row_inner = jnp.sum(d_probs * row_probs, axis=-1, keepdims=True)
        d_scores = (row_probs * (d_probs - row_inner)).astype(jnp.bfloat16)
        d_value = jnp.einsum(
            "hqk,qhd->khd",
            row_probs.astype(jnp.bfloat16),
            grad_heads,
            preferred_element_type=jnp.float32,
        )
        d_query = (
            jnp.einsum("hqk,khd->qhd", d_scores, key_rows, preferred_element_type=jnp.float32)
            * score_scale
        )
        d_key = (
            jnp.einsum("hqk,qhd->khd", d_scores, query_rows, preferred_element_type=jnp.float32)
            * score_scale
        )
        return (
            d_query.astype(jnp.bfloat16).reshape(seq_len, local_width),
            d_key.astype(jnp.bfloat16).reshape(seq_len, local_width),
            d_value.astype(jnp.bfloat16).reshape(seq_len, local_width),
        )

    grad_context_rows = d_context.reshape(rows_here, seq_len, local_width)
    d_rows = lax.map(
        row_backward,
        (heads_split[0], heads_split[1], heads_split[2], segment_ids, lse_rows, grad_context_rows),
    )
    d_proj = jnp.stack(d_rows).reshape(3, rows_here * seq_len, local_width)
    project_grad = jnp.einsum("tc,stn->scn", tokens_in, d_proj, preferred_element_type=jnp.float32)
    d_input_part = jnp.einsum("stn,scn->tc", d_proj, proj_copy, preferred_element_type=jnp.float32)
    input_grad = d_resid_one + lax.psum_scatter(
        d_input_part.astype(jnp.bfloat16), "mp", scatter_dimension=0, tiled=True
    ).astype(jnp.float32)
    norm_local = jnp.stack([d_gain_one, d_shift_one, d_gain_two, d_shift_two])
    norm_red = lax.psum_scatter(norm_local, ("dp", "mp"), scatter_dimension=1, tiled=True)
    proj_red, out_red, up_red, down_red = (
        lax.psum_scatter(
            project_grad.astype(jnp.bfloat16), "dp", scatter_dimension=1, tiled=True
        ).astype(jnp.float32),
        lax.psum_scatter(
            output_grad.astype(jnp.bfloat16), "dp", scatter_dimension=0, tiled=True
        ).astype(jnp.float32),
        lax.psum_scatter(
            up_grad.astype(jnp.bfloat16), "dp", scatter_dimension=0, tiled=True
        ).astype(jnp.float32),
        lax.psum_scatter(
            down_grad.astype(jnp.bfloat16), "dp", scatter_dimension=0, tiled=True
        ).astype(jnp.float32),
    )
    proj_new = adam_step(proj_red, project_weight, project_momentum, project_squares, D ** (-0.5))
    out_new = adam_step(out_red, output_weight, output_momentum, output_squares, 4.0 * D ** (-0.5))
    up_new = adam_step(up_red, up_weight, up_momentum, up_squares, D ** (-0.5))
    down_new = adam_step(down_red, down_weight, down_momentum, down_squares, FF ** (-0.5))
    norm_new = adam_step(norm_red, norm_params, norm_momentum, norm_squares, 0.3)
    return (
        layer_out,
        input_grad,
        proj_new[0],
        proj_new[1],
        proj_new[2],
        proj_new[3],
        out_new[0],
        out_new[1],
        out_new[2],
        out_new[3],
        up_new[0],
        up_new[1],
        up_new[2],
        up_new[3],
        down_new[0],
        down_new[1],
        down_new[2],
        down_new[3],
        norm_new[0],
        norm_new[1],
        norm_new[2],
        norm_new[3],
    )


def solution(mesh):
    return jax.shard_map(
        local,
        mesh=mesh,
        in_specs=(
            P("dp", None),
            P(("dp", "mp"), None),
            P("dp", None),
            P(None, "dp", "mp"),
            P(None, "dp", "mp"),
            P(None, "dp", "mp"),
            P("dp", "mp"),
            P("dp", "mp"),
            P("dp", "mp"),
            P("dp", "mp"),
            P("dp", "mp"),
            P("dp", "mp"),
            P("dp", "mp"),
            P("dp", "mp"),
            P("dp", "mp"),
            P(None, ("dp", "mp")),
            P(None, ("dp", "mp")),
            P(None, ("dp", "mp")),
        ),
        out_specs=(
            P(("dp", "mp"), None),
            P(("dp", "mp"), None),
            P(None, "dp", "mp"),
            P(None, "dp", "mp"),
            P(None, "dp", "mp"),
            P(None, "dp", "mp"),
            P("dp", "mp"),
            P("dp", "mp"),
            P("dp", "mp"),
            P("dp", "mp"),
            P("dp", "mp"),
            P("dp", "mp"),
            P("dp", "mp"),
            P("dp", "mp"),
            P("dp", "mp"),
            P("dp", "mp"),
            P("dp", "mp"),
            P("dp", "mp"),
            P(None, ("dp", "mp")),
            P(None, ("dp", "mp")),
            P(None, ("dp", "mp")),
            P(None, ("dp", "mp")),
        ),
        check_vma=False,
    )
```

profile of v0, /device:TPU:0, one launch (start us, length us, event | category | flops | bytes accessed | tf_op | source)
XLA Modules:
  0.0 1195.5 jit_solution(12602901372234016294)
XLA Ops:
  10.6 48.1 %all-gather.9.cloned.1.call-done = bf16[3,1024,512]{2,1,0:T(8,128)(2,1)} async-done(((bf16[3,64,512]{2,1,0:T(8,128)(2,1)}), bf16[3,1024,512]{2,1,0:T(8,128)(2,1)}) %all-gather.9.cloned.1.call-update) | async-done | bytes 3145744 | tf_op jit(solution)/shard_map/all_gather | solution.py:61
  58.7 9.6 convert_bitcast_fusion
  68.4 3.0 fusion.79
  71.3 2.7 squeeze.39
  76.1 4.5 squeeze.40
  80.6 3.5 copy.119
  84.1 4.5 squeeze.41
  88.5 3.4 copy.120
  93.4 38.3 %while.26 = (s32[]{:T(128)}, bf16[4,512,512]{2,1,0:T(8,128)(2,1)}, f32[4,8,512]{2,1,0:T(8,128)}, bf16[4,512,8,64]{1,3,2,0:T(8,128)(2,1)S(1)}, s32[4,512]{1,0:T(4...) while((s32[]{:T(128)}, bf16[4,512,512]{2,1,0:T(8,128)(2,1)}, ...), condition=%wide.region_3.4_spmd, body=%wide.region_0.3_spmd.sunk | while | flops 562556928 | bytes 30548060 | solution.py:101
  94.3 2.7 fusion.123
  103.8 2.7 fusion.123
  113.4 2.7 fusion.123
  122.9 2.7 fusion.123
  131.8 7.0 convolution_convert_fusion.4
  140.6 66.3 %all-gather = bf16[32,32,4]{1,2,0:T(4,128)(2,1)S(1)} all-gather(bf16[1,32,4]{1,2,0:T(4,128)(2,1)S(1)} %convert_bitcast_fusion.2), channel_id=1, replica_groups=mesh['dp'=16,'mp'=2] {'dp','mp'}, dimensions={0}, use_global_device_ids=true | all-gather | bytes 8448 | tf_op jit(solution)/shard_map/all_gather | solution.py:67
  207.1 3.0 fusion.56
  210.1 2.6 multiply_reduce_fusion.4
  216.6 29.5 %all-gather.15.cloned.1.call-done = bf16[1024,2048]{1,0:T(8,128)(2,1)} async-done(((bf16[64,2048]{1,0:T(8,128)(2,1)}), bf16[1024,2048]{1,0:T(8,128)(2,1)}) %all-gather.15.cloned.1.call-update) | async-done | bytes 4194320 | tf_op jit(solution)/shard_map/all_gather | solution.py:63
  246.1 57.3 %all-gather.13.cloned.1.call-done = bf16[2048,1024]{1,0:T(8,128)(2,1)} async-done(((bf16[1024,1024]{1,0:T(8,128)(2,1)}), bf16[2048,1024]{1,0:T(8,128)(2,1)}) %all-gather.13.cloned.1.call-update) | async-done | bytes 4194320 | tf_op jit(solution)/shard_map/all_gather | solution.py:117
  303.4 48.8 %multiply_convert_fusion.1 = (bf16[2048,2048]{1,0:T(8,128)(2,1)}, f32[2048,2048]{1,0:T(8,128)}, f32[2048,2048]{1,0:T(8,128)}) fusion(bf16[2048,1024]{1,0:T(8,128)(2,1)} %all-gather.13.cloned.1.call-done, bf16[1024,2048]{1,0:T(8,128)(2,1)} %all-gather.15.cloned.1.call-done), kind=kOutput, calls=%fused_computation.61 | convolution fusion | flops 8862564352 | bytes 50331648 | tf_op jit(solution)/shard_map/dot_general | solution.py:118
  352.2 4.7 all-gather.17.cloned.1.call-done
  356.8 13.8 %convolution_convert_fusion.3 = bf16[2048,1024]{1,0:T(8,128)(2,1)} fusion(bf16[2048,2048]{1,0:T(8,128)(2,1)} %get-tuple-element.318, bf16[1024,2048]{1,0:T(8,128)(2,1)} %all-gather.17.cloned.1.call-done), kind=kOutput, calls=%fused_computation.107 | convolution fusion | flops 8592031744 | bytes 16777216 | tf_op jit(solution)/shard_map/tf,df->td/dot_general | solution.py:121
  370.7 52.9 %reduce-scatter.13.cloned.1.call-done = bf16[1024,1024]{1,0:T(8,128)(2,1)} async-done(((bf16[2048,1024]{1,0:T(8,128)(2,1)}), bf16[1024,1024]{1,0:T(8,128)(2,1)}) %reduce-scatter.13.cloned.1.call-update) | async-done | bytes 2097168 | tf_op jit(solution)/shard_map/reduce_scatter | solution.py:122
  423.7 13.5 %fusion.77 = (f32[1024]{0:T(1024)S(1)}, f32[1024,1024]{1,0:T(8,128)S(1)}) fusion(bf16[1024,1024]{1,0:T(8,128)(2,1)} %reduce-scatter.13.cloned.1.call-done, f32[1024]{0:T(1024)S(1)} %bitcast.181, f32[1024]{0:T(1024)S(1)} %bitcast.176, f32[1024]{0:T(1024)S(1)} %fusion.64, f32[1024]{0:T(1024)S(1)} %broadcast_multiply_fusion.1, ...), kind=kLoop, calls=%fused_computation.153 | loop fusion | flops 10484736 | bytes 10506244 | tf_op jit(solution)/shard_map/jvp()/reduce_sum | solution.py:21
  440.7 3.2 fusion.76
  447.5 56.9 %all-gather.19.cloned.1.call-done = bf16[2048,1024]{1,0:T(8,128)(2,1)} async-done(((bf16[1024,1024]{1,0:T(8,128)(2,1)}), bf16[2048,1024]{1,0:T(8,128)(2,1)}) %all-gather.19.cloned.1.call-update) | async-done | bytes 4194320 | tf_op jit(solution)/shard_map/all_gather | solution.py:135
  504.4 26.4 %add_convert_fusion = bf16[2048,2048]{1,0:T(8,128)(2,1)} fusion(f32[2048,2048]{1,0:T(8,128)} %get-tuple-element.319, f32[2048,2048]{1,0:T(8,128)} %get-tuple-element.334, bf16[2048,1024]{1,0:T(8,128)(2,1)} %all-gather.19.cloned.1.call-done, bf16[1024,2048]{1,0:T(8,128)(2,1)} %all-gather.17.cloned.1.call-done), kind=kOutput, calls=%fused_computation.60 | convolution fusion | flops 8648654848 | bytes 50331648 | tf_op jit(solution)/shard_map/dot_general | solution.py:137
  530.8 13.9 %convolution_convert_fusion.2 = bf16[2048,1024]{1,0:T(8,128)(2,1)} fusion(bf16[2048,2048]{1,0:T(8,128)(2,1)} %add_convert_fusion, bf16[1024,2048]{1,0:T(8,128)(2,1)} %all-gather.15.cloned.1.call-done), kind=kOutput, calls=%fused_computation.106 | convolution fusion | flops 8592031744 | bytes 16777216 | tf_op jit(solution)/shard_map/tf,cf->tc/dot_general | solution.py:140
  544.7 54.4 %reduce-scatter.15.cloned.1.call-done = bf16[1024,1024]{1,0:T(8,128)(2,1)} async-done(((bf16[2048,1024]{1,0:T(8,128)(2,1)}), bf16[1024,1024]{1,0:T(8,128)(2,1)}) %reduce-scatter.15.cloned.1.call-update) | async-done | bytes 2097168 | tf_op jit(solution)/shard_map/reduce_scatter | solution.py:141
  599.1 5.5 multiply_reduce_fusion.1
  611.8 14.1 %convolution_convert_fusion = bf16[1024,2048]{1,0:T(8,128)(2,1)} fusion(bf16[2048,1024]{1,0:T(8,128)(2,1)} %all-gather.19.cloned.1.call-done, bf16[2048,2048]{1,0:T(8,128)(2,1)} %get-tuple-element.318), kind=kOutput, calls=%fused_computation.104 | convolution fusion | flops 8592031744 | bytes 16777216 | tf_op jit(solution)/shard_map/td,tf->df/dot_general | solution.py:136
  626.0 14.1 %convolution_convert_fusion.1 = bf16[1024,2048]{1,0:T(8,128)(2,1)} fusion(bf16[2048,1024]{1,0:T(8,128)(2,1)} %all-gather.13.cloned.1.call-done, bf16[2048,2048]{1,0:T(8,128)(2,1)} %add_convert_fusion), kind=kOutput, calls=%fused_computation.105 | convolution fusion | flops 8592031744 | bytes 16777216 | tf_op jit(solution)/shard_map/tc,tf->cf/dot_general | solution.py:139
  641.3 27.4 %all-gather.21.cloned.1.call-done = bf16[2048,1024]{1,0:T(8,128)(2,1)} async-done(((bf16[1024,1024]{1,0:T(8,128)(2,1)}), bf16[2048,1024]{1,0:T(8,128)(2,1)}) %all-gather.21.cloned.1.call-update) | async-done | bytes 4194320 | tf_op jit(solution)/shard_map/all_gather | solution.py:145
  668.7 5.9 convolution_convert_fusion.5
  679.0 135.8 %while.27 = (s32[]{:T(128)}, bf16[4,512,512]{2,1,0:T(8,128)(2,1)}, bf16[4,512,512]{2,1,0:T(8,128)(2,1)}, bf16[4,512,512]{2,1,0:T(8,128)(2,1)}, bf16[4,512,8,64]{...) while((s32[]{:T(128)}, bf16[4,512,512]{2,1,0:T(8,128)(2,1)}, ...), condition=%wide.region_17.18_spmd, body=%wide.region_15.17_spmd.sunk | while | flops 1375203328 | bytes 119662280 | solution.py:180
  679.2 5.8 fusion.135
  688.0 5.6 multiply_reduce_fusion.6
  694.8 2.6 multiply_convert_fusion.3
  702.1 5.8 fusion.137
  709.2 3.1 fusion.136
  713.4 5.8 fusion.135
  722.1 5.3 multiply_reduce_fusion.6
  728.4 2.6 multiply_convert_fusion.3
  735.7 5.6 fusion.137
  742.5 3.2 fusion.136
  746.7 5.8 fusion.135
  755.5 5.6 multiply_reduce_fusion.6
  762.4 2.6 multiply_convert_fusion.3
  769.7 5.5 fusion.137
  776.5 3.7 fusion.136
  781.2 5.8 fusion.135
  790.0 5.2 multiply_reduce_fusion.6
  796.3 2.6 multiply_convert_fusion.3
  803.6 5.7 fusion.137
  810.6 3.2 fusion.136
  814.8 10.6 convert_bitcast_fusion.1
  825.5 5.8 copy.131
  831.5 6.4 convolution_convert_fusion.6
  838.0 10.8 bitcast_convert_fusion
  855.8 100.2 %reduce-scatter.25.cloned.1.call-done = f32[32,4]{1,0:T(8,128)} async-done(((f32[1024,4]{1,0:T(8,128)}), f32[32,4]{1,0:T(8,128)}) %reduce-scatter.25.cloned.1.call-update) | async-done | bytes 528
  957.5 109.6 %all-reduce.3.cloned.1.call-done = bf16[3,1024,512]{2,0,1:T(4,128)(2,1)} async-done(((bf16[3,1024,512]{2,0,1:T(4,128)(2,1)}), bf16[3,1024,512]{2,0,1:T(4,128)(2,1)}) %all-reduce.3.cloned.1.call-update) | async-done | bytes 3145744
  1068.1 59.2 %reduce-scatter.19.cloned.1.call-done = bf16[64,512]{1,0:T(8,128)(2,1)} async-done(((bf16[1024,512]{1,0:T(8,128)(2,1)}), bf16[64,512]{1,0:T(8,128)(2,1)}) %reduce-scatter.19.cloned.1.call-update) | async-done | bytes 65552 | tf_op jit(solution)/shard_map/reduce_scatter | solution.py:196
  1130.3 53.1 %reduce-scatter.17.cloned.1.call-done = bf16[1024,1024]{1,0:T(8,128)(2,1)} async-done(((bf16[2048,1024]{1,0:T(8,128)(2,1)}), bf16[1024,1024]{1,0:T(8,128)(2,1)}) %reduce-scatter.17.cloned.1.call-update) | async-done | bytes 2097168 | tf_op jit(solution)/shard_map/reduce_scatter | solution.py:187
  1183.4 5.3 convert_add_fusion
  (244 shorter events, 116.2 us)
Async XLA Ops:
  7.2 51.5 %all-gather.9.cloned.1.call-start = ((), (), s32[]{:S(2)}) async-start(), calls=%async_computation.8 | async-start | bytes 3342336 | tf_op jit(solution)/shard_map/all_gather | solution.py:61
  9.0 122.8 %all-gather.11.cloned.1.call-start = ((), (), s32[]{:S(2)}) async-start(), calls=%async_computation.9 | async-start | bytes 1114112 | tf_op jit(solution)/shard_map/all_gather | solution.py:62
  10.6 196.5 %reduce-scatter.11.cloned.1.call-start = ((), (), s32[]{:S(2)}) async-start(), calls=%async_computation.10 | async-start | bytes 6291456 | tf_op jit(solution)/shard_map/reduce_scatter | solution.py:106
  131.7 7.0 copy-start.7
  138.8 1.0 copy-start.12
  138.8 1.9 copy-start.30
  138.8 107.3 %all-gather.15.cloned.1.call-start = ((), (), s32[]{:S(2)}) async-start(), calls=%async_computation.12 | async-start | bytes 4456448 | tf_op jit(solution)/shard_map/all_gather | solution.py:63
  140.6 162.9 %all-gather.13.cloned.1.call-start = ((), (), s32[]{:S(2)}) async-start(), calls=%async_computation.11 | async-start | bytes 6291456 | tf_op jit(solution)/shard_map/all_gather | solution.py:117
  207.1 3.0 copy-start.1
  207.1 6.2 copy-start.5
  212.7 0.6 copy-start.27
  213.3 2.4 copy-start.10
  215.7 141.1 %all-gather.17.cloned.1.call-start = ((), (), s32[]{:S(2)}) async-start(), calls=%async_computation.13 | async-start | bytes 4456448 | tf_op jit(solution)/shard_map/all_gather | solution.py:64
  216.5 207.1 %reduce-scatter.13.cloned.1.call-start = ((), (), s32[]{:S(2)}) async-start(), calls=%async_computation.14 | async-start | bytes 6291456 | tf_op jit(solution)/shard_map/reduce_scatter | solution.py:122
  370.7 133.7 %all-gather.19.cloned.1.call-start = ((), (), s32[]{:S(2)}) async-start(), calls=%async_computation.15 | async-start | bytes 6291456 | tf_op jit(solution)/shard_map/all_gather | solution.py:135
  437.2 1.6 copy-start.9
  443.9 2.0 copy-start.2
  447.5 151.6 %reduce-scatter.15.cloned.1.call-start = ((), (), s32[]{:S(2)}) async-start(), calls=%async_computation.16 | async-start | bytes 6291456 | tf_op jit(solution)/shard_map/reduce_scatter | solution.py:141
  544.6 60.0 %copy-start.28 = (f32[1024]{0:T(1024)S(1)}, f32[1024]{0:T(1024)}, u32[]{:S(2)}) copy-start(f32[1024]{0:T(1024)} %copy-done.27) | copy-start | bytes 12292
  544.7 124.0 %all-gather.21.cloned.1.call-start = ((), (), s32[]{:S(2)}) async-start(), calls=%async_computation.17 | async-start | bytes 6291456 | tf_op jit(solution)/shard_map/all_gather | solution.py:145
  599.1 5.5 copy-start.3
  599.1 5.9 copy-start.6
  599.1 6.5 copy-start.8
  608.1 2.0 copy-start.4
  608.1 2.0 copy-start.25
  611.8 238.9 %reduce-scatter.23.cloned.1.call-start = ((), (), s32[]{:S(2)}) async-start(), calls=%async_computation.21 | async-start | bytes 4456448 | tf_op jit(solution)/shard_map/reduce_scatter | solution.py:202
  625.9 227.3 %reduce-scatter.21.cloned.1.call-start = ((), (), s32[]{:S(2)}) async-start(), calls=%async_computation.20 | async-start | bytes 4456448 | tf_op jit(solution)/shard_map/reduce_scatter | solution.py:199
  640.0 28.6 %copy-start.34 = (bf16[1024,512]{1,0:T(8,128)(2,1)S(1)}, bf16[1024,512]{1,0:T(8,128)(2,1)}, u32[]{:S(2)}) copy-start(bf16[1024,512]{1,0:T(8,128)(2,1)} %all-gather.11.cloned.1.call-done) | copy-start | bytes 3145732
  640.1 316.0 %reduce-scatter.25.cloned.1.call-start = ((), (), s32[]{:S(2)}) async-start(), calls=%async_computation.22 | async-start | bytes 540672
  641.2 425.9 %all-reduce.3.cloned.1.call-start = ((), (), s32[]{:S(2)}) async-start(), calls=%async_computation.23 | async-start | bytes 8388608
  688.0 5.6 slice-start
  688.0 6.8 slice-start.1
  697.4 2.0 copy-start
  722.1 5.3 slice-start
  722.1 6.2 slice-start.1
  731.0 2.0 copy-start
  755.4 5.7 slice-start
  755.4 6.9 slice-start.1
  765.0 2.0 copy-start
  789.9 5.3 slice-start
  790.0 6.3 slice-start.1
  798.9 2.0 copy-start
  831.3 6.7 copy-start.14
  831.3 296.1 %reduce-scatter.19.cloned.1.call-start = ((), (), s32[]{:S(2)}) async-start(), calls=%async_computation.19 | async-start | bytes 1114112 | tf_op jit(solution)/shard_map/reduce_scatter | solution.py:196
  837.9 345.5 %reduce-scatter.17.cloned.1.call-start = ((), (), s32[]{:S(2)}) async-start(), calls=%async_computation.18 | async-start | bytes 6291456 | tf_op jit(solution)/shard_map/reduce_scatter | solution.py:187
  848.8 0.7 copy-start.35
  848.8 1.9 copy-start.11
  848.8 1.9 copy-start.16
  848.8 1.9 copy-start.17
  848.8 4.5 copy-start.13
  848.8 4.5 copy-start.18
  848.8 4.5 copy-start.19
  848.9 108.0 %copy-start.31 = (f32[4,32]{1,0:T(4,128)S(1)}, f32[4,32]{1,0:T(4,128)}, u32[]{:S(2)}) copy-start(f32[4,32]{1,0:T(4,128)} %param.37) | copy-start | bytes 1540
  848.9 108.0 %copy-start.32 = (f32[4,32]{1,0:T(4,128)S(1)}, f32[4,32]{1,0:T(4,128)}, u32[]{:S(2)}) copy-start(f32[4,32]{1,0:T(4,128)} %param.39) | copy-start | bytes 1540
  848.9 107.9 %copy-start.33 = (f32[4,32]{1,0:T(4,128)S(1)}, f32[4,32]{1,0:T(4,128)}, u32[]{:S(2)}) copy-start(f32[4,32]{1,0:T(4,128)} %param.38) | copy-start | bytes 1540
  850.7 278.3 %copy-start.15 = (f32[3,64,512]{2,1,0:T(8,128)S(1)}, f32[3,64,512]{2,1,0:T(8,128)}, u32[]{:S(2)}) copy-start(f32[3,64,512]{2,1,0:T(8,128)} %param.25) | copy-start | bytes 1179652
  853.2 274.1 %copy-start.20 = (f32[64,512]{1,0:T(8,128)S(1)}, f32[64,512]{1,0:T(8,128)}, u32[]{:S(2)}) copy-start(f32[64,512]{1,0:T(8,128)} %param.28) | copy-start | bytes 393220
  853.2 274.1 %copy-start.23 = (f32[64,512]{1,0:T(8,128)S(1)}, f32[64,512]{1,0:T(8,128)}, u32[]{:S(2)}) copy-start(f32[64,512]{1,0:T(8,128)} %param.30) | copy-start | bytes 393220
  853.2 274.1 %copy-start.24 = (f32[64,512]{1,0:T(8,128)S(1)}, f32[64,512]{1,0:T(8,128)}, u32[]{:S(2)}) copy-start(f32[64,512]{1,0:T(8,128)} %param.29) | copy-start | bytes 393220
  853.2 275.8 %copy-start.21 = (f32[3,64,512]{2,1,0:T(8,128)S(1)}, f32[3,64,512]{2,1,0:T(8,128)}, u32[]{:S(2)}) copy-start(f32[3,64,512]{2,1,0:T(8,128)} %param.27) | copy-start | bytes 1179652
  853.2 275.8 %copy-start.22 = (f32[3,64,512]{2,1,0:T(8,128)S(1)}, f32[3,64,512]{2,1,0:T(8,128)}, u32[]{:S(2)}) copy-start(f32[3,64,512]{2,1,0:T(8,128)} %param.26) | copy-start | bytes 1179652
  853.2 330.2 %copy-start.26 = (f32[1024]{0:T(1024)S(1)}, f32[1024]{0:T(1024)}, u32[]{:S(2)}) copy-start(f32[1024]{0:T(1024)} %copy-done.25) | copy-start | bytes 12292
  956.8 231.9 %copy-start.29 = (f32[4,32]{1,0:T(4,128)}, f32[4,32]{1,0:T(4,128)S(1)}, u32[]{:S(2)}) copy-start(f32[4,32]{1,0:T(4,128)S(1)} %copy.139) | copy-start | bytes 1540
Sparse Core Ops, SparseCore 0:
  10.8 47.8 all-gather.8
  61.5 36.7 all-gather.10
  138.9 53.6 reduce-scatter.10
  195.4 50.6 all-gather.14
  248.1 55.2 all-gather.12
  306.2 50.5 all-gather.16
  370.8 52.7 reduce-scatter.12
  447.6 56.7 all-gather.18
  544.8 54.2 reduce-scatter.14
  611.9 56.7 all-gather.20
  673.0 72.6 reduce-scatter.22
  749.5 71.4 reduce-scatter.20
  823.3 132.7 reduce-scatter.24
  959.6 107.4 all-reduce.2
  1071.0 56.3 reduce-scatter.18
  1130.1 53.3 reduce-scatter.16
where the time goes:
time: 1200 us
  waiting for transfers between devices  654 us (54%)
  matrix products  292 us (24%)
  local copies, waits for them, and re-layouts  87.5 us (7%)
  other arithmetic  78.6 us (7%)
  blocking collectives  66.3 us (6%)
  between operations  15.3 us (1%)
    unnamed x18, waiting for transfers between devices  210 us
    all_gather x1, blocking collectives, local(): lax.all_gather(norm_params.astype(jnp.bfloat16), ('dp', 'mp'), axis=1, ti...  66.3 us
    reduce_scatter x1, waiting for transfers between devices, local(): lax.psum_scatter(output_grad.astype(jnp.bfloat16), 'dp', scatter_dimensio...  59.2 us
    all_gather x1, waiting for transfers between devices, local(): lax.all_gather(hidden_one.astype(jnp.bfloat16), 'mp', axis=0, tiled=True)  57.3 us
    all_gather x1, waiting for transfers between devices, local(): lax.all_gather(d_resid_two.astype(jnp.bfloat16), 'mp', axis=0, tiled=True)  56.9 us
    reduce_scatter x1, waiting for transfers between devices, local(): lax.psum_scatter(d_hidden_part.astype(jnp.bfloat16), 'mp', scatter_dimens...  54.4 us
    reduce_scatter x1, waiting for transfers between devices, local(): lax.psum_scatter(d_input_part.astype(jnp.bfloat16), 'mp', scatter_dimensi...  53.1 us
    reduce_scatter x1, waiting for transfers between devices, local(): lax.psum_scatter(ffn_part.astype(jnp.bfloat16), 'mp', scatter_dimension=0...  52.9 us
  transfers between devices with their start and end apart: 16, of which 12 were waited for; matrix products, arithmetic and copies ran while one was open for 28% of the time, Pallas kernels for 0%

commit v1 on v0

--- a/solution.py
+++ b/solution.py
@@ -1,6 +1,10 @@
+import functools
+
 import jax
 import jax.numpy as jnp
 from jax import lax
+from jax.experimental import pallas as pl
+from jax.experimental.pallas import tpu as pltpu
 from jax.sharding import PartitionSpec as P
 
 D = 1024
@@ -37,7 +41,7 @@
     return (gradient, moment, square, updated)
 
 
-def local(
+def local_plain(
     tokens_in,
     cotangent,
     segment_ids,
@@ -234,9 +238,565 @@
     )
 
 
+MESH = pl.DeviceIdType.MESH
+BF16 = jnp.bfloat16
+F32 = jnp.float32
+ANY = pl.BlockSpec(memory_space=pl.ANY)
+VMEM = pl.BlockSpec(memory_space=pltpu.VMEM)
+DMA = pltpu.SemaphoreType.DMA
+
+HOP_X, HOP_Y, HOP_C, OWN = (0, 1, 0, 0), (0, 0, 0, 1), (0, 0, 1, 0), (0, 0, 0, 0)
+
+
+def hop_z(mask):
+    return (mask, 0, 0, 0)
+
+
+def position():
+    dp = lax.axis_index("dp")
+    return (dp // 4, (dp // 2) % 2, dp % 2, lax.axis_index("mp"))
+
+
+def moved(me, hop):
+    return tuple(m ^ h if h else m for m, h in zip(me, hop))
+
+
+def device_at(me, hop):
+    z, x, c, y = moved(me, hop)
+    return (z * 4 + x * 2 + c, y)
+
+
+def entry_barrier(me, nz):
+    barrier = pltpu.get_barrier_semaphore()
+    hops = [HOP_X, HOP_Y, HOP_C] + [hop_z(a) for a in range(1, nz)]
+    for hop in hops:
+        pl.semaphore_signal(barrier, inc=1, device_id=device_at(me, hop), device_id_type=MESH)
+    pl.semaphore_wait(barrier, len(hops))
+
+
+def view_rows(ref, pos):
+    z, x, c, y = pos
+    half = ref.shape[4] // 2
+    return ref.at[z, x, c, :, pl.ds(pl.multiple_of(y * half, half), half)]
+
+
+def view_stack(ref, pos):
+    z, x, c, y = pos
+    half = ref.shape[5] // 2
+    return ref.at[:, z, x, c, :, pl.ds(pl.multiple_of(y * half, half), half)]
+
+
+class Gather:
+    def __init__(self, me, nz, own, out, view, send_sem, recv_sem, base):
+        self.me, self.nz, self.own, self.out, self.view = me, nz, own, out, view
+        self.send_sem, self.recv_sem, self.base = send_sem, recv_sem, base
+        self.sent = []
+
+    def slot(self, rel):
+        a, b, d, e = rel
+        return self.base + ((a * 2 + b) * 2 + d) * 2 + e
+
+    def piece(self, rel):
+        return self.view(self.out, moved(self.me, rel))
+
+    def copy(self, rel, hop):
+        arrives = tuple(r ^ h for r, h in zip(rel, hop))
+        return pltpu.make_async_remote_copy(
+            src_ref=self.own if rel == OWN else self.piece(rel),
+            dst_ref=self.piece(rel),
+            send_sem=self.send_sem.at[self.slot(arrives)],
+            recv_sem=self.recv_sem.at[self.slot(arrives)],
+            device_id=device_at(self.me, hop),
+            device_id_type=MESH,
+        )
+
+    def send(self, rel, hop):
+        copy = self.copy(rel, hop)
+        copy.start()
+        self.sent.append(copy)
+
+    def wait(self, rel):
+        pltpu.make_async_remote_copy(
+            src_ref=self.own,
+            dst_ref=self.piece(rel),
+            send_sem=self.send_sem.at[self.slot(rel)],
+            recv_sem=self.recv_sem.at[self.slot(rel)],
+            device_id=device_at(self.me, HOP_C),
+            device_id_type=MESH,
+        ).wait_recv()
+
+    def run(self, steps):
+        for kind, rel, hop in steps:
+            if kind == "send":
+                self.send(rel, hop)
+            else:
+                self.wait(rel)
+
+    def steps_first(self):
+        out = [("send", OWN, HOP_X), ("send", OWN, HOP_Y)]
+        out += [("send", OWN, hop_z(a)) for a in range(1, self.nz)]
+        return out + [("send", OWN, HOP_C)]
+
+    def steps_square(self, a):
+        out = [("wait", (a, 1, 0, 0), None), ("wait", (a, 0, 0, 1), None)]
+        if a < self.nz // 2:
+            out.append(("send", (a, 1, 0, 0), HOP_Y))
+        else:
+            out.append(("send", (a, 0, 0, 1), HOP_X))
+        return out + [("send", (a, 1, 0, 0), HOP_C), ("send", (a, 0, 0, 1), HOP_C)]
+
+    def steps_level(self, a):
+        piece = hop_z(a)
+        return [("wait", piece, None)] + [("send", piece, hop) for hop in (HOP_X, HOP_Y, HOP_C)]
+
+    def steps_middle(self):
+        out = []
+        for a in range(1, self.nz):
+            out += self.steps_level(a) + self.steps_square(a - 1)
+        return out + self.steps_square(self.nz - 1)
+
+    def steps_diagonal(self):
+        out = []
+        for a in range(self.nz):
+            out += [("wait", (a, 1, 0, 1), None), ("send", (a, 1, 0, 1), HOP_C)]
+        return out
+
+    def steps_last(self):
+        return [("wait", (a, b, 1, e), None) for a in range(self.nz) for b in range(2) for e in range(2)]
+
+    def drain(self):
+        for copy in self.sent:
+            copy.wait_send()
+
+
+def sum_hops(nz):
+    hops, mask = [HOP_C, HOP_X, HOP_Y], 1
+    while mask < nz:
+        hops.append(hop_z(mask))
+        mask *= 2
+    return hops
+
+
+class SmallSum:
+    def __init__(self, me, nz, parts, came, send_sem, recv_sem):
+        self.me, self.hops, self.parts, self.came = me, sum_hops(nz), parts, came
+        self.send_sem, self.recv_sem = send_sem, recv_sem
+
+    def copy(self, i):
+        return pltpu.make_async_remote_copy(
+            src_ref=self.parts.at[i],
+            dst_ref=self.came.at[i],
+            send_sem=self.send_sem.at[i],
+            recv_sem=self.recv_sem.at[i],
+            device_id=device_at(self.me, self.hops[i]),
+            device_id_type=MESH,
+        )
+
+    def start(self, i):
+        self.copy(i).start()
+
+    def finish(self, i):
+        self.copy(i).wait()
+        self.parts[i + 1] = self.parts[i] + self.came[i]
+
+
+def gather_kernel(nz, proj, out, up, down, norm, proj_all, out_all, up_all, down_all, norm_all,
+                  send_sem, recv_sem, local_sem, parts, came, sum_send, sum_recv):
+    me = position()
+    entry_barrier(me, nz)
+    n = 8 * nz
+    small = SmallSum(me, nz, parts, came, sum_send, sum_recv)
+    parts[0] = norm[...]
+    owns, fulls = (proj, out, up, down), (proj_all, out_all, up_all, down_all)
+    views = (view_stack, view_rows, view_rows, view_rows)
+    gathers = [
+        Gather(me, nz, owns[i], fulls[i], views[i], send_sem, recv_sem, n * i) for i in range(4)
+    ]
+    locals_ = [pltpu.make_async_copy(g.own, g.piece(OWN), local_sem.at[i]) for i, g in enumerate(gathers)]
+    for copy in locals_:
+        copy.start()
+    for i in range(len(small.hops)):
+        small.start(i)
+        small.finish(i)
+    norm_all[...] = parts[len(small.hops)]
+    gathers[0].run(gathers[0].steps_first())
+    for i, g in enumerate(gathers):
+        g.run(g.steps_middle())
+        if i + 1 < len(gathers):
+            gathers[i + 1].run(gathers[i + 1].steps_first())
+        g.run(g.steps_diagonal())
+        g.run(g.steps_last())
+    for copy in locals_:
+        copy.wait()
+    for g in gathers:
+        g.drain()
+
+
+def gather_weights(nz, proj, out, up, down, norm):
+    n_sum = len(sum_hops(nz))
+    full = lambda s: jax.ShapeDtypeStruct((nz, 2, 2, s.shape[0], s.shape[1] * 2), BF16)
+    results = pl.pallas_call(
+        functools.partial(gather_kernel, nz),
+        out_shape=[
+            jax.ShapeDtypeStruct((3, nz, 2, 2, proj.shape[1], proj.shape[2] * 2), BF16),
+            full(out),
+            full(up),
+            full(down),
+            jax.ShapeDtypeStruct(norm.shape, F32),
+        ],
+        in_specs=[ANY] * 4 + [VMEM],
+        out_specs=[ANY] * 4 + [VMEM],
+        scratch_shapes=[
+            DMA((32 * nz,)),
+            DMA((32 * nz,)),
+            DMA((4,)),
+            pltpu.VMEM((n_sum + 1,) + norm.shape, F32),
+            pltpu.VMEM((n_sum,) + norm.shape, F32),
+            DMA((n_sum,)),
+            DMA((n_sum,)),
+        ],
+        compiler_params=pltpu.CompilerParams(collective_id=0, has_side_effects=True),
+        name="gather_weights",
+    )(proj, out, up, down, norm)
+    proj_all, out_all, up_all, down_all, norm_all = results
+    return (
+        proj_all.reshape(3, D, -1),
+        out_all.reshape(D, -1),
+        up_all.reshape(D, -1),
+        down_all.reshape(D, -1),
+        norm_all,
+    )
+
+
+def blocks_of(ref, rows=16):
+    return ref.shape[-2] // rows
+
+
+def add_blocks(dst, terms, rows=16):
+    lead = range(dst.shape[0]) if len(dst.shape) == 3 else (None,)
+
+    def body(i, carry):
+        start = pl.multiple_of(i * rows, rows)
+        for s in lead:
+            idx = (pl.ds(start, rows), slice(None)) if s is None else (s, pl.ds(start, rows), slice(None))
+            total = terms[0][idx].astype(F32)
+            for term in terms[1:]:
+                total = total + term[idx].astype(F32)
+            dst[idx] = total.astype(dst.dtype)
+        return carry
+
+    lax.fori_loop(0, dst.shape[-2] // rows, body, 0)
+
+
+class Scatter:
+    def __init__(self, me, nz, grad, result, view, held, from_c, from_d, from_x, from_y, from_z,
+                 load_sem, send_sem, recv_sem, base):
+        self.me, self.nz, self.grad, self.result, self.view = me, nz, grad, result, view
+        self.held, self.from_c, self.from_d = held, from_c, from_d
+        self.from_x, self.from_y, self.from_z = from_x, from_y, from_z
+        self.load_sem, self.send_sem, self.recv_sem, self.base = load_sem, send_sem, recv_sem, base
+        self.sent = []
+
+    def index(self, a, b, e):
+        return (a * 2 + b) * 2 + e
+
+    def remote(self, src, dst, slot, hop):
+        sem = self.base * 8 * self.nz + slot
+        return pltpu.make_async_remote_copy(
+            src_ref=src, dst_ref=dst, send_sem=self.send_sem.at[sem], recv_sem=self.recv_sem.at[sem],
+            device_id=device_at(self.me, hop), device_id_type=MESH,
+        )
+
+    def send(self, src, dst, slot, hop):
+        copy = self.remote(src, dst, slot, hop)
+        copy.start()
+        self.sent.append(copy)
+
+    def wait(self, dst, slot):
+        self.remote(dst, dst, slot, HOP_C).wait_recv()
+
+    def load(self, a, b, e):
+        i = self.index(a, b, e)
+        return pltpu.make_async_copy(
+            self.view(self.grad, moved(self.me, (a, b, 0, e))), self.held.at[i],
+            self.load_sem.at[self.base * 4 * self.nz + i],
+        )
+
+    def stage_core(self, a):
+        for b, e in ((1, 1), (1, 0), (0, 1), (0, 0)):
+            i = self.index(a, b, e)
+            self.send(self.view(self.grad, moved(self.me, (a, b, 1, e))), self.from_c.at[i], i, HOP_C)
+            self.load(a, b, e).start()
+
+    def slot_of(self, kind, a):
+        return 4 * self.nz + self.nz * "dxyz".index(kind) + a
+
+    def stage_diagonal(self, a):
+        for b, e in ((1, 1), (1, 0), (0, 1), (0, 0)):
+            i = self.index(a, b, e)
+            self.load(a, b, e).wait()
+            self.wait(self.from_c.at[i], i)
+            add_blocks(self.held.at[i], [self.held.at[i], self.from_c.at[i]])
+            if (b, e) == (1, 1):
+                hop = HOP_Y if a < self.nz // 2 else HOP_X
+                self.send(self.held.at[i], self.from_d.at[a], self.slot_of("d", a), hop)
+            elif (b, e) == (1, 0) and a >= self.nz // 2:
+                self.send(self.held.at[i], self.from_x.at[a], self.slot_of("x", a), HOP_X)
+            elif (b, e) == (0, 1) and a < self.nz // 2:
+                self.send(self.held.at[i], self.from_y.at[a], self.slot_of("y", a), HOP_Y)
+
+    def stage_square(self, a):
+        self.wait(self.from_d.at[a], self.slot_of("d", a))
+        if a < self.nz // 2:
+            i = self.index(a, 1, 0)
+            add_blocks(self.held.at[i], [self.held.at[i], self.from_d.at[a]])
+            self.send(self.held.at[i], self.from_x.at[a], self.slot_of("x", a), HOP_X)
+        else:
+            i = self.index(a, 0, 1)
+            add_blocks(self.held.at[i], [self.held.at[i], self.from_d.at[a]])
+            self.send(self.held.at[i], self.from_y.at[a], self.slot_of("y", a), HOP_Y)
+
+    def stage_column(self, a):
+        self.wait(self.from_x.at[a], self.slot_of("x", a))
+        self.wait(self.from_y.at[a], self.slot_of("y", a))
+        i = self.index(a, 0, 0)
+        terms = [self.held.at[i], self.from_x.at[a], self.from_y.at[a]]
+        if a:
+            add_blocks(self.held.at[i], terms)
+            self.send(self.held.at[i], self.from_z.at[a], self.slot_of("z", a), hop_z(a))
+        else:
+            for other in range(1, self.nz):
+                self.wait(self.from_z.at[other], self.slot_of("z", other))
+                terms.append(self.from_z.at[other])
+            add_blocks(self.result, terms)
+
+    def order(self):
+        half = self.nz // 2
+        out = []
+        for k in range(half):
+            out += [self.nz - 1 - k, half - 1 - k]
+        return out
+
+    def stages(self):
+        order = self.order()
+        calls = [(self.stage_core, a) for a in order]
+        kinds = (self.stage_diagonal, self.stage_square, self.stage_column)
+        for t in range(len(order) + 2):
+            for lag, kind in enumerate(kinds):
+                if 0 <= t - lag < len(order):
+                    calls.append((kind, order[t - lag]))
+        return calls
+
+    def drain(self):
+        for copy in self.sent:
+            copy.wait_send()
+
+
+def scatter_kernel(nz, *refs):
+    grads, norm = refs[:4], refs[4]
+    results, norm_all = refs[5:9], refs[9]
+    buffers, rest = refs[10:34], refs[34:]
+    load_sem, send_sem, recv_sem, parts, came, sum_send, sum_recv = rest
+    me = position()
+    entry_barrier(me, nz)
+    views = (view_rows, view_rows, view_rows, view_stack)
+    scatters = [
+        Scatter(me, nz, grads[i], results[i], views[i], *buffers[6 * i : 6 * i + 6],
+                load_sem, send_sem, recv_sem, i)
+        for i in range(4)
+    ]
+    small = SmallSum(me, nz, parts, came, sum_send, sum_recv)
+    parts[0] = norm[...]
+    for i in range(len(small.hops)):
+        small.start(i)
+        small.finish(i)
+    norm_all[...] = parts[len(small.hops)]
+    for s in scatters:
+        for call, a in s.stages():
+            call(a)
+    for s in scatters:
+        s.drain()
+
+
+def scatter_grads(nz, down, up, out, proj, norm):
+    grads = [g.reshape(nz, 2, 2, D // (4 * nz), g.shape[1]) for g in (down, up, out)]
+    grads.append(proj.reshape(3, nz, 2, 2, D // (4 * nz), proj.shape[2]))
+    shapes, buffers = [], []
+    for g in grads:
+        piece = (g.shape[-2], g.shape[-1] // 2)
+        if g.ndim == 6:
+            piece = (3,) + piece
+        shapes.append(jax.ShapeDtypeStruct(piece, F32))
+        for count in (4 * nz, 4 * nz, nz, nz, nz, nz):
+            buffers.append(pltpu.VMEM((count,) + piece, BF16))
+    n_sum = len(sum_hops(nz))
+    return pl.pallas_call(
+        functools.partial(scatter_kernel, nz),
+        out_shape=shapes + [jax.ShapeDtypeStruct(norm.shape, F32)],
+        in_specs=[ANY] * 4 + [VMEM],
+        out_specs=[VMEM] * 5,
+        scratch_shapes=buffers
+        + [
+            DMA((16 * nz,)),
+            DMA((32 * nz,)),
+            DMA((32 * nz,)),
+            pltpu.VMEM((n_sum + 1,) + norm.shape, F32),
+            pltpu.VMEM((n_sum,) + norm.shape, F32),
+            DMA((n_sum,)),
+            DMA((n_sum,)),
+        ],
+        compiler_params=pltpu.CompilerParams(
+            collective_id=1, has_side_effects=True, vmem_limit_bytes=56 << 20
+        ),
+        name="scatter_grads",
+    )(*grads, norm)
+
+
+def dot_f32(spec, a, b):
+    return jnp.einsum(spec, a, b, preferred_element_type=F32)
+
+
+def local_rows(
+    tokens_in,
+    cotangent,
+    segment_ids,
+    project_weight,
+    project_momentum,
+    project_squares,
+    output_weight,
+    output_momentum,
+    output_squares,
+    up_weight,
+    up_momentum,
+    up_squares,
+    down_weight,
+    down_momentum,
+    down_squares,
+    norm_params,
+    norm_momentum,
+    norm_squares,
+):
+    nz = lax.axis_size("dp") // 4
+    dp, mp = lax.axis_index("dp"), lax.axis_index("mp")
+    norm_cols = norm_params.shape[1]
+    norm_start = (dp * 2 + mp) * norm_cols
+    norm_wide = lax.dynamic_update_slice(
+        jnp.zeros((8, D), F32), norm_params.astype(BF16).astype(F32), (0, norm_start)
+    )
+    proj_w, out_w, up_w, down_w, norm_full = gather_weights(
+        nz,
+        project_weight.astype(BF16),
+        output_weight.astype(BF16),
+        up_weight.astype(BF16),
+        down_weight.astype(BF16),
+        norm_wide,
+    )
+    rows_here = segment_ids.shape[0] // 2
+    seq_len = segment_ids.shape[1]
+    tokens_here = rows_here * seq_len
+    heads = D // HEAD_DIM
+    score_scale = HEAD_DIM ** (-0.5)
+    tokens = lax.dynamic_slice_in_dim(tokens_in, mp * tokens_here, tokens_here, 0)
+    segments = lax.dynamic_slice_in_dim(segment_ids, mp * rows_here, rows_here, 0)
+    projected = dot_f32("tc,scn->stn", tokens, proj_w).astype(BF16)
+    heads_split = projected.reshape(3, rows_here, seq_len, heads, HEAD_DIM)
+
+    def masked_scores(query_rows, key_rows, row_segments):
+        scores = dot_f32("qhd,khd->hqk", query_rows, key_rows) * score_scale
+        same_doc = row_segments[:, None] == row_segments[None, :]
+        return jnp.where(same_doc[None], scores, NEG_FILL)
+
+    def row_forward(packed):
+        query_rows, key_rows, value_rows, row_segments = packed
+        scores = masked_scores(query_rows, key_rows, row_segments)
+        row_max = jnp.max(scores, axis=-1, keepdims=True)
+        row_exp = jnp.exp(scores - row_max)
+        row_total = jnp.sum(row_exp, axis=-1, keepdims=True)
+        row_probs = (row_exp / row_total).astype(BF16)
+        mixed = dot_f32("hqk,khd->qhd", row_probs, value_rows)
+        row_lse = (row_max + jnp.log(row_total))[..., 0]
+        return (mixed.astype(BF16).reshape(seq_len, D), row_lse)
+
+    context_rows, lse_rows = lax.map(
+        row_forward, (heads_split[0], heads_split[1], heads_split[2], segments)
+    )
+    context = context_rows.reshape(tokens_here, D)
+    attended = dot_f32("tn,dn->td", context, out_w)
+    hidden_one, norm_one_back = jax.vjp(
+        layer_norm, tokens.astype(F32) + attended, norm_full[0], norm_full[1]
+    )
+    hidden_low = hidden_one.astype(BF16)
+    pre_act = jnp.dot(hidden_low, up_w, preferred_element_type=F32)
+    act_full, gelu_back = jax.vjp(exact_gelu, pre_act)
+    act_low = act_full.astype(BF16)
+    ffn_out = dot_f32("tf,df->td", act_low, down_w)
+    result, norm_two_back = jax.vjp(layer_norm, hidden_one + ffn_out, norm_full[2], norm_full[3])
+    layer_out = result.astype(BF16)
+    d_resid_two, d_gain_two, d_shift_two = norm_two_back(cotangent.astype(F32))
+    d_ffn = d_resid_two.astype(BF16)
+    down_grad = dot_f32("td,tf->df", d_ffn, act_low).astype(BF16)
+    d_act = jnp.dot(d_ffn, down_w, preferred_element_type=F32)
+    d_pre = gelu_back(d_act)[0].astype(BF16)
+    up_grad = dot_f32("tc,tf->cf", hidden_low, d_pre).astype(BF16)
+    d_hidden = d_resid_two + dot_f32("tf,cf->tc", d_pre, up_w)
+    d_resid_one, d_gain_one, d_shift_one = norm_one_back(d_hidden)
+    d_attn = d_resid_one.astype(BF16)
+    output_grad = dot_f32("td,tn->dn", d_attn, context).astype(BF16)
+    d_context = jnp.dot(d_attn, out_w, preferred_element_type=F32).astype(BF16)
+
+    def row_backward(packed):
+        query_rows, key_rows, value_rows, row_segments, row_lse, row_grad = packed
+        scores = masked_scores(query_rows, key_rows, row_segments)
+        row_probs = jnp.exp(scores - row_lse[..., None])
+        grad_heads = row_grad.reshape(seq_len, heads, HEAD_DIM)
+        d_probs = dot_f32("qhd,khd->hqk", grad_heads, value_rows)
+        row_inner = jnp.sum(d_probs * row_probs, axis=-1, keepdims=True)
+        d_scores = (row_probs * (d_probs - row_inner)).astype(BF16)
+        d_value = dot_f32("hqk,qhd->khd", row_probs.astype(BF16), grad_heads)
+        d_query = dot_f32("hqk,khd->qhd", d_scores, key_rows) * score_scale
+        d_key = dot_f32("hqk,qhd->khd", d_scores, query_rows) * score_scale
+        return tuple(g.astype(BF16).reshape(seq_len, D) for g in (d_query, d_key, d_value))
+
+    d_rows = lax.map(
+        row_backward,
+        (
+            heads_split[0],
+            heads_split[1],
+            heads_split[2],
+            segments,
+            lse_rows,
+            d_context.reshape(rows_here, seq_len, D),
+        ),
+    )
+    d_proj = jnp.stack(d_rows).reshape(3, tokens_here, D)
+    project_grad = dot_f32("tc,stn->scn", tokens, d_proj).astype(BF16)
+    input_grad = d_resid_one + dot_f32("stn,scn->tc", d_proj, proj_w)
+    norm_local = jnp.stack([d_gain_one, d_shift_one, d_gain_two, d_shift_two])
+    norm_local = jnp.concatenate([norm_local, jnp.zeros_like(norm_local)])
+    down_red, up_red, out_red, proj_red, norm_sum = scatter_grads(
+        nz, down_grad, up_grad, output_grad, project_grad, norm_local
+    )
+    norm_red = lax.dynamic_slice(norm_sum, (0, norm_start), (4, norm_cols))
+    return (
+        layer_out,
+        input_grad,
+        *adam_step(proj_red, project_weight, project_momentum, project_squares, D ** (-0.5)),
+        *adam_step(out_red, output_weight, output_momentum, output_squares, 4.0 * D ** (-0.5)),
+        *adam_step(up_red, up_weight, up_momentum, up_squares, D ** (-0.5)),
+        *adam_step(down_red, down_weight, down_momentum, down_squares, FF ** (-0.5)),
+        *adam_step(norm_red, norm_params, norm_momentum, norm_squares, 0.3),
+    )
+
+
+def by_rows(mesh):
+    dp, mp = mesh.shape["dp"], mesh.shape["mp"]
+    return mp == 2 and dp >= 8 and dp & (dp - 1) == 0 and D % (64 * dp) == 0
+
+
 def solution(mesh):
+    body = local_rows if by_rows(mesh) else local_plain
     return jax.shard_map(
-        local,
+        body,
         mesh=mesh,
         in_specs=(
             P("dp", None),

time: 1200 us -> 756 us (0.63)
  waiting for transfers between devices: 654 us -> 0 us
  Pallas kernels: 0 us -> 339 us
  blocking collectives: 66.3 us -> 0 us
  local copies, waits for them, and re-layouts: 87.5 us -> 45.5 us
  between operations: 15.3 us -> 1.83 us
    pallas_call x0 -> x2, Pallas kernels: none -> 339 us  [the longest x1 181 us: scatter_grads(): pl.pallas_call(functools.partial(scatter_kernel, nz), out_shape=shapes +...]
    all_gather x7 -> x0, waiting for transfers between devices: 224 us -> none  [the longest x1 57.3 us: local(): lax.all_gather(hidden_one.astype(jnp.bfloat16), 'mp', axis=0, tiled=True)]
    reduce_scatter x7 -> x0, waiting for transfers between devices: 220 us -> none  [the longest x1 59.2 us: local(): lax.psum_scatter(output_grad.astype(jnp.bfloat16), 'dp', scatter_dimensio...]
    unnamed x18 -> x0, waiting for transfers between devices: 210 us -> none
    all_gather x1 -> x0, blocking collectives: 66.3 us -> none  [local(): lax.all_gather(norm_params.astype(jnp.bfloat16), ('dp', 'mp'), axis=1, ti...]
    reduce_sum x4 -> x2, other arithmetic: 22.2 us -> 5.99 us  [layer_norm(): center = values - jnp.mean(values, axis=-1, keepdims=True)]
    while x27 -> x11, local copies, waits for them, and re-layouts: 21.3 us -> 5.4 us  [the longest x3 5.39 us: local_rows(): lax.map(row_forward, (heads_split[0], heads_split[1], heads_split[2], seg...]
    convert_element_type x12 -> x7, other arithmetic: 20.8 us -> 30.6 us  [the longest x2 23.2 us: row_backward(): d_scores = (row_probs * (d_probs - row_inner)).astype(BF16)]
  transfers between devices with their start and end apart: 16 -> 0, of which waited for: 12 -> 0; matrix products, arithmetic and copies ran while one was open for 28% -> 0% of each run, Pallas kernels for 0% -> 0%
where the time goes in v1:
time: 756 us; the launch traced here: 748 us
  Pallas kernels  339 us (45%)
  matrix products  293 us (39%)
  other arithmetic  68.8 us (9%)
  local copies, waits for them, and re-layouts  45.5 us (6%)
    dot_general x23, matrix products, dot_f32(): return jnp.einsum(spec, a, b, preferred_element_type=F32)  217 us
    pallas_call x1, Pallas kernels, scatter_grads(): pl.pallas_call(functools.partial(scatter_kernel, nz), out_shape=shapes +...  181 us
    pallas_call x1, Pallas kernels, gather_weights(): pl.pallas_call(functools.partial(gather_kernel, nz), out_shape=[jax.Shape...  157 us
    dot_general x1, matrix products, local_rows(): pre_act = jnp.dot(hidden_low, up_w, preferred_element_type=F32)  49 us
    dot_general x1, matrix products, local_rows(): d_act = jnp.dot(d_ffn, down_w, preferred_element_type=F32)  23.3 us
    convert_element_type x2, other arithmetic, row_backward(): d_scores = (row_probs * (d_probs - row_inner)).astype(BF16)  23.2 us
    reduce_sum x2, other arithmetic, row_forward(): row_total = jnp.sum(row_exp, axis=-1, keepdims=True)  18.8 us

profile of v1, /device:TPU:0, one launch (start us, length us, event | category | flops | bytes accessed | tf_op | source)
XLA Modules:
  0.0 748.3 jit_solution(1915841554967881303)
XLA Ops:
  0.7 1.7 convert_element_type.100.proj
  2.4 1.5 convert_element_type.101.out
  3.9 1.8 convert_element_type.102.up
  5.7 1.8 convert_element_type.103.down
  9.0 157.0 %gather_weights.1 = (bf16[3,4,2,2,64,1024]{5,4,3,2,1,0:T(8,128)(2,1)}, bf16[4,2,2,64,1024]{4,3,2,1,0:T(8,128)(2,1)}, bf16[4,2,2,64,4096]{4,3,2,1,0:T(8,128)(2,1)...) custom-call(bf16[3,64,512]{2,1,0:T(8,128)(2,1)} %convert_element_type.100.proj, ...), custom_call_target="tpu_custom_call" | custom-call | tf_op jit(solution)/shard_map/gather_weights/pallas_call | solution.py:438
  166.1 10.2 %convert_bitcast_fusion = bf16[3,1024,1024]{1,2,0:T(8,128)(2,1)S(1)} fusion(bf16[3,1024,1024]{2,1,0:T(8,128)(2,1)} %bitcast.188, bf16[2048,1024]{1,0:T(8,128)(2,1)} %param.22, s32[]{:T(128)S(6)} %select_n.17), kind=kOutput, calls=%fused_computation.77 | convolution fusion | flops 6445596672 | bytes 14680068 | tf_op jit(solution)/shard_map/tc,scn->stn/dot_general | solution.py:656
  176.3 2.9 fusion.75
  179.2 3.3 squeeze.39
  182.5 1.8 copy.63
  184.3 3.3 squeeze.40
  187.6 1.8 copy.64
  189.4 3.3 squeeze.41
  192.7 1.8 copy.65
  194.5 1.6 broadcast.178.clone2
  196.1 59.4 %while.26 = (s32[]{:T(128)}, bf16[2,512,1024]{2,1,0:T(8,128)(2,1)}, f32[2,16,512]{2,1,0:T(8,128)S(1)}, bf16[2,512,16,64]{1,3,2,0:T(8,128)(2,1)}, s32[2,512]{1,0:...) while((s32[]{:T(128)}, bf16[2,512,1024]{2,1,0:T(8,128)(2,1)}, ...), condition=%wide.region_3.4_spmd, body=%wide.region_0.3_spmd.sunk | while | flops 1124851712 | bytes 60038252 | solution.py:720
  196.5 9.9 %fusion.112 = (f32[16,512]{1,0:T(8,128)S(1)}, f32[16,512,512]{1,2,0:T(8,128)}) fusion(pred[512,512]{0,1:T(8,128)(4,1)S(1)} %broadcast_compare_fusion.4, bf16[2,512,16,64]{1,3,2,0:T(8,128)(2,1)} %get-tuple-element.396, s32[]{:T(128)S(6)} %copy.114, bf16[2,512,16,64]{1,3,2,0:T(8,128)(2,1)} %get-tuple-element.395), kind=kOutput, calls=%fused_computation.3.clone.1 | convolution fusion | flops 549445632 | bytes 19170304 | tf_op jit(solution)/shard_map/while/body/eval_jaxpr/qhd,khd->hqk/dot_general | solution.py:656
  206.5 9.4 %fusion.113 = f32[16,512]{1,0:T(8,128)S(1)} fusion(f32[16,512,512]{1,2,0:T(8,128)} %get-tuple-element.358, f32[16,512]{1,0:T(8,128)S(1)} %get-tuple-element.359, pred[512,512]{0,1:T(8,128)(4,1)S(1)} %broadcast_compare_fusion.4), kind=kLoop, calls=%fused_computation.4.clone.1 | loop fusion | flops 16769024 | bytes 17104896 | tf_op jit(solution)/shard_map/while/body/eval_jaxpr/reduce_sum | solution.py:714
  215.9 8.4 %fusion.114 = bf16[16,64,512]{2,1,0:T(8,128)(2,1)S(1)} fusion(f32[16,512,512]{1,2,0:T(8,128)} %get-tuple-element.358, f32[16,512]{1,0:T(8,128)S(1)} %fusion.113, f32[16,512]{1,0:T(8,128)S(1)} %get-tuple-element.359, pred[512,512]{0,1:T(8,128)(4,1)S(1)} %broadcast_compare_fusion.4, bf16[2,512,16,64]{1,3,2,0:T(8,128)(2,1)} %get-tuple-element.393, ...), kind=kOutput, calls=%fused_computation.6.clone.1 | convolution fusion | flops 558366720 | bytes 19202052 | tf_op jit(solution)/shard_map/while/body/eval_jaxpr/hqk,khd->qhd/dot_general | solution.py:656
  224.8 1.1 constant_dynamic-update-slice_fusion.7
  226.1 9.9 %fusion.112 = (f32[16,512]{1,0:T(8,128)S(1)}, f32[16,512,512]{1,2,0:T(8,128)}) fusion(pred[512,512]{0,1:T(8,128)(4,1)S(1)} %broadcast_compare_fusion.4, bf16[2,512,16,64]{1,3,2,0:T(8,128)(2,1)} %get-tuple-element.396, s32[]{:T(128)S(6)} %copy.114, bf16[2,512,16,64]{1,3,2,0:T(8,128)(2,1)} %get-tuple-element.395), kind=kOutput, calls=%fused_computation.3.clone.1 | convolution fusion | flops 549445632 | bytes 19170304 | tf_op jit(solution)/shard_map/while/body/eval_jaxpr/qhd,khd->hqk/dot_general | solution.py:656
  236.1 9.4 %fusion.113 = f32[16,512]{1,0:T(8,128)S(1)} fusion(f32[16,512,512]{1,2,0:T(8,128)} %get-tuple-element.358, f32[16,512]{1,0:T(8,128)S(1)} %get-tuple-element.359, pred[512,512]{0,1:T(8,128)(4,1)S(1)} %broadcast_compare_fusion.4), kind=kLoop, calls=%fused_computation.4.clone.1 | loop fusion | flops 16769024 | bytes 17104896 | tf_op jit(solution)/shard_map/while/body/eval_jaxpr/reduce_sum | solution.py:714
  245.5 8.4 %fusion.114 = bf16[16,64,512]{2,1,0:T(8,128)(2,1)S(1)} fusion(f32[16,512,512]{1,2,0:T(8,128)} %get-tuple-element.358, f32[16,512]{1,0:T(8,128)S(1)} %fusion.113, f32[16,512]{1,0:T(8,128)S(1)} %get-tuple-element.359, pred[512,512]{0,1:T(8,128)(4,1)S(1)} %broadcast_compare_fusion.4, bf16[2,512,16,64]{1,3,2,0:T(8,128)(2,1)} %get-tuple-element.393, ...), kind=kOutput, calls=%fused_computation.6.clone.1 | convolution fusion | flops 558366720 | bytes 19202052 | tf_op jit(solution)/shard_map/while/body/eval_jaxpr/hqk,khd->qhd/dot_general | solution.py:656
  254.4 1.0 constant_dynamic-update-slice_fusion.7
  255.6 5.5 fusion.77
  262.4 49.0 %multiply_convert_fusion.3 = (bf16[1024,4096]{1,0:T(8,128)(2,1)}, f32[1024,4096]{1,0:T(8,128)}, f32[1024,4096]{1,0:T(8,128)}) fusion(bf16[1024,4096]{1,0:T(8,128)(2,1)S(1)} %bitcast.185, f32[1024,1024]{1,0:T(8,128)S(1)} %get-tuple-element.250, f32[1024]{0:T(1024)S(1)} %bitcast.179, f32[1024]{0:T(1024)S(1)} %bitcast.171, f32[1024]{0:T(1024)S(1)} %fusion.56, ...), kind=kOutput, calls=%fused_computation.55 | convolution fusion | flops 8867807232 | bytes 54542336 | tf_op jit(solution)/shard_map/dot_general | solution.py:729
  311.4 14.1 %fusion.78 = (f32[1024]{0:T(1024)S(1)}, f32[1024,1024]{1,0:T(8,128)S(1)}) fusion(bf16[1024,4096]{1,0:T(8,128)(2,1)} %get-tuple-element.233, bf16[1024,4096]{1,0:T(8,128)(2,1)} %bitcast.186, f32[1024]{0:T(1024)S(1)} %bitcast.180, f32[1024]{0:T(1024)S(1)} %bitcast.172, f32[1024]{0:T(1024)S(1)} %fusion.56, f32[1024,1024]{1,0:T(8,128)S(1)} %get-tuple-element.250, ...), kind=kOutput, calls=%fused_computation.147 | convolution fusion | flops 8596225024 | bytes 25186304 | tf_op jit(solution)/shard_map/tf,df->td/dot_general | solution.py:656
  326.1 1.0 copy-done.6
  327.1 2.4 fusion.44
  329.5 4.2 fusion.73
  333.8 23.3 %add_convert_fusion = bf16[1024,4096]{1,0:T(8,128)(2,1)} fusion(f32[1024,4096]{1,0:T(8,128)} %get-tuple-element.234, f32[1024,4096]{1,0:T(8,128)} %get-tuple-element.251, bf16[1024,4096]{1,0:T(8,128)(2,1)} %bitcast.187, f32[1024,1024]{1,0:T(8,128)} %get-tuple-element.232, f32[1024]{0:T(1024)S(1)} %negate_multiply_fusion.2), kind=kOutput, calls=%fused_computation.54 | convolution fusion | flops 8650752000 | bytes 54530048 | tf_op jit(solution)/shard_map/dot_general | solution.py:738
  357.1 16.1 %multiply_reduce_fusion.1 = (f32[1024]{0:T(1024)}, f32[1024]{0:T(1024)S(1)}, f32[1024]{0:T(1024)}, f32[1024,1024]{1,0:T(8,128)S(1)}) fusion(f32[1024,1024]{1,0:T(8,128)S(1)} %get-tuple-element.250, f32[1024]{0:T(1024)S(1)} %fusion.56, f32[1024]{0:T(1024)S(1)} %broadcast_multiply_fusion.1, f32[1024]{0:T(1024)S(1)} %bitcast.173, ...), kind=kOutput, calls=%fused_computation.83 | convolution fusion | flops 8600417280 | bytes 29388800 | tf_op jit(solution)/shard_map/tf,cf->tc/dot_general | solution.py:656
  373.3 1.8 fusion.72
  375.7 3.7 convolution_convert_fusion.4
  379.5 1.7 broadcast.178.clone
  381.2 1.6 broadcast.178.clone2.1
  382.8 1.6 broadcast.178.clone2.2
  384.4 114.8 %while.27 = (s32[]{:T(128)}, bf16[2,512,1024]{2,1,0:T(8,128)(2,1)}, bf16[2,512,1024]{2,1,0:T(8,128)(2,1)}, bf16[2,512,1024]{2,1,0:T(8,128)(2,1)}, bf16[2,512,16,...) while((s32[]{:T(128)}, bf16[2,512,1024]{2,1,0:T(8,128)(2,1)}, ...), condition=%wide.region_14.15_spmd, body=%wide.region_12.14_spmd.sunk | while | flops 2724978688 | bytes 195730640 | solution.py:760
  384.8 11.4 %subtract_exponential_fusion.3 = f32[16,512,512]{1,2,0:T(8,128)} fusion(f32[16,512]{1,0:T(8,128)S(1)} %dynamic-slice_bitcast_fusion.2, pred[512,512]{0,1:T(8,128)(4,1)S(1)} %broadcast_compare_fusion.5, bf16[2,512,16,64]{1,3,2,0:T(8,128)(2,1)} %get-tuple-element.426, s32[]{:T(128)S(6)} %copy.124, bf16[2,512,16,64]{1,3,2,0:T(8,128)(2,1)} %get-tuple-element.424), kind=kOutput, calls=%fused_computation.24.clone.1 | convolution fusion | flops 549453824 | bytes 19170304 | tf_op jit(solution)/shard_map/while/body/eval_jaxpr/qhd,khd->hqk/dot_general | solution.py:656
  396.9 11.0 %multiply_reduce_fusion.6 = (f32[16,512]{1,0:T(8,128)S(1)}, f32[16,512,512]{1,2,0:T(8,128)}) fusion(f32[16,512,512]{1,2,0:T(8,128)} %subtract_exponential_fusion.3, bf16[512,16,64]{0,2,1:T(8,128)(2,1)S(1)} %bitcast.146, bf16[2,512,16,64]{1,3,2,0:T(8,128)(2,1)} %get-tuple-element.429, s32[]{:T(128)S(6)} %copy.124), kind=kOutput, calls=%fused_computation.23.clone.1 | convolution fusion | flops 545251328 | bytes 35684356 | tf_op jit(solution)/shard_map/while/body/eval_jaxpr/qhd,khd->hqk/dot_general | solution.py:656
  407.8 11.6 %multiply_convert_fusion.7 = bf16[16,512,512]{1,2,0:T(8,128)(2,1)S(1)} fusion(f32[16,512,512]{1,2,0:T(8,128)} %subtract_exponential_fusion.3, f32[16,512,512]{1,2,0:T(8,128)} %get-tuple-element.370, f32[16,512]{1,0:T(8,128)S(1)} %get-tuple-element.371), kind=kLoop, calls=%fused_computation.22.clone.1 | loop fusion | flops 12582912 | bytes 41975808 | tf_op jit(solution)/shard_map/while/body/eval_jaxpr/convert_element_type | solution.py:754
  419.4 3.5 multiply_convert_fusion.8
  423.4 1.0 constant_dynamic-update-slice_fusion.8
  424.5 8.4 %fusion.124 = bf16[16,64,512]{2,1,0:T(8,128)(2,1)S(1)} fusion(bf16[512,16,64]{0,2,1:T(8,128)(2,1)S(1)} %bitcast.147, f32[16,512,512]{1,2,0:T(8,128)} %subtract_exponential_fusion.3), kind=kOutput, calls=%fused_computation.29.clone.1 | convolution fusion | flops 541589504 | bytes 18874368 | tf_op jit(solution)/shard_map/while/body/eval_jaxpr/hqk,qhd->khd/dot_general | solution.py:656
  433.4 6.4 multiply_convert_fusion.9
  440.3 1.5 constant_dynamic-update-slice_fusion.9
  442.1 11.4 %subtract_exponential_fusion.3 = f32[16,512,512]{1,2,0:T(8,128)} fusion(f32[16,512]{1,0:T(8,128)S(1)} %dynamic-slice_bitcast_fusion.2, pred[512,512]{0,1:T(8,128)(4,1)S(1)} %broadcast_compare_fusion.5, bf16[2,512,16,64]{1,3,2,0:T(8,128)(2,1)} %get-tuple-element.426, s32[]{:T(128)S(6)} %copy.124, bf16[2,512,16,64]{1,3,2,0:T(8,128)(2,1)} %get-tuple-element.424), kind=kOutput, calls=%fused_computation.24.clone.1 | convolution fusion | flops 549453824 | bytes 19170304 | tf_op jit(solution)/shard_map/while/body/eval_jaxpr/qhd,khd->hqk/dot_general | solution.py:656
  454.1 11.0 %multiply_reduce_fusion.6 = (f32[16,512]{1,0:T(8,128)S(1)}, f32[16,512,512]{1,2,0:T(8,128)}) fusion(f32[16,512,512]{1,2,0:T(8,128)} %subtract_exponential_fusion.3, bf16[512,16,64]{0,2,1:T(8,128)(2,1)S(1)} %bitcast.146, bf16[2,512,16,64]{1,3,2,0:T(8,128)(2,1)} %get-tuple-element.429, s32[]{:T(128)S(6)} %copy.124), kind=kOutput, calls=%fused_computation.23.clone.1 | convolution fusion | flops 545251328 | bytes 35684356 | tf_op jit(solution)/shard_map/while/body/eval_jaxpr/qhd,khd->hqk/dot_general | solution.py:656
  465.1 11.6 %multiply_convert_fusion.7 = bf16[16,512,512]{1,2,0:T(8,128)(2,1)S(1)} fusion(f32[16,512,512]{1,2,0:T(8,128)} %subtract_exponential_fusion.3, f32[16,512,512]{1,2,0:T(8,128)} %get-tuple-element.370, f32[16,512]{1,0:T(8,128)S(1)} %get-tuple-element.371), kind=kLoop, calls=%fused_computation.22.clone.1 | loop fusion | flops 12582912 | bytes 41975808 | tf_op jit(solution)/shard_map/while/body/eval_jaxpr/convert_element_type | solution.py:754
  476.7 3.5 multiply_convert_fusion.8
  480.7 1.1 constant_dynamic-update-slice_fusion.8
  481.8 8.4 %fusion.124 = bf16[16,64,512]{2,1,0:T(8,128)(2,1)S(1)} fusion(bf16[512,16,64]{0,2,1:T(8,128)(2,1)S(1)} %bitcast.147, f32[16,512,512]{1,2,0:T(8,128)} %subtract_exponential_fusion.3), kind=kOutput, calls=%fused_computation.29.clone.1 | convolution fusion | flops 541589504 | bytes 18874368 | tf_op jit(solution)/shard_map/while/body/eval_jaxpr/hqk,qhd->khd/dot_general | solution.py:656
  490.8 6.4 multiply_convert_fusion.9
  497.7 1.5 constant_dynamic-update-slice_fusion.9
  499.2 13.3 %bitcast_add_fusion = f32[1024,1024]{1,0:T(8,128)} fusion(f32[1024,1024]{1,0:T(8,128)} %copy-done.7, f32[1024]{0:T(1024)S(1)} %copy-done.54, bf16[3,1024,1024]{2,1,0:T(8,128)(2,1)} %bitcast.189, bf16[1,1024,1024]{2,1,0:T(8,128)(2,1)} %bitcast.161, bf16[1,1024,1024]{2,1,0:T(8,128)(2,1)} %bitcast.159, bf16[1,1024,1024]{2,1,0:T(8,128)(2,1)} %bitcast.157), kind=kOutput, calls=%fused_computation.82 | convolution fusion | flops 6450839552 | bytes 20975616 | tf_op jit(solution)/shard_map/stn,scn->tc/dot_general | solution.py:656
  512.6 11.7 %convolution_convert_fusion.1 = bf16[1024,4096]{1,0:T(8,128)(2,1)} fusion(bf16[1024,4096]{1,0:T(8,128)(2,1)S(1)} %copy-done.61, f32[1024,1024]{1,0:T(8,128)S(1)} %copy-done.9, f32[1024]{0:T(1024)S(1)} %copy-done.52), kind=kOutput, calls=%fused_computation.70 | convolution fusion | flops 8596226048 | bytes 20975616 | tf_op jit(solution)/shard_map/td,tf->df/dot_general | solution.py:656
  524.3 15.4 %convolution_convert_fusion = bf16[1024,4096]{1,0:T(8,128)(2,1)} fusion(bf16[1024,4096]{1,0:T(8,128)(2,1)} %add_convert_fusion, f32[1024,1024]{1,0:T(8,128)S(1)} %copy-done.4, f32[1024]{0:T(1024)S(1)} %bitcast.181, f32[1024]{0:T(1024)S(1)} %bitcast.175, f32[1024]{0:T(1024)S(1)} %copy-done.43, f32[1024]{0:T(1024)S(1)} %copy-done.37), kind=kOutput, calls=%fused_computation.69 | convolution fusion | flops 8599371776 | bytes 20987904 | tf_op jit(solution)/shard_map/tc,tf->cf/dot_general | solution.py:656
  539.7 4.0 convolution_convert_fusion.3
  543.7 0.8 copy-done.59
  544.5 8.9 %convolution_convert_fusion.2 = bf16[3,1024,1024]{1,2,0:T(8,128)(2,1)} fusion(bf16[1,1024,1024]{2,1,0:T(8,128)(2,1)S(1)} %bitcast.162, bf16[1,1024,1024]{2,1,0:T(8,128)(2,1)S(1)} %bitcast.160, bf16[1,1024,1024]{2,1,0:T(8,128)(2,1)S(1)} %bitcast.158, bf16[2048,1024]{1,0:T(8,128)(2,1)S(1)} %copy-done.59, s32[]{:T(128)S(6)} %select_n.17), kind=kOutput, calls=%fused_computation.93 | convolution fusion | flops 6451888128 | bytes 14680068 | tf_op jit(solution)/shard_map/tc,stn->scn/dot_general | solution.py:656
  554.3 181.5 %scatter_grads.1 = (f32[64,2048]{1,0:T(8,128)}, f32[64,2048]{1,0:T(8,128)}, f32[64,512]{1,0:T(8,128)}, f32[3,64,512]{2,1,0:T(8,128)}, f32[8,1024]{1,0:T(8,128)}) custom-call(bf16[4,2,2,64,4096]{4,3,2,1,0:T(8,128)(2,1)} %bitcast.153, bf16[4,2,2,64,4096]{4,3,2,1,0:T(8,128)(2,1)} %bitcast.154, bf16[4,2,2,64,1024]{4,3,2,1,0:T(8,128)(2,1)} %bitcast.156, ...), custom_call_target="tpu_custom_call" | custom-call | tf_op jit(solution)/shard_map/scatter_grads/pallas_call | solution.py:633
  735.8 2.2 multiply_subtract_fusion.2
  738.0 1.8 multiply_subtract_fusion.3
  739.9 3.6 multiply_subtract_fusion
  743.5 1.3 multiply_subtract_fusion.4
  (177 shorter events, 14.4 us)
Async XLA Ops:
  0.7 183.6 %copy-start = (s32[4,512]{1,0:T(4,128)S(1)}, s32[4,512]{1,0:T(4,128)}, u32[]{:S(2)}) copy-start(s32[4,512]{1,0:T(4,128)} %param.24) | copy-start | bytes 24580
  255.5 5.5 copy-start.26
  255.5 5.5 copy-start.30
  255.5 6.8 slice-start
  255.5 5.5 copy-start.48
  255.5 6.8 slice-start.1
  261.0 112.2 %copy-start.3 = (f32[1024,1024]{1,0:T(8,128)}, f32[1024,1024]{1,0:T(8,128)S(1)}, u32[]{:S(2)}) copy-start(f32[1024,1024]{1,0:T(8,128)S(1)} %get-tuple-element.250) | copy-start | bytes 12582916
  261.7 49.7 %copy-start.55 = (f32[1,1024]{1,0:T(1,128)}, f32[1,1024]{1,0:T(1,128)S(1)}, u32[]{:S(2)}) copy-start(f32[1,1024]{1,0:T(1,128)S(1)} %get-tuple-element.247) | copy-start | bytes 12292
  261.7 111.5 %copy-start.44 = (f32[1,1024]{1,0:T(1,128)}, f32[1,1024]{1,0:T(1,128)S(1)}, u32[]{:S(2)}) copy-start(f32[1,1024]{1,0:T(1,128)S(1)} %get-tuple-element.248) | copy-start | bytes 12292
  261.7 111.5 %copy-start.36 = (f32[1024]{0:T(1024)}, f32[1024]{0:T(1024)S(1)}, u32[]{:S(2)}) copy-start(f32[1024]{0:T(1024)S(1)} %broadcast_multiply_fusion.1) | copy-start | bytes 12292
  262.3 49.1 %copy-start.38 = (f32[1024]{0:T(1024)}, f32[1024]{0:T(1024)S(1)}, u32[]{:S(2)}) copy-start(f32[1024]{0:T(1024)S(1)} %multiply_reduce_fusion.4) | copy-start | bytes 12292
  262.3 110.9 %copy-start.42 = (f32[1024]{0:T(1024)}, f32[1024]{0:T(1024)S(1)}, u32[]{:S(2)}) copy-start(f32[1024]{0:T(1024)S(1)} %fusion.56) | copy-start | bytes 12292
  325.5 1.6 copy-start.6
  325.5 1.6 copy-start.35
  326.1 3.5 copy-start.46
  333.8 23.3 %copy-start.51 = (f32[1024]{0:T(1024)}, f32[1024]{0:T(1024)S(1)}, u32[]{:S(2)}) copy-start(f32[1024]{0:T(1024)S(1)} %negate_multiply_fusion.2) | copy-start | bytes 12292
  357.1 16.1 %copy-start.39 = (f32[1024]{0:T(1024)S(1)}, f32[1024]{0:T(1024)}, u32[]{:S(2)}) copy-start(f32[1024]{0:T(1024)} %copy-done.38) | copy-start | bytes 12292
  373.3 2.5 copy-start.60
  375.1 4.4 copy-start.7
  379.5 4.9 copy-start.27
  379.5 4.9 copy-start.31
  384.4 114.8 %copy-start.54 = (f32[1024]{0:T(1024)S(1)}, f32[1024]{0:T(1024)}, u32[]{:S(2)}) copy-start(f32[1024]{0:T(1024)} %copy-done.53) | copy-start | bytes 12292
  384.8 11.4 %copy-start.5 = (bf16[2,512,1024]{2,1,0:T(8,128)(2,1)S(1)}, bf16[2,512,1024]{2,1,0:T(8,128)(2,1)}, u32[]{:S(2)}) copy-start(bf16[2,512,1024]{2,1,0:T(8,128)(2,1)} %get-tuple-element.428) | copy-start | bytes 6291460 | tf_op jit(solution)/shard_map/while
  419.4 3.5 copy-start.2
  442.1 11.4 %copy-start.5 = (bf16[2,512,1024]{2,1,0:T(8,128)(2,1)S(1)}, bf16[2,512,1024]{2,1,0:T(8,128)(2,1)}, u32[]{:S(2)}) copy-start(bf16[2,512,1024]{2,1,0:T(8,128)(2,1)} %get-tuple-element.428) | copy-start | bytes 6291460 | tf_op jit(solution)/shard_map/while
  476.7 3.5 copy-start.2
  499.2 13.3 %copy-start.9 = (f32[1024,1024]{1,0:T(8,128)S(1)}, f32[1024,1024]{1,0:T(8,128)}, u32[]{:S(2)}) copy-start(f32[1024,1024]{1,0:T(8,128)} %get-tuple-element.232) | copy-start | bytes 12582916
  499.2 13.3 %copy-start.52 = (f32[1024]{0:T(1024)S(1)}, f32[1024]{0:T(1024)}, u32[]{:S(2)}) copy-start(f32[1024]{0:T(1024)} %copy-done.51) | copy-start | bytes 12292
  499.2 13.3 %copy-start.61 = (bf16[1024,4096]{1,0:T(8,128)(2,1)S(1)}, bf16[1024,4096]{1,0:T(8,128)(2,1)}, u32[]{:S(2)}) copy-start(bf16[1024,4096]{1,0:T(8,128)(2,1)} %get-tuple-element.233) | copy-start | bytes 25165828
  512.5 11.7 %copy-start.4 = (f32[1024,1024]{1,0:T(8,128)S(1)}, f32[1024,1024]{1,0:T(8,128)}, u32[]{:S(2)}) copy-start(f32[1024,1024]{1,0:T(8,128)} %copy-done.3) | copy-start | bytes 12582916
  512.5 11.7 %copy-start.37 = (f32[1024]{0:T(1024)S(1)}, f32[1024]{0:T(1024)}, u32[]{:S(2)}) copy-start(f32[1024]{0:T(1024)} %copy-done.36) | copy-start | bytes 12292
  512.6 11.7 %copy-start.43 = (f32[1024]{0:T(1024)S(1)}, f32[1024]{0:T(1024)}, u32[]{:S(2)}) copy-start(f32[1024]{0:T(1024)} %copy-done.42) | copy-start | bytes 12292
  512.6 11.7 %copy-start.45 = (f32[1,1024]{1,0:T(1,128)S(1)}, f32[1,1024]{1,0:T(1,128)}, u32[]{:S(2)}) copy-start(f32[1,1024]{1,0:T(1,128)} %copy-done.44) | copy-start | bytes 12292
  512.6 11.7 %copy-start.56 = (f32[1,1024]{1,0:T(1,128)S(1)}, f32[1,1024]{1,0:T(1,128)}, u32[]{:S(2)}) copy-start(f32[1,1024]{1,0:T(1,128)} %copy-done.55) | copy-start | bytes 12292
  524.3 15.4 %copy-start.8 = (f32[1024,1024]{1,0:T(8,128)S(1)}, f32[1024,1024]{1,0:T(8,128)}, u32[]{:S(2)}) copy-start(f32[1024,1024]{1,0:T(8,128)} %copy-done.7) | copy-start | bytes 12582916
  524.3 15.4 %copy-start.17 = (bf16[2,512,1024]{2,1,0:T(8,128)(2,1)S(1)}, bf16[2,512,1024]{2,1,0:T(8,128)(2,1)}, u32[]{:S(2)}) copy-start(bf16[2,512,1024]{2,1,0:T(8,128)(2,1)} %get-tuple-element.125) | copy-start | bytes 6291460
  539.7 4.0 copy-start.14
  539.7 4.0 copy-start.15
  539.7 4.0 copy-start.16
  539.7 4.8 copy-start.59
  544.5 9.0 %copy-start.40 = (f32[1024]{0:T(1024)S(1)}, f32[1024]{0:T(1024)}, u32[]{:S(2)}) copy-start(f32[1024]{0:T(1024)} %get-tuple-element.175) | copy-start | bytes 12292
  544.5 9.0 %copy-start.41 = (f32[1024]{0:T(1024)S(1)}, f32[1024]{0:T(1024)}, u32[]{:S(2)}) copy-start(f32[1024]{0:T(1024)} %get-tuple-element.178) | copy-start | bytes 12292
  544.5 9.0 %copy-start.49 = (f32[1024]{0:T(1024)S(1)}, f32[1024]{0:T(1024)}, u32[]{:S(2)}) copy-start(f32[1024]{0:T(1024)} %get-tuple-element.173) | copy-start | bytes 12292
  544.5 9.0 %copy-start.50 = (f32[1024]{0:T(1024)S(1)}, f32[1024]{0:T(1024)}, u32[]{:S(2)}) copy-start(f32[1024]{0:T(1024)} %get-tuple-element.177) | copy-start | bytes 12292
  554.2 181.6 %copy-start.18 = (f32[3,64,512]{2,1,0:T(8,128)S(1)}, f32[3,64,512]{2,1,0:T(8,128)}, u32[]{:S(2)}) copy-start(f32[3,64,512]{2,1,0:T(8,128)} %param.25) | copy-start | bytes 1179652
  554.2 181.6 %copy-start.28 = (f32[3,64,512]{2,1,0:T(8,128)S(1)}, f32[3,64,512]{2,1,0:T(8,128)}, u32[]{:S(2)}) copy-start(f32[3,64,512]{2,1,0:T(8,128)} %param.27) | copy-start | bytes 1179652
  554.2 181.6 %copy-start.29 = (f32[3,64,512]{2,1,0:T(8,128)S(1)}, f32[3,64,512]{2,1,0:T(8,128)}, u32[]{:S(2)}) copy-start(f32[3,64,512]{2,1,0:T(8,128)} %param.26) | copy-start | bytes 1179652
  554.2 183.9 %copy-start.24 = (f32[64,512]{1,0:T(8,128)S(1)}, f32[64,512]{1,0:T(8,128)}, u32[]{:S(2)}) copy-start(f32[64,512]{1,0:T(8,128)} %param.28) | copy-start | bytes 393220
  554.2 183.9 %copy-start.32 = (f32[64,512]{1,0:T(8,128)S(1)}, f32[64,512]{1,0:T(8,128)}, u32[]{:S(2)}) copy-start(f32[64,512]{1,0:T(8,128)} %param.30) | copy-start | bytes 393220
  554.2 183.9 %copy-start.33 = (f32[64,512]{1,0:T(8,128)S(1)}, f32[64,512]{1,0:T(8,128)}, u32[]{:S(2)}) copy-start(f32[64,512]{1,0:T(8,128)} %param.29) | copy-start | bytes 393220
  554.2 185.6 %copy-start.10 = (f32[64,2048]{1,0:T(8,128)S(1)}, f32[64,2048]{1,0:T(8,128)}, u32[]{:S(2)}) copy-start(f32[64,2048]{1,0:T(8,128)} %param.31) | copy-start | bytes 1572868
  554.2 185.6 %copy-start.11 = (f32[64,2048]{1,0:T(8,128)S(1)}, f32[64,2048]{1,0:T(8,128)}, u32[]{:S(2)}) copy-start(f32[64,2048]{1,0:T(8,128)} %param.34) | copy-start | bytes 1572868
  554.2 185.6 %copy-start.20 = (f32[64,2048]{1,0:T(8,128)S(1)}, f32[64,2048]{1,0:T(8,128)}, u32[]{:S(2)}) copy-start(f32[64,2048]{1,0:T(8,128)} %param.36) | copy-start | bytes 1572868
  554.2 185.6 %copy-start.21 = (f32[64,2048]{1,0:T(8,128)S(1)}, f32[64,2048]{1,0:T(8,128)}, u32[]{:S(2)}) copy-start(f32[64,2048]{1,0:T(8,128)} %param.35) | copy-start | bytes 1572868
  554.2 185.6 %copy-start.22 = (f32[64,2048]{1,0:T(8,128)S(1)}, f32[64,2048]{1,0:T(8,128)}, u32[]{:S(2)}) copy-start(f32[64,2048]{1,0:T(8,128)} %param.33) | copy-start | bytes 1572868
  554.2 185.6 %copy-start.23 = (f32[64,2048]{1,0:T(8,128)S(1)}, f32[64,2048]{1,0:T(8,128)}, u32[]{:S(2)}) copy-start(f32[64,2048]{1,0:T(8,128)} %param.32) | copy-start | bytes 1572868
  738.0 5.5 copy-start.47
  738.0 5.5 copy-start.57
  738.0 5.5 copy-start.58
  738.0 6.8 copy-start.19
  739.8 5.8 copy-start.25
  739.8 8.0 %copy-start.1 = (s32[4,512]{1,0:T(4,128)S(1)}, s32[4,512]{1,0:T(4,128)}, u32[]{:S(2)}) copy-start(s32[4,512]{1,0:T(4,128)} %param.24) | copy-start | bytes 24580
  739.9 6.4 copy-start.13
  739.9 7.1 copy-start.12
  (2 other events, 1.3 us)

commit v2 on v1

--- a/solution.py
+++ b/solution.py
@@ -311,9 +311,8 @@
         )
 
     def send(self, rel, hop):
-        copy = self.copy(rel, hop)
-        copy.start()
-        self.sent.append(copy)
+        self.copy(rel, hop).start()
+        self.sent.append((rel, hop))
 
     def wait(self, rel):
         pltpu.make_async_remote_copy(
@@ -365,8 +364,8 @@
         return [("wait", (a, b, 1, e), None) for a in range(self.nz) for b in range(2) for e in range(2)]
 
     def drain(self):
-        for copy in self.sent:
-            copy.wait_send()
+        for rel, hop in self.sent:
+            self.copy(rel, hop).wait_send()
 
 
 def sum_hops(nz):
@@ -398,78 +397,6 @@
     def finish(self, i):
         self.copy(i).wait()
         self.parts[i + 1] = self.parts[i] + self.came[i]
-
-
-def gather_kernel(nz, proj, out, up, down, norm, proj_all, out_all, up_all, down_all, norm_all,
-                  send_sem, recv_sem, local_sem, parts, came, sum_send, sum_recv):
-    me = position()
-    entry_barrier(me, nz)
-    n = 8 * nz
-    small = SmallSum(me, nz, parts, came, sum_send, sum_recv)
-    parts[0] = norm[...]
-    owns, fulls = (proj, out, up, down), (proj_all, out_all, up_all, down_all)
-    views = (view_stack, view_rows, view_rows, view_rows)
-    gathers = [
-        Gather(me, nz, owns[i], fulls[i], views[i], send_sem, recv_sem, n * i) for i in range(4)
-    ]
-    locals_ = [pltpu.make_async_copy(g.own, g.piece(OWN), local_sem.at[i]) for i, g in enumerate(gathers)]
-    for copy in locals_:
-        copy.start()
-    for i in range(len(small.hops)):
-        small.start(i)
-        small.finish(i)
-    norm_all[...] = parts[len(small.hops)]
-    gathers[0].run(gathers[0].steps_first())
-    for i, g in enumerate(gathers):
-        g.run(g.steps_middle())
-        if i + 1 < len(gathers):
-            gathers[i + 1].run(gathers[i + 1].steps_first())
-        g.run(g.steps_diagonal())
-        g.run(g.steps_last())
-    for copy in locals_:
-        copy.wait()
-    for g in gathers:
-        g.drain()
-
-
-def gather_weights(nz, proj, out, up, down, norm):
-    n_sum = len(sum_hops(nz))
-    full = lambda s: jax.ShapeDtypeStruct((nz, 2, 2, s.shape[0], s.shape[1] * 2), BF16)
-    results = pl.pallas_call(
-        functools.partial(gather_kernel, nz),
-        out_shape=[
-            jax.ShapeDtypeStruct((3, nz, 2, 2, proj.shape[1], proj.shape[2] * 2), BF16),
-            full(out),
-            full(up),
-            full(down),
-            jax.ShapeDtypeStruct(norm.shape, F32),
-        ],
-        in_specs=[ANY] * 4 + [VMEM],
-        out_specs=[ANY] * 4 + [VMEM],
-        scratch_shapes=[
-            DMA((32 * nz,)),
-            DMA((32 * nz,)),
-            DMA((4,)),
-            pltpu.VMEM((n_sum + 1,) + norm.shape, F32),
-            pltpu.VMEM((n_sum,) + norm.shape, F32),
-            DMA((n_sum,)),
-            DMA((n_sum,)),
-        ],
-        compiler_params=pltpu.CompilerParams(collective_id=0, has_side_effects=True),
-        name="gather_weights",
-    )(proj, out, up, down, norm)
-    proj_all, out_all, up_all, down_all, norm_all = results
-    return (
-        proj_all.reshape(3, D, -1),
-        out_all.reshape(D, -1),
-        up_all.reshape(D, -1),
-        down_all.reshape(D, -1),
-        norm_all,
-    )
-
-
-def blocks_of(ref, rows=16):
-    return ref.shape[-2] // rows
 
 
 def add_blocks(dst, terms, rows=16):
@@ -652,6 +579,356 @@
     )(*grads, norm)
 
 
+ERFC_SLOPE = 0.33 * 0.5**0.5
+ERFC_POLY = (
+    0.1863683316091749,
+    0.1828075671230129,
+    0.2020873146971517,
+    0.044528074107268695,
+    0.41336767744180025,
+    -0.35626105794547547,
+    0.4631297570306923,
+    -0.13602774732192066,
+)
+PDF_SCALE = 0.3989422804014327
+
+
+def gelu_pair(u):
+    size = jnp.abs(u)
+    t = 1.0 / (1.0 + ERFC_SLOPE * size)
+    poly = 0.5 * ERFC_POLY[-1]
+    for coefficient in ERFC_POLY[-2::-1]:
+        poly = poly * t + 0.5 * coefficient
+    bell = jnp.exp(u * u * -0.5)
+    tail = poly * t * bell
+    phi = jnp.where(u >= 0.0, 1.0 - tail, tail)
+    return u * phi, phi + u * bell * PDF_SCALE
+
+
+def dot_nn(a, b):
+    return jnp.dot(a, b, preferred_element_type=F32)
+
+
+def dot_nt(a, b):
+    return lax.dot_general(a, b, (((1,), (1,)), ((), ())), preferred_element_type=F32)
+
+
+def normed(rows):
+    center = rows - jnp.mean(rows, axis=-1, keepdims=True)
+    scale = lax.rsqrt(jnp.mean(center * center, axis=-1, keepdims=True) + EPS_NORM)
+    return center * scale, scale
+
+
+def norm_backward(grad, n, scale):
+    inner = jnp.mean(grad * n, axis=-1, keepdims=True)
+    return scale * (grad - jnp.mean(grad, axis=-1, keepdims=True) - n * inner)
+
+
+def at_slots(i, plan):
+    for k in sorted(plan):
+        @pl.when(i == k)
+        def _(k=k):
+            for call in plan[k]:
+                call()
+
+
+def phase(count, body, plan):
+    def step(i, carry):
+        at_slots(i, plan)
+        body(i)
+        return carry
+
+    lax.fori_loop(0, count, step, 0)
+
+
+def spread(calls, spans):
+    plans, calls = [{} for _ in spans], list(calls)
+    for plan, (count, start, each) in zip(plans, spans):
+        for i in range(count):
+            while calls and calls[0][0] <= start + i * each:
+                plan.setdefault(i, []).append(calls.pop(0)[1])
+    return plans, [call for _, call in calls]
+
+
+def gather_calls(gathers, costs, start):
+    calls, marks, clock = [], [], start
+    nz = gathers[0].nz
+
+    def add(when, g, steps):
+        calls.append((when, functools.partial(g.run, steps)))
+
+    for i, (g, cost) in enumerate(zip(gathers, costs)):
+        first = g.steps_first()
+        if i == 0:
+            add(clock, g, first)
+        unit = cost / (3 * nz - 1)
+        tick = 0
+        for a in range(1, nz):
+            tick += 1
+            add(clock + tick * unit, g, g.steps_level(a))
+            if a == nz - 1 and i + 1 < len(gathers):
+                add(clock + tick * unit, gathers[i + 1], gathers[i + 1].steps_first()[2:-1])
+            tick += 1
+            add(clock + tick * unit, g, g.steps_square(a - 1))
+        tick += 1
+        add(clock + tick * unit, g, g.steps_square(nz - 1))
+        if i + 1 < len(gathers):
+            nxt = gathers[i + 1].steps_first()
+            add(clock + tick * unit, gathers[i + 1], nxt[:2] + nxt[-1:])
+        steps = g.steps_diagonal()
+        for a in range(nz):
+            tick += 1
+            add(clock + tick * unit, g, steps[2 * a : 2 * a + 2])
+        add(clock + cost, g, g.steps_last())
+        marks.append(len(calls))
+        clock += cost
+    return calls, marks
+
+
+def forward_kernel(nz, tokens, cotangent, seg_col, seg_row, proj, out, up, down, norm,
+                   proj_all, out_all, up_all, down_all, norm_all, qkv_out, ctx_out, lse,
+                   resid_out, hidden_out, act_out, slope_out, layer_out, dres_out, dffn_out, dnorm,
+                   tok, cot, w_small, w_up, qkv, ctx, bias, res, hidden, act, pre, slope,
+                   send_sem, recv_sem, local_sem, parts, came, sum_send, sum_recv, io_sem):
+    me = position()
+    t_here, seq = tok.shape[0], seg_row.shape[2]
+    rows_here, pairs = t_here // seq, D // 128
+    copies = {}
+
+    def begin(key, src, dst, sem):
+        copies[key] = pltpu.make_async_copy(src, dst, io_sem.at[sem])
+        copies[key].start()
+
+    mine = pl.ds(pl.multiple_of(me[3] * t_here, t_here), t_here)
+    begin("tok", tokens.at[mine, :], tok, 0)
+    begin("cot", cotangent, cot, 1)
+    parts[0] = norm[...]
+    entry_barrier(me, nz)
+    owns, fulls = (proj, out, up, down), (proj_all, out_all, up_all, down_all)
+    views = (view_stack, view_rows, view_rows, view_rows)
+    n = 8 * nz
+    gathers = [
+        Gather(me, nz, owns[i], fulls[i], views[i], send_sem, recv_sem, n * i) for i in range(4)
+    ]
+    keep = [pltpu.make_async_copy(g.own, g.piece(OWN), local_sem.at[i]) for i, g in enumerate(gathers)]
+    costs = FORWARD_COSTS
+    calls, marks = gather_calls(gathers, costs, 0.0)
+    calls[0][1]()
+    for copy in keep:
+        copy.start()
+    small = SmallSum(me, nz, parts, came, sum_send, sum_recv)
+    for i in range(len(small.hops)):
+        small.start(i)
+        small.finish(i)
+    norm_all[...] = parts[len(small.hops)]
+
+    def bias_step(r):
+        rows = pl.ds(pl.multiple_of(r * seq, seq), seq)
+        same = seg_col[rows, 0:1] == seg_row[r]
+        bias[r] = jnp.where(same, 0.0, NEG_FILL)
+
+    phase(rows_here, bias_step, {})
+    for _, call in calls[1 : marks[0]]:
+        call()
+    for copy in keep:
+        copy.wait()
+    copies["tok"].wait()
+    begin("proj", proj_all, w_small.at[pl.ds(0, 3)], 2)
+
+    step_q, step_a, step_o, step_u = FORWARD_STEPS
+    n_q, n_a, n_o, n_u = 3 * D // 256, rows_here * pairs, t_here // 256, FF // 256
+    start_q = costs[0] + 2.0
+    start_a = start_q + n_q * step_q
+    plans, _ = spread(
+        calls[marks[0] : marks[2]], [(n_q, start_q, step_q), (n_a, start_a, step_a)]
+    )
+    done = sum(len(c) for plan in plans for c in plan.values())
+    rest_out = calls[marks[0] + done : marks[1]]
+    later = marks[0] + done + len(rest_out)
+    copies["proj"].wait()
+
+    def qkv_step(j):
+        s, col = j // (D // 256), pl.ds(pl.multiple_of((j % (D // 256)) * 256, 256), 256)
+        weight = w_small[s, :, :, :, :, col].reshape(D, 256)
+        qkv[s, :, col] = dot_nn(tok[...], weight).astype(BF16)
+
+    phase(n_q, qkv_step, plans[0])
+    begin("qkv", qkv, qkv_out, 3)
+    head_of = lax.broadcasted_iota(jnp.int32, (128, 128), 1) // HEAD_DIM
+
+    def attend_step(u):
+        r, p = u // pairs, u % pairs
+        col = pl.ds(pl.multiple_of(p * 128, 128), 128)
+        for qb in range(seq // 128):
+            low, high = max(0, qb - 2) * 128, min(seq // 128, qb + 3) * 128
+            q_rows = pl.ds(pl.multiple_of(r * seq + qb * 128, 128), 128)
+            k_rows = pl.ds(pl.multiple_of(r * seq + low, 128), high - low)
+            q = qkv[0, q_rows, col] * jnp.asarray(HEAD_DIM**-0.5, BF16)
+            both = jnp.concatenate([jnp.where(head_of == h, q, jnp.zeros_like(q)) for h in range(2)])
+            block = bias[r, qb * 128 : qb * 128 + 128, low:high]
+            scores = dot_nt(both, qkv[1, k_rows, col]) + jnp.concatenate([block, block])
+            top = jnp.max(scores, axis=-1, keepdims=True)
+            weights = jnp.exp(scores - top)
+            total = jnp.sum(weights, axis=-1, keepdims=True)
+            probs = (weights * (1.0 / total)).astype(BF16)
+            mixed = dot_nn(probs, qkv[2, k_rows, col])
+            ctx[q_rows, col] = jnp.where(head_of == 0, mixed[:128], mixed[128:]).astype(BF16)
+            level = top + jnp.log(total)
+            for h in range(2):
+                wide = jnp.broadcast_to(level[h * 128 : h * 128 + 128], (128, 128))
+                lse[u, h : h + 1, qb * 128 : qb * 128 + 128] = wide.T[0:1]
+
+    phase(n_a, attend_step, plans[1])
+    for _, call in rest_out:
+        call()
+    begin("out", out_all, w_small.at[3], 4)
+    begin("ctx", ctx, ctx_out, 5)
+    start_o = max(start_a + n_a * step_a, costs[0] + costs[1])
+    plans, rest_up = spread(calls[later : marks[2]], [(n_o, start_o, step_o)])
+    copies["out"].wait()
+
+    def out_step(m):
+        rows = pl.ds(pl.multiple_of(m * 256, 256), 256)
+        attended = dot_nt(ctx[rows, :], w_small[3].reshape(D, D))
+        total = tok[rows, :].astype(F32) + attended
+        res[rows, :] = total
+        unit, _ = normed(total)
+        hidden[rows, :] = (unit * norm_all[0:1, :] + norm_all[1:2, :]).astype(BF16)
+
+    phase(n_o, out_step, plans[0])
+    begin("res", res, resid_out, 6)
+    begin("hidden", hidden, hidden_out, 7)
+    for call in rest_up:
+        call()
+    begin("up", up_all, w_up, 8)
+    start_u = costs[0] + costs[1] + costs[2] + 2.0
+    plans, rest_down = spread(calls[marks[2] :], [(n_u, start_u, step_u)])
+    copies["up"].wait()
+
+    def up_step(j):
+        col = pl.ds(pl.multiple_of(j * 256, 256), 256)
+        slot = j % 2
+        pre[...] = dot_nn(hidden[...], w_up[:, :, :, :, col].reshape(D, 256))
+
+        @pl.when(j >= 2)
+        def _():
+            slope_copy(j - 2, slot).wait()
+
+        def chunk(i, carry):
+            rows = pl.ds(pl.multiple_of(i * 32, 32), 32)
+            value, tangent = gelu_pair(pre[rows, :])
+            act[rows, col] = value.astype(BF16)
+            slope[slot, rows, :] = tangent.astype(BF16)
+            return carry
+
+        lax.fori_loop(0, t_here // 32, chunk, 0)
+        slope_copy(j, slot).start()
+
+    def slope_copy(j, slot):
+        col = pl.ds(pl.multiple_of(j * 256, 256), 256)
+        return pltpu.make_async_copy(slope.at[slot], slope_out.at[:, col], io_sem.at[9 + slot])
+
+    phase(n_u, up_step, plans[0])
+    begin("act", act, act_out, 11)
+    for call in rest_down:
+        call()
+    for k in range(4):
+        begin(("down", k), down_all.at[:, :, :, :, pl.ds(k * D, D)], w_small.at[k], 12 + k)
+    for j in (n_u - 2, n_u - 1):
+        slope_copy(j, j % 2).wait()
+    for key in ("cot", "res", "hidden") + tuple(("down", k) for k in range(4)):
+        copies[key].wait()
+    dnorm[...] = jnp.zeros_like(dnorm)
+
+    def down_step(m):
+        rows = pl.ds(pl.multiple_of(m * 256, 256), 256)
+        unit, _ = normed(res[rows, :])
+        total = unit * norm_all[0:1, :] + norm_all[1:2, :]
+        for k in range(4):
+            total = total + dot_nt(act[rows, k * D : (k + 1) * D], w_small[k].reshape(D, D))
+        unit, scale = normed(total)
+        tok[rows, :] = (unit * norm_all[2:3, :] + norm_all[3:4, :]).astype(BF16)
+        grad = cot[rows, :].astype(F32)
+        dnorm[0:1, :] = dnorm[0:1, :] + jnp.sum(grad * unit, axis=0, keepdims=True)
+        dnorm[1:2, :] = dnorm[1:2, :] + jnp.sum(grad, axis=0, keepdims=True)
+        dres = norm_backward(grad * norm_all[2:3, :], unit, scale)
+        res[rows, :] = dres
+        hidden[rows, :] = dres.astype(BF16)
+
+    phase(t_here // 256, down_step, {})
+    begin("layer", tok, layer_out, 16)
+    begin("dres", res, dres_out, 17)
+    begin("dffn", hidden, dffn_out, 18)
+    for key in ("qkv", "ctx", "act", "layer", "dres", "dffn"):
+        copies[key].wait()
+    for g in gathers:
+        g.drain()
+
+
+FORWARD_COSTS = (31.0, 10.0, 42.0, 42.0)
+FORWARD_STEPS = (0.8, 1.4, 1.2, 1.7)
+
+
+def run_forward(nz, tokens_in, cotangent, segments, proj, out, up, down, norm):
+    t_here = cotangent.shape[0]
+    rows_here, seq = segments.shape
+    n_sum = len(sum_hops(nz))
+    rows = D // (4 * nz)
+    full = lambda cols: jax.ShapeDtypeStruct((nz, 2, 2, rows, cols), BF16)
+    flat = lambda cols, kind: jax.ShapeDtypeStruct((t_here, cols), kind)
+    seg_col = jnp.broadcast_to(segments.reshape(t_here, 1), (t_here, 128))
+    seg_row = segments.reshape(rows_here, 1, seq)
+    return pl.pallas_call(
+        functools.partial(forward_kernel, nz),
+        out_shape=[
+            jax.ShapeDtypeStruct((3, nz, 2, 2, rows, D), BF16),
+            full(D),
+            full(FF),
+            full(FF),
+            jax.ShapeDtypeStruct(norm.shape, F32),
+            jax.ShapeDtypeStruct((3, t_here, D), BF16),
+            flat(D, BF16),
+            jax.ShapeDtypeStruct((rows_here * (D // 128), 8, seq), F32),
+            flat(D, F32),
+            flat(D, BF16),
+            flat(FF, BF16),
+            flat(FF, BF16),
+            flat(D, BF16),
+            flat(D, F32),
+            flat(D, BF16),
+            jax.ShapeDtypeStruct((8, D), F32),
+        ],
+        in_specs=[ANY, ANY, VMEM, VMEM, ANY, ANY, ANY, ANY, VMEM],
+        out_specs=[ANY] * 4 + [VMEM, ANY, ANY, VMEM] + [ANY] * 7 + [VMEM],
+        scratch_shapes=[
+            pltpu.VMEM((t_here, D), BF16),
+            pltpu.VMEM((t_here, D), BF16),
+            pltpu.VMEM((4, nz, 2, 2, rows, D), BF16),
+            pltpu.VMEM((nz, 2, 2, rows, FF), BF16),
+            pltpu.VMEM((3, t_here, D), BF16),
+            pltpu.VMEM((t_here, D), BF16),
+            pltpu.VMEM((rows_here, seq, seq), F32),
+            pltpu.VMEM((t_here, D), F32),
+            pltpu.VMEM((t_here, D), BF16),
+            pltpu.VMEM((t_here, FF), BF16),
+            pltpu.VMEM((t_here, 256), F32),
+            pltpu.VMEM((2, t_here, 256), BF16),
+            DMA((32 * nz,)),
+            DMA((32 * nz,)),
+            DMA((4,)),
+            pltpu.VMEM((n_sum + 1,) + norm.shape, F32),
+            pltpu.VMEM((n_sum,) + norm.shape, F32),
+            DMA((n_sum,)),
+            DMA((n_sum,)),
+            DMA((19,)),
+        ],
+        compiler_params=pltpu.CompilerParams(
+            collective_id=0, has_side_effects=True, vmem_limit_bytes=60 << 20
+        ),
+        name="forward",
+    )(tokens_in, cotangent, seg_col, seg_row, proj, out, up, down, norm)
+
+
 def dot_f32(spec, a, b):
     return jnp.einsum(spec, a, b, preferred_element_type=F32)
 
@@ -683,63 +960,44 @@
     norm_wide = lax.dynamic_update_slice(
         jnp.zeros((8, D), F32), norm_params.astype(BF16).astype(F32), (0, norm_start)
     )
-    proj_w, out_w, up_w, down_w, norm_full = gather_weights(
+    rows_here = segment_ids.shape[0] // 2
+    seq_len = segment_ids.shape[1]
+    tokens_here = rows_here * seq_len
+    heads = D // HEAD_DIM
+    score_scale = HEAD_DIM ** (-0.5)
+    segments = lax.dynamic_slice_in_dim(segment_ids, mp * rows_here, rows_here, 0)
+    (proj_w, out_w, up_w, down_w, norm_full, qkv, context, lse, resid_one, hidden_low, act_low, slope,
+     layer_out, d_resid_two, d_ffn, d_norm_two) = run_forward(
         nz,
+        tokens_in,
+        cotangent,
+        segments,
         project_weight.astype(BF16),
         output_weight.astype(BF16),
         up_weight.astype(BF16),
         down_weight.astype(BF16),
         norm_wide,
     )
-    rows_here = segment_ids.shape[0] // 2
-    seq_len = segment_ids.shape[1]
-    tokens_here = rows_here * seq_len
-    heads = D // HEAD_DIM
-    score_scale = HEAD_DIM ** (-0.5)
+    proj_w, out_w = proj_w.reshape(3, D, D), out_w.reshape(D, D)
+    up_w, down_w = up_w.reshape(D, FF), down_w.reshape(D, FF)
     tokens = lax.dynamic_slice_in_dim(tokens_in, mp * tokens_here, tokens_here, 0)
-    segments = lax.dynamic_slice_in_dim(segment_ids, mp * rows_here, rows_here, 0)
-    projected = dot_f32("tc,scn->stn", tokens, proj_w).astype(BF16)
-    heads_split = projected.reshape(3, rows_here, seq_len, heads, HEAD_DIM)
+    heads_split = qkv.reshape(3, rows_here, seq_len, heads, HEAD_DIM)
+    lse_rows = lse[:, :2].reshape(rows_here, heads, seq_len)
 
     def masked_scores(query_rows, key_rows, row_segments):
         scores = dot_f32("qhd,khd->hqk", query_rows, key_rows) * score_scale
         same_doc = row_segments[:, None] == row_segments[None, :]
         return jnp.where(same_doc[None], scores, NEG_FILL)
 
-    def row_forward(packed):
-        query_rows, key_rows, value_rows, row_segments = packed
-        scores = masked_scores(query_rows, key_rows, row_segments)
-        row_max = jnp.max(scores, axis=-1, keepdims=True)
-        row_exp = jnp.exp(scores - row_max)
-        row_total = jnp.sum(row_exp, axis=-1, keepdims=True)
-        row_probs = (row_exp / row_total).astype(BF16)
-        mixed = dot_f32("hqk,khd->qhd", row_probs, value_rows)
-        row_lse = (row_max + jnp.log(row_total))[..., 0]
-        return (mixed.astype(BF16).reshape(seq_len, D), row_lse)
-
-    context_rows, lse_rows = lax.map(
-        row_forward, (heads_split[0], heads_split[1], heads_split[2], segments)
-    )
-    context = context_rows.reshape(tokens_here, D)
-    attended = dot_f32("tn,dn->td", context, out_w)
-    hidden_one, norm_one_back = jax.vjp(
-        layer_norm, tokens.astype(F32) + attended, norm_full[0], norm_full[1]
-    )
-    hidden_low = hidden_one.astype(BF16)
-    pre_act = jnp.dot(hidden_low, up_w, preferred_element_type=F32)
-    act_full, gelu_back = jax.vjp(exact_gelu, pre_act)
-    act_low = act_full.astype(BF16)
-    ffn_out = dot_f32("tf,df->td", act_low, down_w)
-    result, norm_two_back = jax.vjp(layer_norm, hidden_one + ffn_out, norm_full[2], norm_full[3])
-    layer_out = result.astype(BF16)
-    d_resid_two, d_gain_two, d_shift_two = norm_two_back(cotangent.astype(F32))
-    d_ffn = d_resid_two.astype(BF16)
+    d_gain_two, d_shift_two = d_norm_two[0], d_norm_two[1]
     down_grad = dot_f32("td,tf->df", d_ffn, act_low).astype(BF16)
     d_act = jnp.dot(d_ffn, down_w, preferred_element_type=F32)
-    d_pre = gelu_back(d_act)[0].astype(BF16)
+    d_pre = (d_act * slope.astype(F32)).astype(BF16)
     up_grad = dot_f32("tc,tf->cf", hidden_low, d_pre).astype(BF16)
     d_hidden = d_resid_two + dot_f32("tf,cf->tc", d_pre, up_w)
-    d_resid_one, d_gain_one, d_shift_one = norm_one_back(d_hidden)
+    unit, unit_scale = normed(resid_one)
+    d_gain_one, d_shift_one = jnp.sum(d_hidden * unit, axis=0), jnp.sum(d_hidden, axis=0)
+    d_resid_one = norm_backward(d_hidden * norm_full[0], unit, unit_scale)
     d_attn = d_resid_one.astype(BF16)
     output_grad = dot_f32("td,tn->dn", d_attn, context).astype(BF16)
     d_context = jnp.dot(d_attn, out_w, preferred_element_type=F32).astype(BF16)

time: 756 us -> 663 us (0.88)
  matrix products: 293 us -> 153 us
  Pallas kernels: 339 us -> 376 us
  local copies, waits for them, and re-layouts: 45.5 us -> 71.9 us
  other arithmetic: 68.8 us -> 49.4 us
    dot_general x23 -> x16, matrix products: 217 us -> 133 us  [dot_f32(): return jnp.einsum(spec, a, b, preferred_element_type=F32)]
    dot_general x1 -> x0, matrix products: 49 us -> none  [local_rows(): pre_act = jnp.dot(hidden_low, up_w, preferred_element_type=F32)]
    pallas_call x1, Pallas kernels: 157 us -> 194 us  [run_forward(): pl.pallas_call(functools.partial(forward_kernel, nz), out_shape=[jax.Shap...]
    reduce_sum x7 -> x2, other arithmetic: 28.3 us -> 5.18 us  [the longest x1 2.74 us: normed(): jnp.mean(center * center, axis=-1, keepdims=True) + EPS_NORM]
    while x11 -> x15, local copies, waits for them, and re-layouts: 5.4 us -> 20.2 us  [the longest x3 16.7 us: local_rows(): lax.map(row_backward, (heads_split[0], heads_split[1], heads_split[2], se...]
where the time goes in v2:
time: 663 us; the launch traced here: 653 us
  Pallas kernels  376 us (57%)
  matrix products  153 us (23%)
  local copies, waits for them, and re-layouts  71.9 us (11%)
  other arithmetic  49.4 us (7%)
    pallas_call x1, Pallas kernels, run_forward(): pl.pallas_call(functools.partial(forward_kernel, nz), out_shape=[jax.Shap...  194 us
    pallas_call x1, Pallas kernels, scatter_grads(): pl.pallas_call(functools.partial(scatter_kernel, nz), out_shape=shapes +...  183 us
    dot_general x16, matrix products, dot_f32(): return jnp.einsum(spec, a, b, preferred_element_type=F32)  133 us
    convert_element_type x2, other arithmetic, row_backward(): d_scores = (row_probs * (d_probs - row_inner)).astype(BF16)  23.4 us
    while x3, local copies, waits for them, and re-layouts, local_rows(): lax.map(row_backward, (heads_split[0], heads_split[1], heads_split[2], se...  16.7 us
    dot_general x1, matrix products, local_rows(): d_act = jnp.dot(d_ffn, down_w, preferred_element_type=F32)  16.2 us

profile of v2, /device:TPU:0, one launch (start us, length us, event | category | flops | bytes accessed | tf_op | source)
XLA Modules:
  0.0 652.9 jit_solution(10545639696267315276)
XLA Ops:
  2.9 1.6 convert_element_type.70.out
  4.4 1.7 convert_element_type.69.proj
  6.1 1.8 convert_element_type.71.up
  7.9 1.8 convert_element_type.72.down
  9.7 1.0 broadcast_in_dim.45.seg_col
  10.7 193.7 %forward.1 = (bf16[3,4,2,2,64,1024]{5,4,3,2,1,0:T(8,128)(2,1)}, bf16[4,2,2,64,1024]{4,3,2,1,0:T(8,128)(2,1)}, bf16[4,2,2,64,4096]{4,3,2,1,0:T(8,128)(2,1)}, bf16...) custom-call(bf16[2048,1024]{1,0:T(8,128)(2,1)} %tokens.1, ...), custom_call_target="tpu_custom_call" | custom-call | tf_op jit(solution)/shard_map/forward/pallas_call | solution.py:881
  205.1 2.4 reduce_sum.63
  207.6 2.7 multiply_reduce_fusion.3
  210.4 1.4 slice.28
  211.7 1.0 slice.26
  213.4 5.6 fusion.38
  218.9 6.3 reshape.172
  225.3 5.7 copy.60
  231.0 6.3 reshape.171
  237.3 5.5 copy.58
  242.8 3.9 reshape.170
  246.7 5.5 copy.57
  252.2 16.2 %multiply_convert_fusion.3 = bf16[1024,4096]{1,0:T(8,128)(2,1)} fusion(bf16[1024,4096]{1,0:T(8,128)(2,1)} %get-tuple-element.102, bf16[1024,1024]{1,0:T(8,128)(2,1)} %get-tuple-element.100, bf16[1024,4096]{1,0:T(8,128)(2,1)} %bitcast.121), kind=kOutput, calls=%fused_computation.30 | convolution fusion | flops 8602517504 | bytes 27262976 | tf_op jit(solution)/shard_map/dot_general | solution.py:994
  268.4 15.8 %multiply_reduce_fusion.1 = (f32[1024]{0:T(1024)}, f32[1024]{0:T(1024)S(1)}, f32[1024]{0:T(1024)S(1)}, f32[1024]{0:T(1024)}, f32[1024,1024]{1,0:T(8,128)S(1)}) fusion(f32[1024,1024]{1,0:T(8,128)S(1)} %copy-done.3, f32[1024]{0:T(1024)S(1)} %add_rsqrt_fusion, f32[1024]{0:T(1024)S(1)} %broadcast_multiply_fusion.2, f32[1024]{0:T(1024)S(1)} %bitcast.115, ...), kind=kOutput, calls=%fused_computation.35 | convolution fusion | flops 8600416256 | bytes 29388800 | tf_op jit(solution)/shard_map/tf,cf->tc/dot_general | solution.py:933
  284.2 24.1 %convolution_convert_fusion = bf16[1024,4096]{1,0:T(8,128)(2,1)} fusion(bf16[1024,1024]{1,0:T(8,128)(2,1)} %get-tuple-element.113, bf16[1024,4096]{1,0:T(8,128)(2,1)} %multiply_convert_fusion.3), kind=kOutput, calls=%fused_computation.31 | convolution fusion | flops 8594128896 | bytes 18874368 | tf_op jit(solution)/shard_map/tc,tf->cf/dot_general | solution.py:933
  308.3 14.6 %convolution_convert_fusion.1 = bf16[1024,4096]{1,0:T(8,128)(2,1)} fusion(bf16[1024,1024]{1,0:T(8,128)(2,1)S(1)} %copy-done.39, bf16[1024,4096]{1,0:T(8,128)(2,1)} %get-tuple-element.112), kind=kOutput, calls=%fused_computation.32 | convolution fusion | flops 8594128896 | bytes 18874368 | tf_op jit(solution)/shard_map/td,tf->df/dot_general | solution.py:933
  322.9 1.3 subtract_multiply_fusion
  324.5 3.8 convolution_convert_fusion.3
  328.3 3.6 convolution_convert_fusion.4
  331.9 100.5 %while.14 = (s32[]{:T(128)}, bf16[2,512,1024]{2,1,0:T(8,128)(2,1)}, bf16[2,512,1024]{2,1,0:T(8,128)(2,1)}, bf16[2,512,1024]{2,1,0:T(8,128)(2,1)}, bf16[2,512,16,...) while((s32[]{:T(128)}, bf16[2,512,1024]{2,1,0:T(8,128)(2,1)}, ...), condition=%wide.region_6.7_spmd, body=%wide.region_4.6_spmd.sunk | while | flops 2724978688 | bytes 237673712 | solution.py:1018
  332.2 1.4 dynamic-slice_bitcast_fusion.2
  333.5 0.9 broadcast_compare_fusion.2
  334.5 1.3 constant_dynamic-slice_fusion.8
  336.3 5.9 subtract_exponential_fusion.2
  342.2 4.3 fusion.74
  346.5 1.7 copy-done.2
  348.3 1.5 copy.89
  349.8 11.1 %multiply_reduce_fusion.6 = (f32[16,512]{1,0:T(8,128)S(1)}, f32[16,512,512]{1,2,0:T(8,128)}) fusion(f32[16,512,512]{1,2,0:T(8,128)} %copy-done.2, bf16[512,16,64]{0,2,1:T(8,128)(2,1)S(1)} %bitcast.100, bf16[2,512,16,64]{1,3,2,0:T(8,128)(2,1)} %get-tuple-element.291, s32[]{:T(128)S(6)} %copy.99), kind=kOutput, calls=%fused_computation.1.clone.1 | convolution fusion | flops 545251328 | bytes 35684356 | tf_op jit(solution)/shard_map/while/body/eval_jaxpr/qhd,khd->hqk/dot_general | solution.py:933
  360.9 11.7 %multiply_convert_fusion.7 = bf16[16,512,512]{1,2,0:T(8,128)(2,1)S(1)} fusion(f32[16,512,512]{1,2,0:T(8,128)} %copy-done.2, f32[16,512,512]{1,2,0:T(8,128)} %get-tuple-element.256, f32[16,512]{1,0:T(8,128)S(1)} %get-tuple-element.257), kind=kLoop, calls=%fused_computation.clone.1 | loop fusion | flops 12582912 | bytes 41975808 | tf_op jit(solution)/shard_map/while/body/eval_jaxpr/convert_element_type | solution.py:1012
  372.6 3.6 multiply_convert_fusion.9
  376.2 1.5 multiply_convert_fusion.8
  378.2 1.5 copy.90
  379.7 1.0 constant_dynamic-update-slice_fusion.5
  380.8 1.5 constant_dynamic-update-slice_fusion.6
  382.3 1.4 dynamic-slice_bitcast_fusion.2
  383.6 0.9 broadcast_compare_fusion.2
  384.6 1.3 constant_dynamic-slice_fusion.8
  386.4 5.9 subtract_exponential_fusion.2
  392.3 4.3 fusion.74
  396.6 1.7 copy-done.2
  398.4 1.5 copy.89
  399.9 11.1 %multiply_reduce_fusion.6 = (f32[16,512]{1,0:T(8,128)S(1)}, f32[16,512,512]{1,2,0:T(8,128)}) fusion(f32[16,512,512]{1,2,0:T(8,128)} %copy-done.2, bf16[512,16,64]{0,2,1:T(8,128)(2,1)S(1)} %bitcast.100, bf16[2,512,16,64]{1,3,2,0:T(8,128)(2,1)} %get-tuple-element.291, s32[]{:T(128)S(6)} %copy.99), kind=kOutput, calls=%fused_computation.1.clone.1 | convolution fusion | flops 545251328 | bytes 35684356 | tf_op jit(solution)/shard_map/while/body/eval_jaxpr/qhd,khd->hqk/dot_general | solution.py:933
  411.0 11.7 %multiply_convert_fusion.7 = bf16[16,512,512]{1,2,0:T(8,128)(2,1)S(1)} fusion(f32[16,512,512]{1,2,0:T(8,128)} %copy-done.2, f32[16,512,512]{1,2,0:T(8,128)} %get-tuple-element.256, f32[16,512]{1,0:T(8,128)S(1)} %get-tuple-element.257), kind=kLoop, calls=%fused_computation.clone.1 | loop fusion | flops 12582912 | bytes 41975808 | tf_op jit(solution)/shard_map/while/body/eval_jaxpr/convert_element_type | solution.py:1012
  422.7 3.6 multiply_convert_fusion.9
  426.3 1.5 multiply_convert_fusion.8
  428.3 1.5 copy.90
  429.8 1.0 constant_dynamic-update-slice_fusion.5
  430.9 1.5 constant_dynamic-update-slice_fusion.6
  432.4 13.6 %bitcast_add_fusion = f32[1024,1024]{1,0:T(8,128)} fusion(f32[1024,1024]{1,0:T(8,128)} %copy-done.7, bf16[3,1024,1024]{2,1,0:T(8,128)(2,1)} %bitcast.122, bf16[1,1024,1024]{2,1,0:T(8,128)(2,1)} %bitcast.108, bf16[1,1024,1024]{2,1,0:T(8,128)(2,1)} %bitcast.110, bf16[1,1024,1024]{2,1,0:T(8,128)(2,1)} %bitcast.112), kind=kOutput, calls=%fused_computation.34 | convolution fusion | flops 6449790976 | bytes 20971520 | tf_op jit(solution)/shard_map/stn,scn->tc/dot_general | solution.py:933
  446.1 8.8 %convolution_convert_fusion.2 = bf16[3,1024,1024]{1,2,0:T(8,128)(2,1)} fusion(bf16[1,1024,1024]{2,1,0:T(8,128)(2,1)S(1)} %bitcast.109, bf16[1,1024,1024]{2,1,0:T(8,128)(2,1)S(1)} %bitcast.111, bf16[1,1024,1024]{2,1,0:T(8,128)(2,1)S(1)} %bitcast.113, bf16[2048,1024]{1,0:T(8,128)(2,1)S(1)} %copy-done.6, s32[]{:T(128)S(6)} %select_n.16), kind=kOutput, calls=%fused_computation.41 | convolution fusion | flops 6464471040 | bytes 14680068 | tf_op jit(solution)/shard_map/tc,stn->scn/dot_general | solution.py:933
  455.7 182.8 %scatter_grads.1 = (f32[64,2048]{1,0:T(8,128)}, f32[64,2048]{1,0:T(8,128)}, f32[64,512]{1,0:T(8,128)}, f32[3,64,512]{2,1,0:T(8,128)}, f32[8,1024]{1,0:T(8,128)}) custom-call(bf16[4,2,2,64,4096]{4,3,2,1,0:T(8,128)(2,1)} %bitcast.106, bf16[4,2,2,64,4096]{4,3,2,1,0:T(8,128)(2,1)} %bitcast.105, bf16[4,2,2,64,1024]{4,3,2,1,0:T(8,128)(2,1)} %bitcast.107, ...), custom_call_target="tpu_custom_call" | custom-call | tf_op jit(solution)/shard_map/scatter_grads/pallas_call | solution.py:560
  638.5 1.5 multiply_subtract_fusion.4
  640.0 1.7 multiply_subtract_fusion.3
  641.7 2.2 multiply_subtract_fusion.2
  644.0 2.6 multiply_subtract_fusion
  646.7 1.4 multiply_subtract_fusion.1
  648.1 1.3 copy.113
  650.8 0.8 copy.116
  651.6 0.8 copy.117
  (110 shorter events, 8.4 us)
Async XLA Ops:
  0.7 1.3 copy-start
  2.9 7.8 %copy-start.26 = (f32[8,1024]{1,0:T(8,128)}, f32[8,1024]{1,0:T(8,128)S(1)}, u32[]{:S(2)}) copy-start(f32[8,1024]{1,0:T(8,128)S(1)} %dynamic_update_slice.13.norm) | copy-start | bytes 98308
  252.2 16.2 %copy-start.3 = (f32[1024,1024]{1,0:T(8,128)S(1)}, f32[1024,1024]{1,0:T(8,128)}, u32[]{:S(2)}) copy-start(f32[1024,1024]{1,0:T(8,128)} %get-tuple-element.98) | copy-start | bytes 12582916
  252.2 16.2 %copy-start.36 = (f32[1024,1024]{1,0:T(8,128)S(1)}, f32[1024,1024]{1,0:T(8,128)}, u32[]{:S(2)}) copy-start(f32[1024,1024]{1,0:T(8,128)} %get-tuple-element.99) | copy-start | bytes 12582916
  284.2 24.1 %copy-start.39 = (bf16[1024,1024]{1,0:T(8,128)(2,1)S(1)}, bf16[1024,1024]{1,0:T(8,128)(2,1)}, u32[]{:S(2)}) copy-start(bf16[1024,1024]{1,0:T(8,128)(2,1)} %get-tuple-element.100) | copy-start | bytes 6291460
  322.9 1.6 copy-start.38
  324.5 3.8 copy-start.7
  324.5 3.8 copy-start.37
  342.2 6.0 copy-start.2
  360.9 11.7 %copy-start.5 = (bf16[2,512,16,64]{1,3,2,0:T(8,128)(2,1)S(1)}, bf16[2,512,16,64]{1,3,2,0:T(8,128)(2,1)}, u32[]{:S(2)}) copy-start(bf16[2,512,16,64]{1,3,2,0:T(8,128)(2,1)} %get-tuple-element.288) | copy-start | bytes 6291460 | tf_op jit(solution)/shard_map/while
  372.6 3.6 copy-start.4
  392.3 6.0 copy-start.2
  411.0 11.7 %copy-start.5 = (bf16[2,512,16,64]{1,3,2,0:T(8,128)(2,1)S(1)}, bf16[2,512,16,64]{1,3,2,0:T(8,128)(2,1)}, u32[]{:S(2)}) copy-start(bf16[2,512,16,64]{1,3,2,0:T(8,128)(2,1)} %get-tuple-element.288) | copy-start | bytes 6291460 | tf_op jit(solution)/shard_map/while
  422.7 3.6 copy-start.4
  432.4 13.6 %copy-start.6 = (bf16[2048,1024]{1,0:T(8,128)(2,1)S(1)}, bf16[2048,1024]{1,0:T(8,128)(2,1)}, u32[]{:S(2)}) copy-start(bf16[2048,1024]{1,0:T(8,128)(2,1)} %tokens.1) | copy-start | bytes 12582916
  432.4 13.6 %copy-start.8 = (bf16[2,512,1024]{2,1,0:T(8,128)(2,1)S(1)}, bf16[2,512,1024]{2,1,0:T(8,128)(2,1)}, u32[]{:S(2)}) copy-start(bf16[2,512,1024]{2,1,0:T(8,128)(2,1)} %get-tuple-element.110) | copy-start | bytes 6291460
  432.4 13.6 %copy-start.9 = (bf16[2,512,1024]{2,1,0:T(8,128)(2,1)S(1)}, bf16[2,512,1024]{2,1,0:T(8,128)(2,1)}, u32[]{:S(2)}) copy-start(bf16[2,512,1024]{2,1,0:T(8,128)(2,1)} %get-tuple-element.109) | copy-start | bytes 6291460
  432.4 13.6 %copy-start.10 = (bf16[2,512,1024]{2,1,0:T(8,128)(2,1)S(1)}, bf16[2,512,1024]{2,1,0:T(8,128)(2,1)}, u32[]{:S(2)}) copy-start(bf16[2,512,1024]{2,1,0:T(8,128)(2,1)} %get-tuple-element.108) | copy-start | bytes 6291460
  446.0 8.8 %copy-start.29 = (f32[2,1024]{1,0:T(2,128)S(1)}, f32[2,1024]{1,0:T(2,128)}, u32[]{:S(2)}) copy-start(f32[2,1024]{1,0:T(2,128)} %slice.28) | copy-start | bytes 24580
  446.1 8.8 %copy-start.31 = (f32[1024]{0:T(1024)S(1)}, f32[1024]{0:T(1024)}, u32[]{:S(2)}) copy-start(f32[1024]{0:T(1024)} %get-tuple-element.141) | copy-start | bytes 12292
  446.1 8.8 %copy-start.32 = (f32[1024]{0:T(1024)S(1)}, f32[1024]{0:T(1024)}, u32[]{:S(2)}) copy-start(f32[1024]{0:T(1024)} %get-tuple-element.144) | copy-start | bytes 12292
  446.1 8.8 %copy-start.35 = (f32[8]{0:T(128)S(1)}, f32[8]{0:T(128)}, u32[]{:S(2)}) copy-start(f32[8]{0:T(128)} %pad.3.clone) | copy-start | bytes 100
  455.5 182.9 %copy-start.30 = (f32[4,32]{1,0:T(4,128)S(1)}, f32[4,32]{1,0:T(4,128)}, u32[]{:S(2)}) copy-start(f32[4,32]{1,0:T(4,128)} %param.35) | copy-start | bytes 1540
  455.6 182.9 %copy-start.33 = (f32[4,32]{1,0:T(4,128)S(1)}, f32[4,32]{1,0:T(4,128)}, u32[]{:S(2)}) copy-start(f32[4,32]{1,0:T(4,128)} %param.37) | copy-start | bytes 1540
  455.6 183.0 %copy-start.34 = (f32[4,32]{1,0:T(4,128)S(1)}, f32[4,32]{1,0:T(4,128)}, u32[]{:S(2)}) copy-start(f32[4,32]{1,0:T(4,128)} %param.36) | copy-start | bytes 1540
  455.6 184.5 %copy-start.22 = (f32[64,512]{1,0:T(8,128)S(1)}, f32[64,512]{1,0:T(8,128)}, u32[]{:S(2)}) copy-start(f32[64,512]{1,0:T(8,128)} %param.26) | copy-start | bytes 393220
  455.6 184.5 %copy-start.27 = (f32[64,512]{1,0:T(8,128)S(1)}, f32[64,512]{1,0:T(8,128)}, u32[]{:S(2)}) copy-start(f32[64,512]{1,0:T(8,128)} %param.28) | copy-start | bytes 393220
  455.6 184.4 %copy-start.28 = (f32[64,512]{1,0:T(8,128)S(1)}, f32[64,512]{1,0:T(8,128)}, u32[]{:S(2)}) copy-start(f32[64,512]{1,0:T(8,128)} %param.27) | copy-start | bytes 393220
  455.6 186.1 %copy-start.16 = (f32[3,64,512]{2,1,0:T(8,128)S(1)}, f32[3,64,512]{2,1,0:T(8,128)}, u32[]{:S(2)}) copy-start(f32[3,64,512]{2,1,0:T(8,128)} %param.23) | copy-start | bytes 1179652
  455.6 186.1 %copy-start.24 = (f32[3,64,512]{2,1,0:T(8,128)S(1)}, f32[3,64,512]{2,1,0:T(8,128)}, u32[]{:S(2)}) copy-start(f32[3,64,512]{2,1,0:T(8,128)} %param.25) | copy-start | bytes 1179652
  455.6 186.1 %copy-start.25 = (f32[3,64,512]{2,1,0:T(8,128)S(1)}, f32[3,64,512]{2,1,0:T(8,128)}, u32[]{:S(2)}) copy-start(f32[3,64,512]{2,1,0:T(8,128)} %param.24) | copy-start | bytes 1179652
  455.6 188.4 %copy-start.11 = (f32[64,2048]{1,0:T(8,128)S(1)}, f32[64,2048]{1,0:T(8,128)}, u32[]{:S(2)}) copy-start(f32[64,2048]{1,0:T(8,128)} %param.32) | copy-start | bytes 1572868
  455.6 188.4 %copy-start.18 = (f32[64,2048]{1,0:T(8,128)S(1)}, f32[64,2048]{1,0:T(8,128)}, u32[]{:S(2)}) copy-start(f32[64,2048]{1,0:T(8,128)} %param.34) | copy-start | bytes 1572868
  455.6 188.3 %copy-start.19 = (f32[64,2048]{1,0:T(8,128)S(1)}, f32[64,2048]{1,0:T(8,128)}, u32[]{:S(2)}) copy-start(f32[64,2048]{1,0:T(8,128)} %param.33) | copy-start | bytes 1572868
  638.4 8.2 %copy-start.12 = (f32[64,2048]{1,0:T(8,128)S(1)}, f32[64,2048]{1,0:T(8,128)}, u32[]{:S(2)}) copy-start(f32[64,2048]{1,0:T(8,128)} %param.29) | copy-start | bytes 1572868
  638.5 8.2 %copy-start.14 = (f32[64,2048]{1,0:T(8,128)S(1)}, f32[64,2048]{1,0:T(8,128)}, u32[]{:S(2)}) copy-start(f32[64,2048]{1,0:T(8,128)} %get-tuple-element.325) | copy-start | bytes 1572868
  638.5 8.2 %copy-start.20 = (f32[64,2048]{1,0:T(8,128)S(1)}, f32[64,2048]{1,0:T(8,128)}, u32[]{:S(2)}) copy-start(f32[64,2048]{1,0:T(8,128)} %param.31) | copy-start | bytes 1572868
  638.5 8.2 %copy-start.21 = (f32[64,2048]{1,0:T(8,128)S(1)}, f32[64,2048]{1,0:T(8,128)}, u32[]{:S(2)}) copy-start(f32[64,2048]{1,0:T(8,128)} %param.30) | copy-start | bytes 1572868
  644.0 4.1 copy-start.15
  646.6 2.8 copy-start.17
  646.7 3.5 copy-start.23
  646.7 5.0 copy-start.13
  646.7 5.8 copy-start.1

commit v3 on v2

--- a/solution.py
+++ b/solution.py
@@ -399,186 +399,6 @@
         self.parts[i + 1] = self.parts[i] + self.came[i]
 
 
-def add_blocks(dst, terms, rows=16):
-    lead = range(dst.shape[0]) if len(dst.shape) == 3 else (None,)
-
-    def body(i, carry):
-        start = pl.multiple_of(i * rows, rows)
-        for s in lead:
-            idx = (pl.ds(start, rows), slice(None)) if s is None else (s, pl.ds(start, rows), slice(None))
-            total = terms[0][idx].astype(F32)
-            for term in terms[1:]:
-                total = total + term[idx].astype(F32)
-            dst[idx] = total.astype(dst.dtype)
-        return carry
-
-    lax.fori_loop(0, dst.shape[-2] // rows, body, 0)
-
-
-class Scatter:
-    def __init__(self, me, nz, grad, result, view, held, from_c, from_d, from_x, from_y, from_z,
-                 load_sem, send_sem, recv_sem, base):
-        self.me, self.nz, self.grad, self.result, self.view = me, nz, grad, result, view
-        self.held, self.from_c, self.from_d = held, from_c, from_d
-        self.from_x, self.from_y, self.from_z = from_x, from_y, from_z
-        self.load_sem, self.send_sem, self.recv_sem, self.base = load_sem, send_sem, recv_sem, base
-        self.sent = []
-
-    def index(self, a, b, e):
-        return (a * 2 + b) * 2 + e
-
-    def remote(self, src, dst, slot, hop):
-        sem = self.base * 8 * self.nz + slot
-        return pltpu.make_async_remote_copy(
-            src_ref=src, dst_ref=dst, send_sem=self.send_sem.at[sem], recv_sem=self.recv_sem.at[sem],
-            device_id=device_at(self.me, hop), device_id_type=MESH,
-        )
-
-    def send(self, src, dst, slot, hop):
-        copy = self.remote(src, dst, slot, hop)
-        copy.start()
-        self.sent.append(copy)
-
-    def wait(self, dst, slot):
-        self.remote(dst, dst, slot, HOP_C).wait_recv()
-
-    def load(self, a, b, e):
-        i = self.index(a, b, e)
-        return pltpu.make_async_copy(
-            self.view(self.grad, moved(self.me, (a, b, 0, e))), self.held.at[i],
-            self.load_sem.at[self.base * 4 * self.nz + i],
-        )
-
-    def stage_core(self, a):
-        for b, e in ((1, 1), (1, 0), (0, 1), (0, 0)):
-            i = self.index(a, b, e)
-            self.send(self.view(self.grad, moved(self.me, (a, b, 1, e))), self.from_c.at[i], i, HOP_C)
-            self.load(a, b, e).start()
-
-    def slot_of(self, kind, a):
-        return 4 * self.nz + self.nz * "dxyz".index(kind) + a
-
-    def stage_diagonal(self, a):
-        for b, e in ((1, 1), (1, 0), (0, 1), (0, 0)):
-            i = self.index(a, b, e)
-            self.load(a, b, e).wait()
-            self.wait(self.from_c.at[i], i)
-            add_blocks(self.held.at[i], [self.held.at[i], self.from_c.at[i]])
-            if (b, e) == (1, 1):
-                hop = HOP_Y if a < self.nz // 2 else HOP_X
-                self.send(self.held.at[i], self.from_d.at[a], self.slot_of("d", a), hop)
-            elif (b, e) == (1, 0) and a >= self.nz // 2:
-                self.send(self.held.at[i], self.from_x.at[a], self.slot_of("x", a), HOP_X)
-            elif (b, e) == (0, 1) and a < self.nz // 2:
-                self.send(self.held.at[i], self.from_y.at[a], self.slot_of("y", a), HOP_Y)
-
-    def stage_square(self, a):
-        self.wait(self.from_d.at[a], self.slot_of("d", a))
-        if a < self.nz // 2:
-            i = self.index(a, 1, 0)
-            add_blocks(self.held.at[i], [self.held.at[i], self.from_d.at[a]])
-            self.send(self.held.at[i], self.from_x.at[a], self.slot_of("x", a), HOP_X)
-        else:
-            i = self.index(a, 0, 1)
-            add_blocks(self.held.at[i], [self.held.at[i], self.from_d.at[a]])
-            self.send(self.held.at[i], self.from_y.at[a], self.slot_of("y", a), HOP_Y)
-
-    def stage_column(self, a):
-        self.wait(self.from_x.at[a], self.slot_of("x", a))
-        self.wait(self.from_y.at[a], self.slot_of("y", a))
-        i = self.index(a, 0, 0)
-        terms = [self.held.at[i], self.from_x.at[a], self.from_y.at[a]]
-        if a:
-            add_blocks(self.held.at[i], terms)
-            self.send(self.held.at[i], self.from_z.at[a], self.slot_of("z", a), hop_z(a))
-        else:
-            for other in range(1, self.nz):
-                self.wait(self.from_z.at[other], self.slot_of("z", other))
-                terms.append(self.from_z.at[other])
-            add_blocks(self.result, terms)
-
-    def order(self):
-        half = self.nz // 2
-        out = []
-        for k in range(half):
-            out += [self.nz - 1 - k, half - 1 - k]
-        return out
-
-    def stages(self):
-        order = self.order()
-        calls = [(self.stage_core, a) for a in order]
-        kinds = (self.stage_diagonal, self.stage_square, self.stage_column)
-        for t in range(len(order) + 2):
-            for lag, kind in enumerate(kinds):
-                if 0 <= t - lag < len(order):
-                    calls.append((kind, order[t - lag]))
-        return calls
-
-    def drain(self):
-        for copy in self.sent:
-            copy.wait_send()
-
-
-def scatter_kernel(nz, *refs):
-    grads, norm = refs[:4], refs[4]
-    results, norm_all = refs[5:9], refs[9]
-    buffers, rest = refs[10:34], refs[34:]
-    load_sem, send_sem, recv_sem, parts, came, sum_send, sum_recv = rest
-    me = position()
-    entry_barrier(me, nz)
-    views = (view_rows, view_rows, view_rows, view_stack)
-    scatters = [
-        Scatter(me, nz, grads[i], results[i], views[i], *buffers[6 * i : 6 * i + 6],
-                load_sem, send_sem, recv_sem, i)
-        for i in range(4)
-    ]
-    small = SmallSum(me, nz, parts, came, sum_send, sum_recv)
-    parts[0] = norm[...]
-    for i in range(len(small.hops)):
-        small.start(i)
-        small.finish(i)
-    norm_all[...] = parts[len(small.hops)]
-    for s in scatters:
-        for call, a in s.stages():
-            call(a)
-    for s in scatters:
-        s.drain()
-
-
-def scatter_grads(nz, down, up, out, proj, norm):
-    grads = [g.reshape(nz, 2, 2, D // (4 * nz), g.shape[1]) for g in (down, up, out)]
-    grads.append(proj.reshape(3, nz, 2, 2, D // (4 * nz), proj.shape[2]))
-    shapes, buffers = [], []
-    for g in grads:
-        piece = (g.shape[-2], g.shape[-1] // 2)
-        if g.ndim == 6:
-            piece = (3,) + piece
-        shapes.append(jax.ShapeDtypeStruct(piece, F32))
-        for count in (4 * nz, 4 * nz, nz, nz, nz, nz):
-            buffers.append(pltpu.VMEM((count,) + piece, BF16))
-    n_sum = len(sum_hops(nz))
-    return pl.pallas_call(
-        functools.partial(scatter_kernel, nz),
-        out_shape=shapes + [jax.ShapeDtypeStruct(norm.shape, F32)],
-        in_specs=[ANY] * 4 + [VMEM],
-        out_specs=[VMEM] * 5,
-        scratch_shapes=buffers
-        + [
-            DMA((16 * nz,)),
-            DMA((32 * nz,)),
-            DMA((32 * nz,)),
-            pltpu.VMEM((n_sum + 1,) + norm.shape, F32),
-            pltpu.VMEM((n_sum,) + norm.shape, F32),
-            DMA((n_sum,)),
-            DMA((n_sum,)),
-        ],
-        compiler_params=pltpu.CompilerParams(
-            collective_id=1, has_side_effects=True, vmem_limit_bytes=56 << 20
-        ),
-        name="scatter_grads",
-    )(*grads, norm)
-
-
 ERFC_SLOPE = 0.33 * 0.5**0.5
 ERFC_POLY = (
     0.1863683316091749,
@@ -632,10 +452,11 @@
                 call()
 
 
-def phase(count, body, plan):
+def phase(count, parts, plan):
     def step(i, carry):
-        at_slots(i, plan)
-        body(i)
+        for k, part in enumerate(parts):
+            at_slots(i, {slot // len(parts): plan[slot] for slot in plan if slot % len(parts) == k})
+            part(i)
         return carry
 
     lax.fori_loop(0, count, step, 0)
@@ -647,7 +468,7 @@
         for i in range(count):
             while calls and calls[0][0] <= start + i * each:
                 plan.setdefault(i, []).append(calls.pop(0)[1])
-    return plans, [call for _, call in calls]
+    return plans, calls
 
 
 def gather_calls(gathers, costs, start):
@@ -727,7 +548,7 @@
         same = seg_col[rows, 0:1] == seg_row[r]
         bias[r] = jnp.where(same, 0.0, NEG_FILL)
 
-    phase(rows_here, bias_step, {})
+    phase(rows_here, [bias_step], {})
     for _, call in calls[1 : marks[0]]:
         call()
     for copy in keep:
@@ -752,7 +573,7 @@
         weight = w_small[s, :, :, :, :, col].reshape(D, 256)
         qkv[s, :, col] = dot_nn(tok[...], weight).astype(BF16)
 
-    phase(n_q, qkv_step, plans[0])
+    phase(n_q, [qkv_step], plans[0])
     begin("qkv", qkv, qkv_out, 3)
     head_of = lax.broadcasted_iota(jnp.int32, (128, 128), 1) // HEAD_DIM
 
@@ -778,7 +599,7 @@
                 wide = jnp.broadcast_to(level[h * 128 : h * 128 + 128], (128, 128))
                 lse[u, h : h + 1, qb * 128 : qb * 128 + 128] = wide.T[0:1]
 
-    phase(n_a, attend_step, plans[1])
+    phase(n_a, [attend_step], plans[1])
     for _, call in rest_out:
         call()
     begin("out", out_all, w_small.at[3], 4)
@@ -795,10 +616,10 @@
         unit, _ = normed(total)
         hidden[rows, :] = (unit * norm_all[0:1, :] + norm_all[1:2, :]).astype(BF16)
 
-    phase(n_o, out_step, plans[0])
+    phase(n_o, [out_step], plans[0])
     begin("res", res, resid_out, 6)
     begin("hidden", hidden, hidden_out, 7)
-    for call in rest_up:
+    for _, call in rest_up:
         call()
     begin("up", up_all, w_up, 8)
     start_u = costs[0] + costs[1] + costs[2] + 2.0
@@ -828,9 +649,9 @@
         col = pl.ds(pl.multiple_of(j * 256, 256), 256)
         return pltpu.make_async_copy(slope.at[slot], slope_out.at[:, col], io_sem.at[9 + slot])
 
-    phase(n_u, up_step, plans[0])
+    phase(n_u, [up_step], plans[0])
     begin("act", act, act_out, 11)
-    for call in rest_down:
+    for _, call in rest_down:
         call()
     for k in range(4):
         begin(("down", k), down_all.at[:, :, :, :, pl.ds(k * D, D)], w_small.at[k], 12 + k)
@@ -855,7 +676,7 @@
         res[rows, :] = dres
         hidden[rows, :] = dres.astype(BF16)
 
-    phase(t_here // 256, down_step, {})
+    phase(t_here // 256, [down_step], {})
     begin("layer", tok, layer_out, 16)
     begin("dres", res, dres_out, 17)
     begin("dffn", hidden, dffn_out, 18)
@@ -929,8 +750,454 @@
     )(tokens_in, cotangent, seg_col, seg_row, proj, out, up, down, norm)
 
 
-def dot_f32(spec, a, b):
-    return jnp.einsum(spec, a, b, preferred_element_type=F32)
+def view_flat(ref, pos):
+    z, x, c, y = pos
+    rows, half = 64, ref.shape[1] // 2
+    row = (z * 4 + x * 2 + c) * rows
+    return ref.at[pl.ds(pl.multiple_of(row, rows), rows), pl.ds(pl.multiple_of(y * half, half), half)]
+
+
+def add_rows(dst, terms, rows=16):
+    def body(i, carry):
+        block = pl.ds(pl.multiple_of(i * rows, rows), rows)
+        total = terms[0][block, :].astype(F32)
+        for term in terms[1:]:
+            total = total + term[block, :].astype(F32)
+        dst[block, :] = total.astype(dst.dtype)
+        return carry
+
+    lax.fori_loop(0, dst.shape[0] // rows, body, 0)
+
+
+class Scatter:
+    def __init__(self, me, nz, index, grad, from_c, held, swap, came, result, sems, before):
+        self.me, self.nz, self.index, self.grad, self.from_c = me, nz, index, grad, from_c
+        self.held, self.swap, self.came, self.result = held, swap, came, result
+        self.load_sem, self.send_sem, self.recv_sem = sems
+        self.before = before
+        half = nz // 2
+        self.order = [a for k in range(half) for a in (nz - 1 - k, half - 1 - k)]
+
+    def where(self, a, b, e):
+        return (a * 2 + b) * 2 + e
+
+    def remote(self, src, dst, slot, hop):
+        sem = self.index * 8 * self.nz + slot
+        return pltpu.make_async_remote_copy(
+            src_ref=src, dst_ref=dst, send_sem=self.send_sem.at[sem], recv_sem=self.recv_sem.at[sem],
+            device_id=device_at(self.me, hop), device_id_type=MESH,
+        )
+
+    def core_copy(self, a, b, e):
+        i = self.where(a, b, e)
+        return self.remote(view_flat(self.grad, moved(self.me, (a, b, 1, e))), self.from_c.at[i], i, HOP_C)
+
+    def hop_copy(self, kind, a):
+        low = a < self.nz // 2
+        b, e = {"d": (1, 1), "x": (1, 0), "y": (0, 1), "z": (0, 0)}[kind]
+        hop = {"d": HOP_Y if low else HOP_X, "x": HOP_X, "y": HOP_Y, "z": hop_z(a)}[kind]
+        k = "dxyz".index(kind)
+        return self.remote(
+            self.held.at[self.where(a, b, e)], self.came.at[k * self.nz + a], (4 + k) * self.nz + a, hop
+        )
+
+    def took(self, kind, a):
+        self.hop_copy(kind, a).wait_recv()
+        return self.came.at["dxyz".index(kind) * self.nz + a]
+
+    def loads(self, a):
+        side = self.order.index(a) % 2
+        out = []
+        for b in range(2):
+            for e in range(2):
+                i, k = self.where(a, b, e), b * 2 + e
+                out.append(pltpu.make_async_copy(
+                    view_flat(self.grad, moved(self.me, (a, b, 0, e))), self.held.at[i], self.load_sem.at[side * 8 + k]
+                ))
+                out.append(pltpu.make_async_copy(
+                    self.from_c.at[i], self.swap.at[side * 4 + k], self.load_sem.at[side * 8 + 4 + k]
+                ))
+        return out
+
+    def exchange(self, a):
+        for b, e in ((1, 1), (1, 0), (0, 1), (0, 0)):
+            self.core_copy(a, b, e).start()
+
+    def fetch(self, a):
+        if self.before is not None:
+            self.before.release(a)
+        for b, e in ((1, 1), (1, 0), (0, 1), (0, 0)):
+            self.core_copy(a, b, e).wait_recv()
+        for load in self.loads(a):
+            load.start()
+
+    def diagonal(self, a):
+        for load in self.loads(a):
+            load.wait()
+        side, low = self.order.index(a) % 2, a < self.nz // 2
+        for b, e in ((1, 1), (1, 0), (0, 1), (0, 0)):
+            mine = self.held.at[self.where(a, b, e)]
+            add_rows(mine, [mine, self.swap.at[side * 4 + b * 2 + e]])
+            if (b, e) == (1, 1):
+                self.hop_copy("d", a).start()
+            elif (b, e) == ((0, 1) if low else (1, 0)):
+                self.hop_copy("y" if low else "x", a).start()
+
+    def square(self, a):
+        low = a < self.nz // 2
+        b, e = (1, 0) if low else (0, 1)
+        mine = self.held.at[self.where(a, b, e)]
+        add_rows(mine, [mine, self.took("d", a)])
+        self.hop_copy("x" if low else "y", a).start()
+
+    def column(self, a):
+        mine = self.held.at[self.where(a, 0, 0)]
+        terms = [mine, self.took("x", a), self.took("y", a)]
+        if a:
+            add_rows(mine, terms)
+            self.hop_copy("z", a).start()
+        else:
+            add_rows(self.result, terms + [self.took("z", k) for k in range(1, self.nz)])
+
+    def release(self, a):
+        for b in range(2):
+            for e in range(2):
+                self.core_copy(a, b, e).wait_send()
+        for kind in "dxyz" if a else "dxy":
+            self.hop_copy(kind, a).wait_send()
+
+    def calls(self, start, cost):
+        n = len(self.order)
+        out = [(start, functools.partial(self.exchange, a)) for a in self.order]
+        kinds = (self.fetch, self.diagonal, self.square, self.column)
+        lags = (0, 2, 3, 4)
+        steps = [
+            functools.partial(kind, self.order[t - lag])
+            for t in range(n + lags[-1])
+            for kind, lag in reversed(list(zip(kinds, lags)))
+            if 0 <= t - lag < n
+        ]
+        unit = cost / len(steps)
+        return out + [(start + unit * (i + 1), step) for i, step in enumerate(steps)]
+
+
+def transpose_into(dst, src):
+    def body(i, carry):
+        block = pl.ds(pl.multiple_of(i * 128, 128), 128)
+        dst[:, block] = src[block, :].T
+        return carry
+
+    lax.fori_loop(0, src.shape[0] // 128, body, 0)
+
+
+def backward_kernel(nz, tokens, seg_col, seg_row, proj, out, up, down, norm, qkv_in, ctx_in, lse,
+                    resid, hidden, act, slope, dres, dffn, dnorm_two,
+                    input_grad, down_red, up_red, mix_red, norm_sum,
+                    down_grad, up_grad, mix_grad, down_c, up_c, mix_c,
+                    tiles, buf_a, buf_b, buf_c, total, dpre, stage, ctx, w_out, bias, dqkv, resid_tile, dq,
+                    held, swap, came_down, came_up, came_mix,
+                    load_sem, send_sem, recv_sem, io_sem, parts, came, sum_send, sum_recv):
+    me = position()
+    t_here, seq = total.shape[0], seg_row.shape[2]
+    rows_here, pairs = t_here // seq, D // 128
+    n_ff = FF // 512
+    copies = {}
+
+    def begin(key, src, dst, sem):
+        copies[key] = pltpu.make_async_copy(src, dst, io_sem.at[sem])
+        copies[key].start()
+
+    def col512(j):
+        return pl.ds(pl.multiple_of(j * 512, 512), 512)
+
+    def tile_copy(src, j, base, sem):
+        return pltpu.make_async_copy(src.at[:, col512(j)], tiles.at[base + j % 2], io_sem.at[sem + j % 2])
+
+    def stage_copy(dst, col, slot):
+        return pltpu.make_async_copy(stage.at[slot], dst.at[:, col], io_sem.at[8 + slot])
+
+    def put_stage(i, value, dst, col):
+        slot = i % 2
+
+        @pl.when(i >= 2)
+        def _():
+            stage_copy(dst, col, slot).wait()
+
+        stage[slot] = value.astype(BF16)
+        stage_copy(dst, col, slot).start()
+
+    def flush_stage(dst):
+        for slot in range(2):
+            stage_copy(dst, pl.ds(0, 512), slot).wait()
+
+    begin("dffn", dffn, buf_a, 10)
+    begin("hidden", hidden, ctx, 11)
+    begin("dres", dres, total, 12)
+    tile_copy(act, 0, 0, 0).start()
+    entry_barrier(me, nz)
+    sems = (load_sem, send_sem, recv_sem)
+    first = Scatter(me, nz, 0, down_grad, down_c, held, swap, came_down, down_red, sems, None)
+    second = Scatter(me, nz, 1, up_grad, up_c, held, swap, came_up, up_red, sems, first)
+    third = Scatter(me, nz, 2, mix_grad, mix_c, held, swap, came_mix, mix_red, sems, second)
+    small = SmallSum(me, nz, parts, came, sum_send, sum_recv)
+
+    step_down, step_ffn, step_ln, step_out, step_attn, step_proj, step_in = BACKWARD_STEPS
+    cost = BACKWARD_COST
+    n_attn, n_m = rows_here * pairs, t_here // 256
+    t_down = n_ff * step_down
+    t_ffn = t_down + 3 * n_ff * step_ffn
+    t_ln = t_ffn + n_m * step_ln
+    t_mix = t_ln + 4 * step_out
+    t_attn = t_mix + n_attn * step_attn
+    t_proj = t_attn + 6 * step_proj
+    calls = first.calls(t_down, cost)
+    plans, left = spread(calls, [(3 * n_ff, t_down, step_ffn)])
+    plan_ffn = plans[0]
+    calls = left + second.calls(max(t_ffn, t_down + cost), cost)
+    n_small = len(small.hops)
+    sums = [(t_ln, functools.partial(small.start, 0))]
+    for i in range(n_small):
+        sums.append((t_mix + 4.0 * (i + 1), functools.partial(small.finish, i)))
+        if i + 1 < n_small:
+            sums.append((t_mix + 4.0 * (i + 1), functools.partial(small.start, i + 1)))
+    calls = sorted(calls + sums, key=lambda c: c[0])
+    plans, left = spread(
+        calls,
+        [(n_m, t_ffn, step_ln), (2, t_ln, step_out), (2, t_ln + 2 * step_out, step_out),
+         (n_attn, t_mix, step_attn), (6, t_attn, step_proj)],
+    )
+    plan_ln, plan_out, plan_ctx, plan_attn, plan_proj = plans
+
+    copies["dffn"].wait()
+    transpose_into(buf_b, buf_a)
+
+    def down_step(j):
+        @pl.when(j + 1 < n_ff)
+        def _():
+            tile_copy(act, j + 1, 0, 0).start()
+
+        tile_copy(act, j, 0, 0).wait()
+        put_stage(j, dot_nn(buf_b[...], tiles[j % 2]), down_grad, col512(j))
+
+    phase(n_ff, [down_step], {})
+    for src, base in ((down, 2), (slope, 4), (up, 6)):
+        tile_copy(src, 0, base, base).start()
+    copies["hidden"].wait()
+    transpose_into(buf_c, ctx)
+    begin("ctx", ctx_in, ctx, 11)
+    begin("w_out", out, w_out, 13)
+    flush_stage(down_grad)
+    copies["dres"].wait()
+
+    def pre_step(j):
+        @pl.when(j + 1 < n_ff)
+        def _():
+            for src, base in ((down, 2), (slope, 4), (up, 6)):
+                tile_copy(src, j + 1, base, base).start()
+
+        for src, base in ((down, 2), (slope, 4), (up, 6)):
+            tile_copy(src, j, base, base).wait()
+        dpre[...] = (dot_nn(buf_a[...], tiles[2 + j % 2]) * tiles[4 + j % 2].astype(F32)).astype(BF16)
+
+    def up_grad_step(j):
+        put_stage(j, dot_nn(buf_c[...], dpre[...]), up_grad, col512(j))
+
+    def hidden_step(j):
+        total[...] += dot_nt(dpre[...], tiles[6 + j % 2])
+
+    phase(n_ff, [pre_step, up_grad_step, hidden_step], plan_ffn)
+    flush_stage(up_grad)
+    for i in range(6):
+        begin(("qkv", i), qkv_in.at[i // 2, :, pl.ds((i % 2) * 512, 512)], tiles.at[i], i)
+    norm_sum[...] = jnp.zeros_like(norm_sum)
+
+    def resid_copy(m):
+        rows = pl.ds(pl.multiple_of(m * 256, 256), 256)
+        return pltpu.make_async_copy(resid.at[rows, :], resid_tile.at[m % 2], io_sem.at[14 + m % 2])
+
+    resid_copy(0).start()
+
+    def norm_step(m):
+        @pl.when(m + 1 < n_m)
+        def _():
+            resid_copy(m + 1).start()
+
+        resid_copy(m).wait()
+        rows = pl.ds(pl.multiple_of(m * 256, 256), 256)
+        unit, scale = normed(resid_tile[m % 2])
+        grad = total[rows, :]
+        norm_sum[0:1, :] = norm_sum[0:1, :] + jnp.sum(grad * unit, axis=0, keepdims=True)
+        norm_sum[1:2, :] = norm_sum[1:2, :] + jnp.sum(grad, axis=0, keepdims=True)
+        moved_grad = norm_backward(grad * norm[0:1, :], unit, scale)
+        total[rows, :] = moved_grad
+        buf_b[rows, :] = moved_grad.astype(BF16)
+
+    phase(n_m, [norm_step], plan_ln)
+    norm_sum[2:4, :] = dnorm_two[0:2, :]
+    parts[0] = norm_sum[...]
+    transpose_into(buf_a, buf_b)
+    copies["ctx"].wait()
+    copies["w_out"].wait()
+
+    def out_grad_step(j):
+        put_stage(j, dot_nn(buf_a[...], ctx[:, col512(j)]), mix_grad, col512(4 * j + 3))
+
+    phase(2, [out_grad_step], plan_out)
+
+    def ctx_step(j):
+        buf_a[:, col512(j)] = dot_nn(buf_b[...], w_out[:, col512(j)]).astype(BF16)
+
+    phase(2, [ctx_step], plan_ctx)
+    flush_stage(mix_grad)
+    mine = pl.ds(pl.multiple_of(me[3] * t_here, t_here), t_here)
+    begin("tok", tokens.at[mine, :], buf_b, 10)
+
+    def bias_step(r):
+        rows = pl.ds(pl.multiple_of(r * seq, seq), seq)
+        bias[r] = jnp.where(seg_col[rows, 0:1] == seg_row[r], 0.0, NEG_FILL)
+
+    phase(rows_here, [bias_step], {})
+    for i in range(6):
+        copies[("qkv", i)].wait()
+    head_of = lax.broadcasted_iota(jnp.int32, (128, 128), 1) // HEAD_DIM
+    head_pick = (
+        lax.broadcasted_iota(jnp.int32, (8, 128), 1) // HEAD_DIM == lax.broadcasted_iota(jnp.int32, (8, 128), 0)
+    ).astype(BF16)
+    shrink = jnp.asarray(HEAD_DIM**-0.5, BF16)
+
+    def per_head(block):
+        return jnp.concatenate([jnp.where(head_of == h, block, jnp.zeros_like(block)) for h in range(2)])
+
+    def attend_step(u):
+        r, p = u // pairs, u % pairs
+        side = p // 4
+        col = pl.ds(pl.multiple_of(p * 128, 128), 128)
+        near = pl.ds(pl.multiple_of((p % 4) * 128, 128), 128)
+        whole = pl.ds(pl.multiple_of(r * seq, seq), seq)
+        product = buf_a[whole, col].astype(F32) * ctx[whole, col].astype(F32)
+        coarse = product.astype(BF16)
+        fine = (product - coarse.astype(F32)).astype(BF16)
+        delta = dot_nt(head_pick, coarse) + dot_nt(head_pick, fine)
+        dq[...] = jnp.zeros_like(dq)
+        for kb in range(seq // 128):
+            low, high = max(0, kb - 2) * 128, min(seq // 128, kb + 3) * 128
+            k_rows = pl.ds(pl.multiple_of(r * seq + kb * 128, 128), 128)
+            q_rows = pl.ds(pl.multiple_of(r * seq + low, 128), high - low)
+            q = tiles[side, q_rows, near] * shrink
+            keys = per_head(tiles[2 + side, k_rows, near])
+            grad = buf_a[q_rows, col]
+            block = bias[r, kb * 128 : kb * 128 + 128, low:high]
+            scores = dot_nt(keys, q)
+            d_probs = dot_nt(per_head(tiles[4 + side, k_rows, near]), grad)
+            probs, d_scores = [], []
+            for h in range(2):
+                part = slice(h * 128, h * 128 + 128)
+                prob = jnp.exp(scores[part] + block - lse[u, h : h + 1, low:high])
+                probs.append(prob.astype(BF16))
+                d_scores.append((prob * (d_probs[part] - delta[h : h + 1, low:high])).astype(BF16))
+            probs, d_scores = jnp.concatenate(probs), jnp.concatenate(d_scores)
+            d_value = dot_nn(probs, grad)
+            d_key = dot_nn(d_scores, q)
+            dqkv[4 + side, k_rows, near] = jnp.where(head_of == 0, d_value[:128], d_value[128:]).astype(BF16)
+            dqkv[2 + side, k_rows, near] = jnp.where(head_of == 0, d_key[:128], d_key[128:]).astype(BF16)
+            dq[:, low:high] += dot_nn(keys.T, d_scores)
+        dqkv[side, whole, near] = (dq[...].T * HEAD_DIM**-0.5).astype(BF16)
+
+    phase(n_attn, [attend_step], plan_attn)
+    for i in range(6):
+        begin(("proj", i), proj.at[i // 2, :, pl.ds((i % 2) * 512, 512)], tiles.at[i], i)
+    copies["tok"].wait()
+    transpose_into(buf_c, buf_b)
+
+    def proj_step(i):
+        put_stage(i, dot_nn(buf_c[...], dqkv[i]), mix_grad, col512((i % 2) * 4 + i // 2))
+
+    phase(6, [proj_step], plan_proj)
+    flush_stage(mix_grad)
+    for i in range(6):
+        copies[("proj", i)].wait()
+    calls = left + third.calls(t_proj, cost)
+    plans, left = spread(calls, [(n_m, t_proj, step_in)])
+
+    def in_copy(m):
+        rows = pl.ds(pl.multiple_of(m * 256, 256), 256)
+        return pltpu.make_async_copy(total.at[rows, :], input_grad.at[rows, :], io_sem.at[16 + m])
+
+    def input_step(m):
+        rows = pl.ds(pl.multiple_of(m * 256, 256), 256)
+        value = total[rows, :]
+        for i in range(6):
+            value = value + dot_nt(dqkv[i, rows, :], tiles[i])
+        total[rows, :] = value
+
+    phase(n_m, [input_step], plans[0])
+    for m in range(n_m):
+        in_copy(m).start()
+    for _, call in left:
+        call()
+    for a in third.order:
+        third.release(a)
+    for m in range(n_m):
+        in_copy(m).wait()
+    norm_sum[...] = parts[n_small]
+
+
+BACKWARD_STEPS = (1.5, 1.5, 1.2, 1.5, 2.6, 1.6, 2.6)
+BACKWARD_COST = 42.0
+
+
+def run_backward(nz, tokens_in, segments, proj, out, up, down, norm, qkv, ctx, lse,
+                 resid, hidden, act, slope, dres, dffn, dnorm_two):
+    t_here = dffn.shape[0]
+    rows_here, seq = segments.shape
+    n_sum = len(sum_hops(nz))
+    piece = (64, FF // 2)
+    seg_col = jnp.broadcast_to(segments.reshape(t_here, 1), (t_here, 128))
+    seg_row = segments.reshape(rows_here, 1, seq)
+    grad = jax.ShapeDtypeStruct((D, FF), BF16)
+    swapped = jax.ShapeDtypeStruct((4 * nz,) + piece, BF16)
+    red = jax.ShapeDtypeStruct(piece, F32)
+    results = pl.pallas_call(
+        functools.partial(backward_kernel, nz),
+        out_shape=[jax.ShapeDtypeStruct((t_here, D), F32), red, red, red, jax.ShapeDtypeStruct(norm.shape, F32)]
+        + [grad] * 3 + [swapped] * 3,
+        in_specs=[ANY, VMEM, VMEM] + [ANY] * 4 + [VMEM, ANY, ANY, VMEM] + [ANY] * 6 + [VMEM],
+        out_specs=[ANY] + [VMEM] * 4 + [ANY] * 6,
+        scratch_shapes=[
+            pltpu.VMEM((8, t_here, 512), BF16),
+            pltpu.VMEM((t_here, D), BF16),
+            pltpu.VMEM((t_here, D), BF16),
+            pltpu.VMEM((t_here, D), BF16),
+            pltpu.VMEM((t_here, D), F32),
+            pltpu.VMEM((t_here, 512), BF16),
+            pltpu.VMEM((2, t_here, 512), BF16),
+            pltpu.VMEM((t_here, D), BF16),
+            pltpu.VMEM((D, D), BF16),
+            pltpu.VMEM((rows_here, seq, seq), F32),
+            pltpu.VMEM((6, t_here, 512), BF16),
+            pltpu.VMEM((2, 256, D), F32),
+            pltpu.VMEM((128, seq), F32),
+            pltpu.VMEM((4 * nz,) + piece, BF16),
+            pltpu.VMEM((8,) + piece, BF16),
+            pltpu.VMEM((4 * nz,) + piece, BF16),
+            pltpu.VMEM((4 * nz,) + piece, BF16),
+            pltpu.VMEM((4 * nz,) + piece, BF16),
+            DMA((16,)),
+            DMA((24 * nz,)),
+            DMA((24 * nz,)),
+            DMA((20,)),
+            pltpu.VMEM((n_sum + 1,) + norm.shape, F32),
+            pltpu.VMEM((n_sum,) + norm.shape, F32),
+            DMA((n_sum,)),
+            DMA((n_sum,)),
+        ],
+        compiler_params=pltpu.CompilerParams(
+            collective_id=1, has_side_effects=True, vmem_limit_bytes=62 << 20
+        ),
+        name="backward",
+    )(tokens_in, seg_col, seg_row, proj, out, up, down, norm, qkv, ctx, lse,
+      resid, hidden, act, slope, dres, dffn, dnorm_two)
+    return results[:5]
 
 
 def local_rows(
@@ -961,10 +1228,6 @@
         jnp.zeros((8, D), F32), norm_params.astype(BF16).astype(F32), (0, norm_start)
     )
     rows_here = segment_ids.shape[0] // 2
-    seq_len = segment_ids.shape[1]
-    tokens_here = rows_here * seq_len
-    heads = D // HEAD_DIM
-    score_scale = HEAD_DIM ** (-0.5)
     segments = lax.dynamic_slice_in_dim(segment_ids, mp * rows_here, rows_here, 0)
     (proj_w, out_w, up_w, down_w, norm_full, qkv, context, lse, resid_one, hidden_low, act_low, slope,
      layer_out, d_resid_two, d_ffn, d_norm_two) = run_forward(
@@ -978,62 +1241,28 @@
         down_weight.astype(BF16),
         norm_wide,
     )
-    proj_w, out_w = proj_w.reshape(3, D, D), out_w.reshape(D, D)
-    up_w, down_w = up_w.reshape(D, FF), down_w.reshape(D, FF)
-    tokens = lax.dynamic_slice_in_dim(tokens_in, mp * tokens_here, tokens_here, 0)
-    heads_split = qkv.reshape(3, rows_here, seq_len, heads, HEAD_DIM)
-    lse_rows = lse[:, :2].reshape(rows_here, heads, seq_len)
-
-    def masked_scores(query_rows, key_rows, row_segments):
-        scores = dot_f32("qhd,khd->hqk", query_rows, key_rows) * score_scale
-        same_doc = row_segments[:, None] == row_segments[None, :]
-        return jnp.where(same_doc[None], scores, NEG_FILL)
-
-    d_gain_two, d_shift_two = d_norm_two[0], d_norm_two[1]
-    down_grad = dot_f32("td,tf->df", d_ffn, act_low).astype(BF16)
-    d_act = jnp.dot(d_ffn, down_w, preferred_element_type=F32)
-    d_pre = (d_act * slope.astype(F32)).astype(BF16)
-    up_grad = dot_f32("tc,tf->cf", hidden_low, d_pre).astype(BF16)
-    d_hidden = d_resid_two + dot_f32("tf,cf->tc", d_pre, up_w)
-    unit, unit_scale = normed(resid_one)
-    d_gain_one, d_shift_one = jnp.sum(d_hidden * unit, axis=0), jnp.sum(d_hidden, axis=0)
-    d_resid_one = norm_backward(d_hidden * norm_full[0], unit, unit_scale)
-    d_attn = d_resid_one.astype(BF16)
-    output_grad = dot_f32("td,tn->dn", d_attn, context).astype(BF16)
-    d_context = jnp.dot(d_attn, out_w, preferred_element_type=F32).astype(BF16)
-
-    def row_backward(packed):
-        query_rows, key_rows, value_rows, row_segments, row_lse, row_grad = packed
-        scores = masked_scores(query_rows, key_rows, row_segments)
-        row_probs = jnp.exp(scores - row_lse[..., None])
-        grad_heads = row_grad.reshape(seq_len, heads, HEAD_DIM)
-        d_probs = dot_f32("qhd,khd->hqk", grad_heads, value_rows)
-        row_inner = jnp.sum(d_probs * row_probs, axis=-1, keepdims=True)
-        d_scores = (row_probs * (d_probs - row_inner)).astype(BF16)
-        d_value = dot_f32("hqk,qhd->khd", row_probs.astype(BF16), grad_heads)
-        d_query = dot_f32("hqk,khd->qhd", d_scores, key_rows) * score_scale
-        d_key = dot_f32("hqk,qhd->khd", d_scores, query_rows) * score_scale
-        return tuple(g.astype(BF16).reshape(seq_len, D) for g in (d_query, d_key, d_value))
-
-    d_rows = lax.map(
-        row_backward,
-        (
-            heads_split[0],
-            heads_split[1],
-            heads_split[2],
-            segments,
-            lse_rows,
-            d_context.reshape(rows_here, seq_len, D),
-        ),
-    )
-    d_proj = jnp.stack(d_rows).reshape(3, tokens_here, D)
-    project_grad = dot_f32("tc,stn->scn", tokens, d_proj).astype(BF16)
-    input_grad = d_resid_one + dot_f32("stn,scn->tc", d_proj, proj_w)
-    norm_local = jnp.stack([d_gain_one, d_shift_one, d_gain_two, d_shift_two])
-    norm_local = jnp.concatenate([norm_local, jnp.zeros_like(norm_local)])
-    down_red, up_red, out_red, proj_red, norm_sum = scatter_grads(
-        nz, down_grad, up_grad, output_grad, project_grad, norm_local
-    )
+    input_grad, down_red, up_red, mix_red, norm_sum = run_backward(
+        nz,
+        tokens_in,
+        segments,
+        proj_w.reshape(3, D, D),
+        out_w.reshape(D, D),
+        up_w.reshape(D, FF),
+        down_w.reshape(D, FF),
+        norm_full,
+        qkv,
+        context,
+        lse,
+        resid_one,
+        hidden_low,
+        act_low,
+        slope,
+        d_resid_two,
+        d_ffn,
+        d_norm_two,
+    )
+    mix_red = mix_red.reshape(mix_red.shape[0], 4, -1).transpose(1, 0, 2)
+    proj_red, out_red = mix_red[:3], mix_red[3]
     norm_red = lax.dynamic_slice(norm_sum, (0, norm_start), (4, norm_cols))
     return (
         layer_out,

time: 663 us -> 432 us (0.65); the launches traced: 653 us -> 431 us
  matrix products: 153 us -> 0 us
  local copies, waits for them, and re-layouts: 71.9 us -> 9.24 us
  other arithmetic: 49.4 us -> 13.2 us
  Pallas kernels: 376 us -> 408 us
    dot_general x18 -> x0, matrix products: 153 us -> none  [the longest x16 133 us: dot_f32(): return jnp.einsum(spec, a, b, preferred_element_type=F32)]
    pallas_call x1, Pallas kernels: 183 us -> 215 us  [run_backward(): pl.pallas_call(functools.partial(backward_kernel, nz), out_shape=[jax.Sha...]
    convert_element_type x2 -> x0, other arithmetic: 23.4 us -> none  [row_backward(): d_scores = (row_probs * (d_probs - row_inner)).astype(BF16)]
    while x15 -> x0, local copies, waits for them, and re-layouts: 20.2 us -> none  [the longest x3 16.7 us: local_rows(): lax.map(row_backward, (heads_split[0], heads_split[1], heads_split[2], se...]
    squeeze x3 -> x0, local copies, waits for them, and re-layouts: 16.6 us -> none  [the longest x1 6.35 us: local_rows(): heads_split[2]]
    dynamic_update_slice x10 -> x0, local copies, waits for them, and re-layouts: 12.1 us -> none  [local_rows(): lax.map(row_backward, (heads_split[0], heads_split[1], heads_split[2], se...]
    slice x4 -> x0, local copies, waits for them, and re-layouts: 8.65 us -> none  [the longest x1 5.56 us: local_rows(): heads_split[2]]
where the time goes in v3:
time: 432 us; the launch traced here: 431 us
  Pallas kernels  408 us (94%)
  other arithmetic  13.2 us (3%)
  local copies, waits for them, and re-layouts  9.24 us (2%)
    pallas_call x1, Pallas kernels, run_backward(): pl.pallas_call(functools.partial(backward_kernel, nz), out_shape=[jax.Sha...  215 us
    pallas_call x1, Pallas kernels, run_forward(): pl.pallas_call(functools.partial(forward_kernel, nz), out_shape=[jax.Shap...  193 us

profile of v3, /device:TPU:0, one launch (start us, length us, event | category | flops | bytes accessed | tf_op | source)
XLA Modules:
  0.0 431.3 jit_solution(10767597864968612324)
XLA Ops:
  0.7 0.0 copy-start
  0.7 0.7 convert_convert_fusion
  1.4 0.0 copy-done
  1.4 0.6 reshape.66.seg_row
  2.0 0.2 dynamic_update_slice.3.norm
  2.3 0.0 copy-start.16
  2.3 1.6 convert_element_type.19.out
  3.8 1.7 convert_element_type.18.proj
  5.5 1.8 convert_element_type.20.up
  7.3 1.8 convert_element_type.21.down
  9.1 1.0 broadcast_in_dim.14.seg_col
  10.1 0.0 copy-done.16
  10.1 193.4 %forward.1 = (bf16[3,4,2,2,64,1024]{5,4,3,2,1,0:T(8,128)(2,1)}, bf16[4,2,2,64,1024]{4,3,2,1,0:T(8,128)(2,1)}, bf16[4,2,2,64,4096]{4,3,2,1,0:T(8,128)(2,1)}, bf16...) custom-call(bf16[2048,1024]{1,0:T(8,128)(2,1)} %tokens.3, ...), custom_call_target="tpu_custom_call" | custom-call | tf_op jit(solution)/shard_map/forward/pallas_call | solution.py:702
  203.4 0.0 copy-start.19
  203.5 0.0 copy-start.20
  203.5 0.0 copy-start.21
  203.5 0.0 copy-start.13
  203.5 0.0 copy-start.17
  203.5 0.0 copy-start.18
  203.5 0.0 copy-start.8
  203.5 0.0 copy-start.14
  203.5 0.0 copy-start.15
  203.6 214.5 %backward.1 = (f32[1024,1024]{1,0:T(8,128)}, f32[64,2048]{1,0:T(8,128)}, f32[64,2048]{1,0:T(8,128)}, f32[64,2048]{1,0:T(8,128)}, f32[8,1024]{1,0:T(8,128)}, /*in...) custom-call(bf16[2048,1024]{1,0:T(8,128)(2,1)} %tokens.3, ...), custom_call_target="tpu_custom_call" | custom-call | tf_op jit(solution)/shard_map/backward/pallas_call | solution.py:1160
  418.1 0.0 copy-start.3
  418.1 0.0 copy-start.4
  418.1 0.0 copy-start.5
  418.1 0.0 copy-start.6
  418.2 0.0 copy-start.9
  418.2 0.0 copy-start.10
  418.2 0.0 copy-start.11
  418.2 0.0 copy-start.12
  418.2 1.2 copy.44
  419.4 0.0 copy-done.19
  419.4 0.0 copy-done.20
  419.5 0.0 copy-done.21
  419.5 1.4 multiply_subtract_fusion.4
  420.9 0.0 copy-done.13
  420.9 0.0 copy-done.17
  420.9 0.0 copy-done.18
  420.9 0.8 multiply_subtract_fusion.3
  421.7 0.0 copy-done.8
  421.7 0.0 copy-done.14
  421.7 0.0 copy-done.15
  421.7 1.3 multiply_subtract_fusion.2
  423.0 0.0 copy-start.7
  423.0 0.0 copy-done.3
  423.0 0.0 copy-done.4
  423.0 0.0 copy-done.5
  423.0 0.0 copy-done.6
  423.0 0.0 copy-done.9
  423.0 0.0 copy-done.10
  423.0 0.0 copy-done.11
  423.0 0.0 copy-done.12
  423.0 0.0 copy-start.2
  423.1 2.2 multiply_subtract_fusion
  425.3 0.0 copy-done.7
  425.3 0.0 copy-start.1
  425.3 1.3 copy.50
  426.6 1.1 copy-done.2
  427.7 2.0 copy.51
  429.7 0.8 copy.52
  430.5 0.8 copy.53
  431.3 0.0 copy-done.1
  (4 shorter events, 0.0 us)
Async XLA Ops:
  0.7 0.7 copy-start
  2.3 7.8 %copy-start.16 = (f32[8,1024]{1,0:T(8,128)}, f32[8,1024]{1,0:T(8,128)S(1)}, u32[]{:S(2)}) copy-start(f32[8,1024]{1,0:T(8,128)S(1)} %dynamic_update_slice.3.norm) | copy-start | bytes 98308
  203.4 216.0 %copy-start.19 = (f32[4,32]{1,0:T(4,128)S(1)}, f32[4,32]{1,0:T(4,128)}, u32[]{:S(2)}) copy-start(f32[4,32]{1,0:T(4,128)} %param.33) | copy-start | bytes 1540
  203.5 216.0 %copy-start.20 = (f32[4,32]{1,0:T(4,128)S(1)}, f32[4,32]{1,0:T(4,128)}, u32[]{:S(2)}) copy-start(f32[4,32]{1,0:T(4,128)} %param.35) | copy-start | bytes 1540
  203.5 216.0 %copy-start.21 = (f32[4,32]{1,0:T(4,128)S(1)}, f32[4,32]{1,0:T(4,128)}, u32[]{:S(2)}) copy-start(f32[4,32]{1,0:T(4,128)} %param.34) | copy-start | bytes 1540
  203.5 217.4 %copy-start.13 = (f32[64,512]{1,0:T(8,128)S(1)}, f32[64,512]{1,0:T(8,128)}, u32[]{:S(2)}) copy-start(f32[64,512]{1,0:T(8,128)} %param.24) | copy-start | bytes 393220
  203.5 217.4 %copy-start.17 = (f32[64,512]{1,0:T(8,128)S(1)}, f32[64,512]{1,0:T(8,128)}, u32[]{:S(2)}) copy-start(f32[64,512]{1,0:T(8,128)} %param.26) | copy-start | bytes 393220
  203.5 217.4 %copy-start.18 = (f32[64,512]{1,0:T(8,128)S(1)}, f32[64,512]{1,0:T(8,128)}, u32[]{:S(2)}) copy-start(f32[64,512]{1,0:T(8,128)} %param.25) | copy-start | bytes 393220
  203.5 218.2 %copy-start.8 = (f32[3,64,512]{2,1,0:T(8,128)S(1)}, f32[3,64,512]{2,1,0:T(8,128)}, u32[]{:S(2)}) copy-start(f32[3,64,512]{2,1,0:T(8,128)} %param.21) | copy-start | bytes 1179652
  203.5 218.2 %copy-start.14 = (f32[3,64,512]{2,1,0:T(8,128)S(1)}, f32[3,64,512]{2,1,0:T(8,128)}, u32[]{:S(2)}) copy-start(f32[3,64,512]{2,1,0:T(8,128)} %param.23) | copy-start | bytes 1179652
  203.5 218.2 %copy-start.15 = (f32[3,64,512]{2,1,0:T(8,128)S(1)}, f32[3,64,512]{2,1,0:T(8,128)}, u32[]{:S(2)}) copy-start(f32[3,64,512]{2,1,0:T(8,128)} %param.22) | copy-start | bytes 1179652
  418.1 4.9 %copy-start.3 = (f32[64,2048]{1,0:T(8,128)S(1)}, f32[64,2048]{1,0:T(8,128)}, u32[]{:S(2)}) copy-start(f32[64,2048]{1,0:T(8,128)} %param.27) | copy-start | bytes 1572868
  418.1 4.9 %copy-start.4 = (f32[64,2048]{1,0:T(8,128)S(1)}, f32[64,2048]{1,0:T(8,128)}, u32[]{:S(2)}) copy-start(f32[64,2048]{1,0:T(8,128)} %param.30) | copy-start | bytes 1572868
  418.1 4.9 %copy-start.5 = (f32[64,2048]{1,0:T(8,128)S(1)}, f32[64,2048]{1,0:T(8,128)}, u32[]{:S(2)}) copy-start(f32[64,2048]{1,0:T(8,128)} %get-tuple-element.121) | copy-start | bytes 1572868
  418.1 4.9 %copy-start.6 = (f32[64,2048]{1,0:T(8,128)S(1)}, f32[64,2048]{1,0:T(8,128)}, u32[]{:S(2)}) copy-start(f32[64,2048]{1,0:T(8,128)} %get-tuple-element.117) | copy-start | bytes 1572868
  418.2 4.9 %copy-start.9 = (f32[64,2048]{1,0:T(8,128)S(1)}, f32[64,2048]{1,0:T(8,128)}, u32[]{:S(2)}) copy-start(f32[64,2048]{1,0:T(8,128)} %param.32) | copy-start | bytes 1572868
  418.2 4.9 %copy-start.10 = (f32[64,2048]{1,0:T(8,128)S(1)}, f32[64,2048]{1,0:T(8,128)}, u32[]{:S(2)}) copy-start(f32[64,2048]{1,0:T(8,128)} %param.31) | copy-start | bytes 1572868
  418.2 4.9 %copy-start.11 = (f32[64,2048]{1,0:T(8,128)S(1)}, f32[64,2048]{1,0:T(8,128)}, u32[]{:S(2)}) copy-start(f32[64,2048]{1,0:T(8,128)} %param.29) | copy-start | bytes 1572868
  418.2 4.9 %copy-start.12 = (f32[64,2048]{1,0:T(8,128)S(1)}, f32[64,2048]{1,0:T(8,128)}, u32[]{:S(2)}) copy-start(f32[64,2048]{1,0:T(8,128)} %param.28) | copy-start | bytes 1572868
  423.0 2.3 copy-start.7
  423.0 4.7 %copy-start.2 = (f32[1024,1024]{1,0:T(8,128)S(1)}, f32[1024,1024]{1,0:T(8,128)}, u32[]{:S(2)}) copy-start(f32[1024,1024]{1,0:T(8,128)} %get-tuple-element.108) | copy-start | bytes 12582916
  425.3 6.0 %copy-start.1 = (s32[4,512]{1,0:T(4,128)S(1)}, s32[4,512]{1,0:T(4,128)}, u32[]{:S(2)}) copy-start(s32[4,512]{1,0:T(4,128)} %param.20) | copy-start | bytes 24580

commit v4 on v3

--- a/solution.py
+++ b/solution.py
@@ -280,15 +280,9 @@
     return ref.at[z, x, c, :, pl.ds(pl.multiple_of(y * half, half), half)]
 
 
-def view_stack(ref, pos):
-    z, x, c, y = pos
-    half = ref.shape[5] // 2
-    return ref.at[:, z, x, c, :, pl.ds(pl.multiple_of(y * half, half), half)]
-
-
 class Gather:
-    def __init__(self, me, nz, own, out, view, send_sem, recv_sem, base):
-        self.me, self.nz, self.own, self.out, self.view = me, nz, own, out, view
+    def __init__(self, me, nz, out, view, send_sem, recv_sem, base):
+        self.me, self.nz, self.out, self.view = me, nz, out, view
         self.send_sem, self.recv_sem, self.base = send_sem, recv_sem, base
         self.sent = []
 
@@ -300,68 +294,54 @@
         return self.view(self.out, moved(self.me, rel))
 
     def copy(self, rel, hop):
-        arrives = tuple(r ^ h for r, h in zip(rel, hop))
+        arrives = self.slot(tuple(r ^ h for r, h in zip(rel, hop)))
         return pltpu.make_async_remote_copy(
-            src_ref=self.own if rel == OWN else self.piece(rel),
+            src_ref=self.piece(rel),
             dst_ref=self.piece(rel),
-            send_sem=self.send_sem.at[self.slot(arrives)],
-            recv_sem=self.recv_sem.at[self.slot(arrives)],
+            send_sem=self.send_sem.at[arrives],
+            recv_sem=self.recv_sem.at[arrives],
             device_id=device_at(self.me, hop),
             device_id_type=MESH,
         )
 
-    def send(self, rel, hop):
-        self.copy(rel, hop).start()
-        self.sent.append((rel, hop))
+    def send(self, rel, *hops):
+        for hop in hops:
+            self.copy(rel, hop).start()
+            self.sent.append((rel, hop))
 
     def wait(self, rel):
-        pltpu.make_async_remote_copy(
-            src_ref=self.own,
-            dst_ref=self.piece(rel),
-            send_sem=self.send_sem.at[self.slot(rel)],
-            recv_sem=self.recv_sem.at[self.slot(rel)],
-            device_id=device_at(self.me, HOP_C),
-            device_id_type=MESH,
-        ).wait_recv()
-
-    def run(self, steps):
-        for kind, rel, hop in steps:
-            if kind == "send":
-                self.send(rel, hop)
-            else:
-                self.wait(rel)
-
-    def steps_first(self):
-        out = [("send", OWN, HOP_X), ("send", OWN, HOP_Y)]
-        out += [("send", OWN, hop_z(a)) for a in range(1, self.nz)]
-        return out + [("send", OWN, HOP_C)]
-
-    def steps_square(self, a):
-        out = [("wait", (a, 1, 0, 0), None), ("wait", (a, 0, 0, 1), None)]
-        if a < self.nz // 2:
-            out.append(("send", (a, 1, 0, 0), HOP_Y))
-        else:
-            out.append(("send", (a, 0, 0, 1), HOP_X))
-        return out + [("send", (a, 1, 0, 0), HOP_C), ("send", (a, 0, 0, 1), HOP_C)]
-
-    def steps_level(self, a):
-        piece = hop_z(a)
-        return [("wait", piece, None)] + [("send", piece, hop) for hop in (HOP_X, HOP_Y, HOP_C)]
-
-    def steps_middle(self):
-        out = []
-        for a in range(1, self.nz):
-            out += self.steps_level(a) + self.steps_square(a - 1)
-        return out + self.steps_square(self.nz - 1)
-
-    def steps_diagonal(self):
-        out = []
-        for a in range(self.nz):
-            out += [("wait", (a, 1, 0, 1), None), ("send", (a, 1, 0, 1), HOP_C)]
-        return out
-
-    def steps_last(self):
-        return [("wait", (a, b, 1, e), None) for a in range(self.nz) for b in range(2) for e in range(2)]
+        self.copy(tuple(r ^ h for r, h in zip(rel, HOP_C)), HOP_C).wait_recv()
+
+    def first_square(self):
+        self.send(OWN, HOP_X, HOP_Y, HOP_C)
+
+    def first_column(self, *levels):
+        self.send(OWN, *[hop_z(a) for a in levels])
+
+    def level(self, a):
+        self.wait(hop_z(a))
+        self.send(hop_z(a), HOP_X, HOP_Y, HOP_C)
+
+    def square(self, a):
+        self.wait((a, 1, 0, 0))
+        if a % 4 == 0:
+            self.send((a, 1, 0, 0), HOP_Y)
+        self.wait((a, 0, 0, 1))
+        if a % 4 == 2:
+            self.send((a, 0, 0, 1), HOP_X)
+        self.send((a, 1, 0, 0), HOP_C)
+        self.send((a, 0, 0, 1), HOP_C)
+
+    def diagonal(self, a):
+        self.wait((a, 1, 0, 1))
+        if a % 2 == 0:
+            self.send((a, 1, 0, 1), hop_z(1))
+        self.send((a, 1, 0, 1), HOP_C)
+
+    def whole(self, a):
+        for b in range(2):
+            for e in range(2):
+                self.wait((a, b, 1, e))
 
     def drain(self):
         for rel, hop in self.sent:
@@ -399,30 +379,14 @@
         self.parts[i + 1] = self.parts[i] + self.came[i]
 
 
-ERFC_SLOPE = 0.33 * 0.5**0.5
-ERFC_POLY = (
-    0.1863683316091749,
-    0.1828075671230129,
-    0.2020873146971517,
-    0.044528074107268695,
-    0.41336767744180025,
-    -0.35626105794547547,
-    0.4631297570306923,
-    -0.13602774732192066,
-)
+LOG2_E = 1.4426950408889634
 PDF_SCALE = 0.3989422804014327
 
 
 def gelu_pair(u):
-    size = jnp.abs(u)
-    t = 1.0 / (1.0 + ERFC_SLOPE * size)
-    poly = 0.5 * ERFC_POLY[-1]
-    for coefficient in ERFC_POLY[-2::-1]:
-        poly = poly * t + 0.5 * coefficient
-    bell = jnp.exp(u * u * -0.5)
-    tail = poly * t * bell
-    phi = jnp.where(u >= 0.0, 1.0 - tail, tail)
-    return u * phi, phi + u * bell * PDF_SCALE
+    phi = 0.5 + 0.5 * lax.erf(u * 0.5**0.5)
+    bell = jnp.exp2(u * u * (-0.5 * LOG2_E))
+    return u * phi, phi + u * PDF_SCALE * bell
 
 
 def dot_nn(a, b):
@@ -462,55 +426,37 @@
     lax.fori_loop(0, count, step, 0)
 
 
-def spread(calls, spans):
-    plans, calls = [{} for _ in spans], list(calls)
-    for plan, (count, start, each) in zip(plans, spans):
-        for i in range(count):
-            while calls and calls[0][0] <= start + i * each:
-                plan.setdefault(i, []).append(calls.pop(0)[1])
-    return plans, calls
-
-
-def gather_calls(gathers, costs, start):
-    calls, marks, clock = [], [], start
-    nz = gathers[0].nz
-
-    def add(when, g, steps):
-        calls.append((when, functools.partial(g.run, steps)))
-
-    for i, (g, cost) in enumerate(zip(gathers, costs)):
-        first = g.steps_first()
-        if i == 0:
-            add(clock, g, first)
-        unit = cost / (3 * nz - 1)
-        tick = 0
-        for a in range(1, nz):
-            tick += 1
-            add(clock + tick * unit, g, g.steps_level(a))
-            if a == nz - 1 and i + 1 < len(gathers):
-                add(clock + tick * unit, gathers[i + 1], gathers[i + 1].steps_first()[2:-1])
-            tick += 1
-            add(clock + tick * unit, g, g.steps_square(a - 1))
-        tick += 1
-        add(clock + tick * unit, g, g.steps_square(nz - 1))
-        if i + 1 < len(gathers):
-            nxt = gathers[i + 1].steps_first()
-            add(clock + tick * unit, gathers[i + 1], nxt[:2] + nxt[-1:])
-        steps = g.steps_diagonal()
-        for a in range(nz):
-            tick += 1
-            add(clock + tick * unit, g, steps[2 * a : 2 * a + 2])
-        add(clock + cost, g, g.steps_last())
-        marks.append(len(calls))
-        clock += cost
-    return calls, marks
+ACTORS = "qkvoud"
+METHODS = (
+    "first_square", "first_column", "level", "square", "diagonal", "whole",
+    "exchange", "fetch", "join", "bend", "column",
+)
+
+
+def script_plans(script, actors):
+    plans = {}
+    for place, slots in script:
+        for slot, numbers in slots:
+            calls = plans.setdefault(place, {}).setdefault(slot, [])
+            for number in numbers:
+                actor = actors[ACTORS[number // 1000]]
+                method, level = METHODS[number // 10 % 100], number % 10
+                if method == "fetch":
+                    actor.take_side(level)
+                calls.append(functools.partial(getattr(actor, method), *(() if method == "first_square" else (level,))))
+    return plans
+
+
+def run_calls(plans, name):
+    for call in plans.get(name, {}).get(-1, []):
+        call()
 
 
 def forward_kernel(nz, tokens, cotangent, seg_col, seg_row, proj, out, up, down, norm,
                    proj_all, out_all, up_all, down_all, norm_all, qkv_out, ctx_out, lse,
                    resid_out, hidden_out, act_out, slope_out, layer_out, dres_out, dffn_out, dnorm,
-                   tok, cot, w_small, w_up, qkv, ctx, bias, res, hidden, act, pre, slope,
-                   send_sem, recv_sem, local_sem, parts, came, sum_send, sum_recv, io_sem):
+                   tok, cot, w_small, w_up, w_down, qkv, ctx, bias, res, hidden, act, pre, slope,
+                   send_sem, recv_sem, parts, came, sum_send, sum_recv, io_sem):
     me = position()
     t_here, seq = tok.shape[0], seg_row.shape[2]
     rows_here, pairs = t_here // seq, D // 128
@@ -524,24 +470,23 @@
     begin("tok", tokens.at[mine, :], tok, 0)
     begin("cot", cotangent, cot, 1)
     parts[0] = norm[...]
+    fulls = [w_small.at[i] for i in range(4)] + [w_up, w_down]
+    owns = [proj.at[i] for i in range(3)] + [out, up, down]
+    gathers = {
+        name: Gather(me, nz, fulls[i], view_rows, send_sem, recv_sem, 8 * nz * i) for i, name in enumerate("qkvoud")
+    }
+    for g, own in zip(gathers.values(), owns):
+        g.piece(OWN)[...] = own[...].astype(BF16)
     entry_barrier(me, nz)
-    owns, fulls = (proj, out, up, down), (proj_all, out_all, up_all, down_all)
-    views = (view_stack, view_rows, view_rows, view_rows)
-    n = 8 * nz
-    gathers = [
-        Gather(me, nz, owns[i], fulls[i], views[i], send_sem, recv_sem, n * i) for i in range(4)
-    ]
-    keep = [pltpu.make_async_copy(g.own, g.piece(OWN), local_sem.at[i]) for i, g in enumerate(gathers)]
-    costs = FORWARD_COSTS
-    calls, marks = gather_calls(gathers, costs, 0.0)
-    calls[0][1]()
-    for copy in keep:
-        copy.start()
     small = SmallSum(me, nz, parts, came, sum_send, sum_recv)
+    plans = script_plans(FORWARD_SCRIPT, gathers)
+    run_calls(plans, "start")
+    small.start(0)
     for i in range(len(small.hops)):
-        small.start(i)
-        small.finish(i)
-    norm_all[...] = parts[len(small.hops)]
+        calls = plans.setdefault("attn", {}).setdefault(2 * i, [])
+        calls.append(functools.partial(small.finish, i))
+        if i + 1 < len(small.hops):
+            calls.append(functools.partial(small.start, i + 1))
 
     def bias_step(r):
         rows = pl.ds(pl.multiple_of(r * seq, seq), seq)
@@ -549,64 +494,54 @@
         bias[r] = jnp.where(same, 0.0, NEG_FILL)
 
     phase(rows_here, [bias_step], {})
-    for _, call in calls[1 : marks[0]]:
-        call()
-    for copy in keep:
-        copy.wait()
     copies["tok"].wait()
-    begin("proj", proj_all, w_small.at[pl.ds(0, 3)], 2)
-
-    step_q, step_a, step_o, step_u = FORWARD_STEPS
-    n_q, n_a, n_o, n_u = 3 * D // 256, rows_here * pairs, t_here // 256, FF // 256
-    start_q = costs[0] + 2.0
-    start_a = start_q + n_q * step_q
-    plans, _ = spread(
-        calls[marks[0] : marks[2]], [(n_q, start_q, step_q), (n_a, start_a, step_a)]
-    )
-    done = sum(len(c) for plan in plans for c in plan.values())
-    rest_out = calls[marks[0] + done : marks[1]]
-    later = marks[0] + done + len(rest_out)
-    copies["proj"].wait()
-
-    def qkv_step(j):
-        s, col = j // (D // 256), pl.ds(pl.multiple_of((j % (D // 256)) * 256, 256), 256)
-        weight = w_small[s, :, :, :, :, col].reshape(D, 256)
-        qkv[s, :, col] = dot_nn(tok[...], weight).astype(BF16)
-
-    phase(n_q, [qkv_step], plans[0])
+    n_q, n_a, n_o, n_u = D // 256, rows_here * pairs, t_here // 256, FF // 256
+    for s, name in enumerate("qkv"):
+        run_calls(plans, name)
+
+        def project_step(j, s=s):
+            col = pl.ds(pl.multiple_of(j * 256, 256), 256)
+            qkv[s, :, col] = dot_nn(tok[...], w_small[s, :, :, :, :, col].reshape(D, 256)).astype(BF16)
+
+        phase(n_q, [project_step], plans.get(name + "m", {}))
+    begin("proj", w_small.at[pl.ds(0, 3)], proj_all, 2)
     begin("qkv", qkv, qkv_out, 3)
-    head_of = lax.broadcasted_iota(jnp.int32, (128, 128), 1) // HEAD_DIM
+    head_of = lax.broadcasted_iota(jnp.int32, (seq, 128), 1) // HEAD_DIM
+    ones = jnp.ones((16, seq), BF16)
 
     def attend_step(u):
         r, p = u // pairs, u % pairs
         col = pl.ds(pl.multiple_of(p * 128, 128), 128)
-        for qb in range(seq // 128):
-            low, high = max(0, qb - 2) * 128, min(seq // 128, qb + 3) * 128
-            q_rows = pl.ds(pl.multiple_of(r * seq + qb * 128, 128), 128)
-            k_rows = pl.ds(pl.multiple_of(r * seq + low, 128), high - low)
-            q = qkv[0, q_rows, col] * jnp.asarray(HEAD_DIM**-0.5, BF16)
-            both = jnp.concatenate([jnp.where(head_of == h, q, jnp.zeros_like(q)) for h in range(2)])
-            block = bias[r, qb * 128 : qb * 128 + 128, low:high]
-            scores = dot_nt(both, qkv[1, k_rows, col]) + jnp.concatenate([block, block])
-            top = jnp.max(scores, axis=-1, keepdims=True)
-            weights = jnp.exp(scores - top)
-            total = jnp.sum(weights, axis=-1, keepdims=True)
-            probs = (weights * (1.0 / total)).astype(BF16)
-            mixed = dot_nn(probs, qkv[2, k_rows, col])
-            ctx[q_rows, col] = jnp.where(head_of == 0, mixed[:128], mixed[128:]).astype(BF16)
-            level = top + jnp.log(total)
-            for h in range(2):
-                wide = jnp.broadcast_to(level[h * 128 : h * 128 + 128], (128, 128))
-                lse[u, h : h + 1, qb * 128 : qb * 128 + 128] = wide.T[0:1]
-
-    phase(n_a, [attend_step], plans[1])
-    for _, call in rest_out:
-        call()
-    begin("out", out_all, w_small.at[3], 4)
+        whole = pl.ds(pl.multiple_of(r * seq, seq), seq)
+        keys, values = qkv[1, whole, col], qkv[2, whole, col].T
+        keys = [jnp.where(head_of == h, keys, jnp.zeros_like(keys)) for h in range(2)]
+        values = [jnp.concatenate([values[h * HEAD_DIM : (h + 1) * HEAD_DIM], ones]) for h in range(2)]
+        blocks = [(low, h) for low in range(0, seq, 256) for h in range(2)]
+
+        def score(low, h):
+            q = qkv[0, pl.ds(pl.multiple_of(r * seq + low, 256), 256), col] * jnp.asarray(HEAD_DIM**-0.5, BF16)
+            return dot_nt(keys[h], q) + bias[r, :, low : low + 256]
+
+        waiting, mixed = [score(*blocks[0])], []
+        for n, (low, h) in enumerate(blocks):
+            if n + 1 < len(blocks):
+                waiting.append(score(*blocks[n + 1]))
+            scores = waiting.pop(0)
+            top = jnp.max(scores, axis=0, keepdims=True)
+            weights = jnp.exp(scores - top).astype(BF16)
+            sums = dot_nn(values[h], weights)
+            total = sums[HEAD_DIM : HEAD_DIM + 1]
+            mixed.append(sums[:HEAD_DIM] * (1.0 / total))
+            lse[u, h : h + 1, low : low + 256] = top + jnp.log(total)
+        for n, low in enumerate(range(0, seq, 256)):
+            rows = pl.ds(pl.multiple_of(r * seq + low, 256), 256)
+            ctx[rows, col] = jnp.concatenate(mixed[2 * n : 2 * n + 2]).T.astype(BF16)
+
+    phase(n_a, [attend_step], plans["attn"])
+    run_calls(plans, "o")
+    norm_all[...] = parts[len(small.hops)]
+    begin("out", w_small.at[3], out_all, 4)
     begin("ctx", ctx, ctx_out, 5)
-    start_o = max(start_a + n_a * step_a, costs[0] + costs[1])
-    plans, rest_up = spread(calls[later : marks[2]], [(n_o, start_o, step_o)])
-    copies["out"].wait()
 
     def out_step(m):
         rows = pl.ds(pl.multiple_of(m * 256, 256), 256)
@@ -616,58 +551,81 @@
         unit, _ = normed(total)
         hidden[rows, :] = (unit * norm_all[0:1, :] + norm_all[1:2, :]).astype(BF16)
 
-    phase(n_o, [out_step], plans[0])
+    phase(n_o, [out_step], plans.get("out", {}))
     begin("res", res, resid_out, 6)
     begin("hidden", hidden, hidden_out, 7)
-    for _, call in rest_up:
-        call()
-    begin("up", up_all, w_up, 8)
-    start_u = costs[0] + costs[1] + costs[2] + 2.0
-    plans, rest_down = spread(calls[marks[2] :], [(n_u, start_u, step_u)])
-    copies["up"].wait()
+    run_calls(plans, "u")
+    begin("up", w_up, up_all, 8)
+
+    n_half = 2 * FF // 256
+    rows_half = t_here // 2
+
+    def half_of(i):
+        col = pl.ds(pl.multiple_of((i // 2) * 256, 256), 256)
+        rows = pl.ds(pl.multiple_of((i % 2) * rows_half, rows_half), rows_half)
+        return rows, col
+
+    def up_dot(i, dst):
+        rows, col = half_of(i)
+        dst[...] = dot_nn(hidden[rows, :], w_up[:, :, :, :, col].reshape(D, 256))
+
+    def up_act(i, src):
+        rows, col = half_of(i)
+        for k in range(0, rows_half, 64):
+            part = pl.ds(pl.multiple_of((i % 2) * rows_half + k, 64), 64)
+            value, tangent = gelu_pair(src[k : k + 64, :])
+            act[part, col] = value.astype(BF16)
+            slope[(i // 2) % 2, part, :] = tangent.astype(BF16)
+
+    def slope_copy(j):
+        col = pl.ds(pl.multiple_of(j * 256, 256), 256)
+        return pltpu.make_async_copy(slope.at[j % 2], slope_out.at[:, col], io_sem.at[9 + j % 2])
+
+    up_dot(0, pre.at[0])
 
     def up_step(j):
-        col = pl.ds(pl.multiple_of(j * 256, 256), 256)
-        slot = j % 2
-        pre[...] = dot_nn(hidden[...], w_up[:, :, :, :, col].reshape(D, 256))
-
         @pl.when(j >= 2)
         def _():
-            slope_copy(j - 2, slot).wait()
-
-        def chunk(i, carry):
-            rows = pl.ds(pl.multiple_of(i * 32, 32), 32)
-            value, tangent = gelu_pair(pre[rows, :])
-            act[rows, col] = value.astype(BF16)
-            slope[slot, rows, :] = tangent.astype(BF16)
-            return carry
-
-        lax.fori_loop(0, t_here // 32, chunk, 0)
-        slope_copy(j, slot).start()
-
-    def slope_copy(j, slot):
-        col = pl.ds(pl.multiple_of(j * 256, 256), 256)
-        return pltpu.make_async_copy(slope.at[slot], slope_out.at[:, col], io_sem.at[9 + slot])
-
-    phase(n_u, [up_step], plans[0])
+            slope_copy(j - 2).wait()
+
+        up_dot(2 * j + 1, pre.at[1])
+        up_act(2 * j, pre.at[0])
+
+    def up_next(j):
+        up_dot((2 * j + 2) % n_half, pre.at[0])
+        up_act(2 * j + 1, pre.at[1])
+        slope_copy(j).start()
+
+    phase(n_u, [up_step, up_next], plans.get("up", {}))
     begin("act", act, act_out, 11)
-    for _, call in rest_down:
-        call()
-    for k in range(4):
-        begin(("down", k), down_all.at[:, :, :, :, pl.ds(k * D, D)], w_small.at[k], 12 + k)
     for j in (n_u - 2, n_u - 1):
-        slope_copy(j, j % 2).wait()
-    for key in ("cot", "res", "hidden") + tuple(("down", k) for k in range(4)):
+        slope_copy(j).wait()
+    for key in ("cot", "res", "hidden"):
         copies[key].wait()
     dnorm[...] = jnp.zeros_like(dnorm)
 
-    def down_step(m):
-        rows = pl.ds(pl.multiple_of(m * 256, 256), 256)
+    def hidden_step(m):
+        rows = pl.ds(pl.multiple_of(m * 128, 128), 128)
         unit, _ = normed(res[rows, :])
-        total = unit * norm_all[0:1, :] + norm_all[1:2, :]
-        for k in range(4):
-            total = total + dot_nt(act[rows, k * D : (k + 1) * D], w_small[k].reshape(D, D))
-        unit, scale = normed(total)
+        res[rows, :] = unit * norm_all[0:1, :] + norm_all[1:2, :]
+
+    phase(t_here // 128, [hidden_step], {})
+    for a in DOWN_LEVELS:
+        run_calls(plans, "d%d" % a)
+        level = me[0] ^ a
+        width = D // nz
+        col = pl.ds(pl.multiple_of(level * width, width), width)
+
+        def down_step(m):
+            rows = pl.ds(pl.multiple_of(m * 512, 512), 512)
+            res[rows, col] += dot_nt(act[rows, :], w_down[level].reshape(width, FF))
+
+        phase(t_here // 512, [down_step], {})
+    begin("down", w_down, down_all, 12)
+
+    def norm_step(m):
+        rows = pl.ds(pl.multiple_of(m * 128, 128), 128)
+        unit, scale = normed(res[rows, :])
         tok[rows, :] = (unit * norm_all[2:3, :] + norm_all[3:4, :]).astype(BF16)
         grad = cot[rows, :].astype(F32)
         dnorm[0:1, :] = dnorm[0:1, :] + jnp.sum(grad * unit, axis=0, keepdims=True)
@@ -676,18 +634,76 @@
         res[rows, :] = dres
         hidden[rows, :] = dres.astype(BF16)
 
-    phase(t_here // 256, [down_step], {})
-    begin("layer", tok, layer_out, 16)
-    begin("dres", res, dres_out, 17)
-    begin("dffn", hidden, dffn_out, 18)
-    for key in ("qkv", "ctx", "act", "layer", "dres", "dffn"):
+    phase(t_here // 128, [norm_step], {})
+    begin("layer", tok, layer_out, 13)
+    begin("dres", res, dres_out, 14)
+    begin("dffn", hidden, dffn_out, 15)
+    for g in gathers.values():
+        g.drain()
+    for key in ("proj", "out", "up", "down", "qkv", "ctx", "act", "layer", "dres", "dffn"):
         copies[key].wait()
-    for g in gathers:
-        g.drain()
-
-
-FORWARD_COSTS = (31.0, 10.0, 42.0, 42.0)
-FORWARD_STEPS = (0.8, 1.4, 1.2, 1.7)
+
+
+FORWARD_SCRIPT = (
+    ("start", (
+        (-1, (12, 11, 1000, 0, 1013, 1012, 13, 3011, 3000, 2000, 3012,)),
+    )),
+    ("q", (
+        (-1, (30, 2012, 22, 21, 2011, 4011, 1023, 2030, 1022, 3021, 1011, 4012, 32, 3022, 2022, 1030, 2021,
+            2040, 3032, 4000, 1032, 40, 42, 23, 1040, 3013, 3030, 2013, 2032, 3042, 52, 41, 1021, 1042, 4030,
+            31, 1033, 3040, 3052, 3023, 1041, 2023, 33, 3043, 43, 1031, 1043, 2042, 4022, 2050, 4013, 5011,
+            1052, 5000, 4021, 53, 2041, 1051, 3041, 3031, 1053, 2031, 50, 3050, 2052, 51,)),
+    )),
+    ("qm", (
+        (0, (1050,)),
+        (3, (2043,)),
+    )),
+    ("k", (
+        (-1, ()),
+    )),
+    ("km", (
+        (1, (3051, 3033, 2051,)),
+        (2, (2033, 5012,)),
+    )),
+    ("v", (
+        (-1, (3053, 5013, 4040, 2053,)),
+    )),
+    ("attn", (
+        (1, (4032,)),
+        (5, (5030,)),
+        (10, (4041, 4042, 4023,)),
+        (13, (5022, 5021, 5040,)),
+    )),
+    ("o", (
+        (-1, ()),
+    )),
+    ("out", (
+        (0, (5050, 4031, 4052,)),
+        (1, (4033, 4043,)),
+    )),
+    ("u", (
+        (-1, (5041, 4050, 4053, 4051,)),
+    )),
+    ("up", (
+        (1, (5032, 5023,)),
+        (17, (5042, 5031,)),
+        (26, (5033,)),
+        (29, (5043, 5052, 5051,)),
+    )),
+    ("d0", (
+        (-1, ()),
+    )),
+    ("d1", (
+        (-1, ()),
+    )),
+    ("d2", (
+        (-1, ()),
+    )),
+    ("d3", (
+        (-1, (5053,)),
+    )),
+)
+DOWN_LEVELS = (0, 1, 2, 3)
 
 
 def run_forward(nz, tokens_in, cotangent, segments, proj, out, up, down, norm):
@@ -719,12 +735,13 @@
             flat(D, BF16),
             jax.ShapeDtypeStruct((8, D), F32),
         ],
-        in_specs=[ANY, ANY, VMEM, VMEM, ANY, ANY, ANY, ANY, VMEM],
+        in_specs=[ANY, ANY] + [VMEM] * 7,
         out_specs=[ANY] * 4 + [VMEM, ANY, ANY, VMEM] + [ANY] * 7 + [VMEM],
         scratch_shapes=[
             pltpu.VMEM((t_here, D), BF16),
             pltpu.VMEM((t_here, D), BF16),
             pltpu.VMEM((4, nz, 2, 2, rows, D), BF16),
+            pltpu.VMEM((nz, 2, 2, rows, FF), BF16),
             pltpu.VMEM((nz, 2, 2, rows, FF), BF16),
             pltpu.VMEM((3, t_here, D), BF16),
             pltpu.VMEM((t_here, D), BF16),
@@ -732,19 +749,18 @@
             pltpu.VMEM((t_here, D), F32),
             pltpu.VMEM((t_here, D), BF16),
             pltpu.VMEM((t_here, FF), BF16),
-            pltpu.VMEM((t_here, 256), F32),
+            pltpu.VMEM((2, t_here // 2, 256), F32),
             pltpu.VMEM((2, t_here, 256), BF16),
-            DMA((32 * nz,)),
-            DMA((32 * nz,)),
-            DMA((4,)),
+            DMA((48 * nz,)),
+            DMA((48 * nz,)),
             pltpu.VMEM((n_sum + 1,) + norm.shape, F32),
             pltpu.VMEM((n_sum,) + norm.shape, F32),
             DMA((n_sum,)),
             DMA((n_sum,)),
-            DMA((19,)),
+            DMA((16,)),
         ],
         compiler_params=pltpu.CompilerParams(
-            collective_id=0, has_side_effects=True, vmem_limit_bytes=60 << 20
+            collective_id=0, has_side_effects=True, vmem_limit_bytes=62 << 20
         ),
         name="forward",
     )(tokens_in, cotangent, seg_col, seg_row, proj, out, up, down, norm)
@@ -769,17 +785,27 @@
     lax.fori_loop(0, dst.shape[0] // rows, body, 0)
 
 
+def add_pair(dst, other, rows=16):
+    def body(i, carry):
+        block = pl.ds(pl.multiple_of(i * rows, rows), rows)
+        dst[block, :] = dst[block, :] + other[block, :]
+        return carry
+
+    lax.fori_loop(0, dst.shape[0] // rows, body, 0)
+
+
 class Scatter:
-    def __init__(self, me, nz, index, grad, from_c, held, swap, came, result, sems, before):
+    def __init__(self, me, nz, index, grad, from_c, cut, held, swap, came, result, sems, counter, before=()):
         self.me, self.nz, self.index, self.grad, self.from_c = me, nz, index, grad, from_c
-        self.held, self.swap, self.came, self.result = held, swap, came, result
+        self.cut, self.held, self.swap, self.came, self.result = cut, held, swap, came, result
         self.load_sem, self.send_sem, self.recv_sem = sems
-        self.before = before
-        half = nz // 2
-        self.order = [a for k in range(half) for a in (nz - 1 - k, half - 1 - k)]
+        self.counter, self.side, self.before = counter, {}, before
 
     def where(self, a, b, e):
         return (a * 2 + b) * 2 + e
+
+    def part(self, ref, i):
+        return ref.at[i, :, pl.ds(*self.cut)]
 
     def remote(self, src, dst, slot, hop):
         sem = self.index * 8 * self.nz + slot
@@ -793,68 +819,76 @@
         return self.remote(view_flat(self.grad, moved(self.me, (a, b, 1, e))), self.from_c.at[i], i, HOP_C)
 
     def hop_copy(self, kind, a):
-        low = a < self.nz // 2
-        b, e = {"d": (1, 1), "x": (1, 0), "y": (0, 1), "z": (0, 0)}[kind]
-        hop = {"d": HOP_Y if low else HOP_X, "x": HOP_X, "y": HOP_Y, "z": hop_z(a)}[kind]
-        k = "dxyz".index(kind)
+        b, e = {"w": (1, 1), "d": (1, 1), "x": (1, 0), "y": (0, 1), "z": (0, 0)}[kind]
+        hop = {"w": hop_z(1), "d": HOP_Y if a % 4 == 0 else HOP_X, "x": HOP_X, "y": HOP_Y, "z": hop_z(a)}[kind]
+        slot = {"w": a // 2, "d": self.nz // 2 + a // 2, "x": self.nz + a, "y": 2 * self.nz + a, "z": 3 * self.nz + a}[kind]
         return self.remote(
-            self.held.at[self.where(a, b, e)], self.came.at[k * self.nz + a], (4 + k) * self.nz + a, hop
+            self.part(self.held, self.where(a, b, e)), self.part(self.came, slot), 4 * self.nz + slot, hop
         )
 
     def took(self, kind, a):
-        self.hop_copy(kind, a).wait_recv()
-        return self.came.at["dxyz".index(kind) * self.nz + a]
+        copy = self.hop_copy(kind, a)
+        copy.wait_recv()
+        return copy.dst_ref
+
+    def mine(self, a, b, e):
+        return self.part(self.held, self.where(a, b, e))
+
+    def pairs(self, a):
+        return [(self.where(a, b, e), b * 2 + e, (a, b, 0, e)) for b in range(2) for e in range(2)]
 
     def loads(self, a):
-        side = self.order.index(a) % 2
-        out = []
-        for b in range(2):
-            for e in range(2):
-                i, k = self.where(a, b, e), b * 2 + e
-                out.append(pltpu.make_async_copy(
-                    view_flat(self.grad, moved(self.me, (a, b, 0, e))), self.held.at[i], self.load_sem.at[side * 8 + k]
-                ))
-                out.append(pltpu.make_async_copy(
-                    self.from_c.at[i], self.swap.at[side * 4 + k], self.load_sem.at[side * 8 + 4 + k]
-                ))
+        out, side = [], self.side[a]
+        for i, k, rel in self.pairs(a):
+            out.append(pltpu.make_async_copy(
+                view_flat(self.grad, moved(self.me, rel)), self.part(self.held, i), self.load_sem.at[side * 8 + k]
+            ))
+            out.append(pltpu.make_async_copy(
+                self.from_c.at[i], self.part(self.swap, side * 4 + k), self.load_sem.at[side * 8 + 4 + k]
+            ))
         return out
 
     def exchange(self, a):
         for b, e in ((1, 1), (1, 0), (0, 1), (0, 0)):
             self.core_copy(a, b, e).start()
 
+    def take_side(self, a):
+        self.side[a] = len(self.counter) % 2
+        self.counter.append(a)
+
     def fetch(self, a):
-        if self.before is not None:
-            self.before.release(a)
+        for other in self.before:
+            other.release(a)
         for b, e in ((1, 1), (1, 0), (0, 1), (0, 0)):
             self.core_copy(a, b, e).wait_recv()
         for load in self.loads(a):
             load.start()
 
-    def diagonal(self, a):
+    def join(self, a):
         for load in self.loads(a):
             load.wait()
-        side, low = self.order.index(a) % 2, a < self.nz // 2
-        for b, e in ((1, 1), (1, 0), (0, 1), (0, 0)):
-            mine = self.held.at[self.where(a, b, e)]
-            add_rows(mine, [mine, self.swap.at[side * 4 + b * 2 + e]])
-            if (b, e) == (1, 1):
-                self.hop_copy("d", a).start()
-            elif (b, e) == ((0, 1) if low else (1, 0)):
-                self.hop_copy("y" if low else "x", a).start()
+        for i, k, _ in self.pairs(a):
+            add_pair(self.part(self.held, i), self.part(self.swap, self.side[a] * 4 + k))
+        if a % 2:
+            self.hop_copy("w", a).start()
+        if a % 4 != 0:
+            self.hop_copy("x", a).start()
+        if a % 4 != 2:
+            self.hop_copy("y", a).start()
+
+    def bend(self, a):
+        add_pair(self.mine(a, 1, 1), self.took("w", a))
+        self.hop_copy("d", a).start()
 
     def square(self, a):
-        low = a < self.nz // 2
-        b, e = (1, 0) if low else (0, 1)
-        mine = self.held.at[self.where(a, b, e)]
-        add_rows(mine, [mine, self.took("d", a)])
-        self.hop_copy("x" if low else "y", a).start()
+        kind, b, e = ("x", 1, 0) if a % 4 == 0 else ("y", 0, 1)
+        add_pair(self.mine(a, b, e), self.took("d", a))
+        self.hop_copy(kind, a).start()
 
     def column(self, a):
-        mine = self.held.at[self.where(a, 0, 0)]
-        terms = [mine, self.took("x", a), self.took("y", a)]
+        terms = [self.mine(a, 0, 0), self.took("x", a), self.took("y", a)]
         if a:
-            add_rows(mine, terms)
+            add_rows(terms[0], terms)
             self.hop_copy("z", a).start()
         else:
             add_rows(self.result, terms + [self.took("z", k) for k in range(1, self.nz)])
@@ -863,22 +897,8 @@
         for b in range(2):
             for e in range(2):
                 self.core_copy(a, b, e).wait_send()
-        for kind in "dxyz" if a else "dxy":
+        for kind in ("w", "x", "y", "z") if a % 2 else ("d", "x", "y", "z") if a else ("d", "x", "y"):
             self.hop_copy(kind, a).wait_send()
-
-    def calls(self, start, cost):
-        n = len(self.order)
-        out = [(start, functools.partial(self.exchange, a)) for a in self.order]
-        kinds = (self.fetch, self.diagonal, self.square, self.column)
-        lags = (0, 2, 3, 4)
-        steps = [
-            functools.partial(kind, self.order[t - lag])
-            for t in range(n + lags[-1])
-            for kind, lag in reversed(list(zip(kinds, lags)))
-            if 0 <= t - lag < n
-        ]
-        unit = cost / len(steps)
-        return out + [(start + unit * (i + 1), step) for i, step in enumerate(steps)]
 
 
 def transpose_into(dst, src):
@@ -892,11 +912,12 @@
 
 def backward_kernel(nz, tokens, seg_col, seg_row, proj, out, up, down, norm, qkv_in, ctx_in, lse,
                     resid, hidden, act, slope, dres, dffn, dnorm_two,
-                    input_grad, down_red, up_red, mix_red, norm_sum,
-                    down_grad, up_grad, mix_grad, down_c, up_c, mix_c,
-                    tiles, buf_a, buf_b, buf_c, total, dpre, stage, ctx, w_out, bias, dqkv, resid_tile, dq,
-                    held, swap, came_down, came_up, came_mix,
-                    load_sem, send_sem, recv_sem, io_sem, parts, came, sum_send, sum_recv):
+                    input_grad, *refs):
+    red, norm_sum, grads, swaps, refs = refs[:6], refs[6], refs[7:13], refs[13:19], refs[19:]
+    down_grad, up_grad, out_grad = grads[:3]
+    (tiles, buf_a, buf_b, buf_c, total, dpre, stage, ctx, w_out, bias, dqkv, resid_tile, dq,
+     held, swap, came_down, came_up, came_mix,
+     load_sem, send_sem, recv_sem, io_sem, parts, came, sum_send, sum_recv) = refs
     me = position()
     t_here, seq = total.shape[0], seg_row.shape[2]
     rows_here, pairs = t_here // seq, D // 128
@@ -936,37 +957,26 @@
     tile_copy(act, 0, 0, 0).start()
     entry_barrier(me, nz)
     sems = (load_sem, send_sem, recv_sem)
-    first = Scatter(me, nz, 0, down_grad, down_c, held, swap, came_down, down_red, sems, None)
-    second = Scatter(me, nz, 1, up_grad, up_c, held, swap, came_up, up_red, sems, first)
-    third = Scatter(me, nz, 2, mix_grad, mix_c, held, swap, came_mix, mix_red, sems, second)
+    counter = []
+    half = D // 2
+    cuts = [(0, FF // 2)] * 2 + [(i * half, half) for i in (3, 0, 1, 2)]
+    arrivals = (came_down, came_up) + (came_mix,) * 4
+    scatters = {}
+    for i, name in enumerate("duoqkv"):
+        before = {"u": "d", "o": "u"}.get(name)
+        scatters[name] = Scatter(
+            me, nz, i, grads[i], swaps[i], cuts[i], held, swap, arrivals[i], red[i], sems, counter,
+            [scatters[before]] if before else [],
+        )
     small = SmallSum(me, nz, parts, came, sum_send, sum_recv)
-
-    step_down, step_ffn, step_ln, step_out, step_attn, step_proj, step_in = BACKWARD_STEPS
-    cost = BACKWARD_COST
+    n_small = len(small.hops)
     n_attn, n_m = rows_here * pairs, t_here // 256
-    t_down = n_ff * step_down
-    t_ffn = t_down + 3 * n_ff * step_ffn
-    t_ln = t_ffn + n_m * step_ln
-    t_mix = t_ln + 4 * step_out
-    t_attn = t_mix + n_attn * step_attn
-    t_proj = t_attn + 6 * step_proj
-    calls = first.calls(t_down, cost)
-    plans, left = spread(calls, [(3 * n_ff, t_down, step_ffn)])
-    plan_ffn = plans[0]
-    calls = left + second.calls(max(t_ffn, t_down + cost), cost)
-    n_small = len(small.hops)
-    sums = [(t_ln, functools.partial(small.start, 0))]
+    plans = script_plans(BACKWARD_SCRIPT, scatters)
     for i in range(n_small):
-        sums.append((t_mix + 4.0 * (i + 1), functools.partial(small.finish, i)))
+        calls = plans.setdefault("attn", {}).setdefault(2 * i + 1, [])
+        calls.append(functools.partial(small.finish, i))
         if i + 1 < n_small:
-            sums.append((t_mix + 4.0 * (i + 1), functools.partial(small.start, i + 1)))
-    calls = sorted(calls + sums, key=lambda c: c[0])
-    plans, left = spread(
-        calls,
-        [(n_m, t_ffn, step_ln), (2, t_ln, step_out), (2, t_ln + 2 * step_out, step_out),
-         (n_attn, t_mix, step_attn), (6, t_attn, step_proj)],
-    )
-    plan_ln, plan_out, plan_ctx, plan_attn, plan_proj = plans
+            calls.append(functools.partial(small.start, i + 1))
 
     copies["dffn"].wait()
     transpose_into(buf_b, buf_a)
@@ -1005,7 +1015,7 @@
     def hidden_step(j):
         total[...] += dot_nt(dpre[...], tiles[6 + j % 2])
 
-    phase(n_ff, [pre_step, up_grad_step, hidden_step], plan_ffn)
+    phase(n_ff, [pre_step, up_grad_step, hidden_step], plans.get("ffn", {}))
     flush_stage(up_grad)
     for i in range(6):
         begin(("qkv", i), qkv_in.at[i // 2, :, pl.ds((i % 2) * 512, 512)], tiles.at[i], i)
@@ -1032,23 +1042,24 @@
         total[rows, :] = moved_grad
         buf_b[rows, :] = moved_grad.astype(BF16)
 
-    phase(n_m, [norm_step], plan_ln)
+    phase(n_m, [norm_step], plans.get("ln", {}))
     norm_sum[2:4, :] = dnorm_two[0:2, :]
     parts[0] = norm_sum[...]
+    small.start(0)
     transpose_into(buf_a, buf_b)
     copies["ctx"].wait()
     copies["w_out"].wait()
 
     def out_grad_step(j):
-        put_stage(j, dot_nn(buf_a[...], ctx[:, col512(j)]), mix_grad, col512(4 * j + 3))
-
-    phase(2, [out_grad_step], plan_out)
+        put_stage(j, dot_nn(buf_a[...], ctx[:, col512(j)]), out_grad, col512(j))
+
+    phase(2, [out_grad_step], plans.get("out", {}))
+    flush_stage(out_grad)
 
     def ctx_step(j):
         buf_a[:, col512(j)] = dot_nn(buf_b[...], w_out[:, col512(j)]).astype(BF16)
 
-    phase(2, [ctx_step], plan_ctx)
-    flush_stage(mix_grad)
+    phase(2, [ctx_step], plans.get("ctx", {}))
     mine = pl.ds(pl.multiple_of(me[3] * t_here, t_here), t_here)
     begin("tok", tokens.at[mine, :], buf_b, 10)
 
@@ -1079,16 +1090,27 @@
         fine = (product - coarse.astype(F32)).astype(BF16)
         delta = dot_nt(head_pick, coarse) + dot_nt(head_pick, fine)
         dq[...] = jnp.zeros_like(dq)
-        for kb in range(seq // 128):
-            low, high = max(0, kb - 2) * 128, min(seq // 128, kb + 3) * 128
+        n_blocks = seq // 128
+
+        def block_of(kb):
+            low, high = max(0, kb - 2) * 128, min(n_blocks, kb + 3) * 128
             k_rows = pl.ds(pl.multiple_of(r * seq + kb * 128, 128), 128)
             q_rows = pl.ds(pl.multiple_of(r * seq + low, 128), high - low)
+            return low, high, k_rows, q_rows
+
+        def products(kb):
+            low, high, k_rows, q_rows = block_of(kb)
             q = tiles[side, q_rows, near] * shrink
             keys = per_head(tiles[2 + side, k_rows, near])
-            grad = buf_a[q_rows, col]
+            return keys, q, dot_nt(keys, q), dot_nt(per_head(tiles[4 + side, k_rows, near]), buf_a[q_rows, col])
+
+        waiting = [products(0)]
+        for kb in range(n_blocks):
+            if kb + 1 < n_blocks:
+                waiting.append(products(kb + 1))
+            keys, q, scores, d_probs = waiting.pop(0)
+            low, high, k_rows, q_rows = block_of(kb)
             block = bias[r, kb * 128 : kb * 128 + 128, low:high]
-            scores = dot_nt(keys, q)
-            d_probs = dot_nt(per_head(tiles[4 + side, k_rows, near]), grad)
             probs, d_scores = [], []
             for h in range(2):
                 part = slice(h * 128, h * 128 + 128)
@@ -1096,29 +1118,28 @@
                 probs.append(prob.astype(BF16))
                 d_scores.append((prob * (d_probs[part] - delta[h : h + 1, low:high])).astype(BF16))
             probs, d_scores = jnp.concatenate(probs), jnp.concatenate(d_scores)
-            d_value = dot_nn(probs, grad)
+            d_value = dot_nn(probs, buf_a[q_rows, col])
             d_key = dot_nn(d_scores, q)
             dqkv[4 + side, k_rows, near] = jnp.where(head_of == 0, d_value[:128], d_value[128:]).astype(BF16)
             dqkv[2 + side, k_rows, near] = jnp.where(head_of == 0, d_key[:128], d_key[128:]).astype(BF16)
             dq[:, low:high] += dot_nn(keys.T, d_scores)
         dqkv[side, whole, near] = (dq[...].T * HEAD_DIM**-0.5).astype(BF16)
 
-    phase(n_attn, [attend_step], plan_attn)
+    phase(n_attn, [attend_step], plans["attn"])
     for i in range(6):
         begin(("proj", i), proj.at[i // 2, :, pl.ds((i % 2) * 512, 512)], tiles.at[i], i)
     copies["tok"].wait()
     transpose_into(buf_c, buf_b)
 
-    def proj_step(i):
-        put_stage(i, dot_nn(buf_c[...], dqkv[i]), mix_grad, col512((i % 2) * 4 + i // 2))
-
-    phase(6, [proj_step], plan_proj)
-    flush_stage(mix_grad)
+    for s, name in enumerate("qkv"):
+
+        def project_step(i, s=s):
+            put_stage(i, dot_nn(buf_c[...], dqkv[2 * s + i]), grads[3 + s], col512(i))
+
+        phase(2, [project_step], plans.get("p" + name, {}))
+        flush_stage(grads[3 + s])
     for i in range(6):
         copies[("proj", i)].wait()
-    calls = left + third.calls(t_proj, cost)
-    plans, left = spread(calls, [(n_m, t_proj, step_in)])
-
     def in_copy(m):
         rows = pl.ds(pl.multiple_of(m * 256, 256), 256)
         return pltpu.make_async_copy(total.at[rows, :], input_grad.at[rows, :], io_sem.at[16 + m])
@@ -1130,20 +1151,73 @@
             value = value + dot_nt(dqkv[i, rows, :], tiles[i])
         total[rows, :] = value
 
-    phase(n_m, [input_step], plans[0])
+    phase(n_m, [input_step], plans.get("in", {}))
     for m in range(n_m):
         in_copy(m).start()
-    for _, call in left:
-        call()
-    for a in third.order:
-        third.release(a)
+    run_calls(plans, "end")
+    for name in "oqkv":
+        for a in range(nz):
+            scatters[name].release(a)
     for m in range(n_m):
         in_copy(m).wait()
     norm_sum[...] = parts[n_small]
 
 
-BACKWARD_STEPS = (1.5, 1.5, 1.2, 1.5, 2.6, 1.6, 2.6)
-BACKWARD_COST = 42.0
+BACKWARD_SCRIPT = (
+    ("ffn", (
+        (0, (5062, 5061, 5060,)),
+        (4, (5072, 5063,)),
+        (6, (5082, 5071,)),
+        (7, (5070,)),
+        (8, (5081,)),
+        (9, (5080, 5073,)),
+        (11, (5083,)),
+        (13, (5090,)),
+        (14, (5101,)),
+        (17, (5092,)),
+        (21, (5103,)),
+        (23, (5032,)),
+    )),
+    ("ln", (
+        (1, (5030, 4063, 4061,)),
+    )),
+    ("out", (
+        (1, (4073, 4062, 4060, 5102,)),
+    )),
+    ("ctx", (
+        (1, (3063, 3060, 3061, 4071, 4083, 3062,)),
+    )),
+    ("attn", (
+        (0, (4072, 4081,)),
+        (4, (5100, 4082, 4103, 3073, 4070, 4092,)),
+        (5, (3083,)),
+        (6, (4080, 4101, 3071,)),
+        (7, (3081,)),
+        (8, (4090,)),
+        (12, (4032,)),
+    )),
+    ("pq", (
+        (0, (4030, 3103,)),
+    )),
+    ("pk", (
+        (0, (4102, 3101, 3072, 63, 61, 62, 60,)),
+        (1, (3082, 3092,)),
+    )),
+    ("pv", (
+        (0, (73, 72, 1061, 1063, 1060, 1062, 83, 82, 71,)),
+        (1, (3032, 81, 1073, 1071,)),
+    )),
+    ("in", (
+        (0, (103, 4100, 92, 1083, 3102, 3070, 1081, 70, 2063, 101, 3080, 3090, 1072, 80, 90, 1070, 2061, 32,
+            1082, 2073, 1080, 2062, 1103, 1092, 2060, 2083,)),
+        (1, (3030, 2072, 2071,)),
+        (2, (30, 1032, 1090, 2082, 1101, 2092, 3100, 102, 2081, 2070,)),
+        (3, (2080, 2103,)),
+    )),
+    ("end", (
+        (-1, (100, 1030, 2032, 2101, 1102, 2090, 2102, 2030, 1100, 2100,)),
+    )),
+)
 
 
 def run_backward(nz, tokens_in, segments, proj, out, up, down, norm, qkv, ctx, lse,
@@ -1154,15 +1228,16 @@
     piece = (64, FF // 2)
     seg_col = jnp.broadcast_to(segments.reshape(t_here, 1), (t_here, 128))
     seg_row = segments.reshape(rows_here, 1, seq)
-    grad = jax.ShapeDtypeStruct((D, FF), BF16)
-    swapped = jax.ShapeDtypeStruct((4 * nz,) + piece, BF16)
-    red = jax.ShapeDtypeStruct(piece, F32)
+    widths = (FF // 2,) * 2 + (D // 2,) * 4
+    reduced = [jax.ShapeDtypeStruct((64, w), F32) for w in widths]
+    grads = [jax.ShapeDtypeStruct((D, 2 * w), BF16) for w in widths]
+    swapped = [jax.ShapeDtypeStruct((4 * nz, 64, w), BF16) for w in widths]
     results = pl.pallas_call(
         functools.partial(backward_kernel, nz),
-        out_shape=[jax.ShapeDtypeStruct((t_here, D), F32), red, red, red, jax.ShapeDtypeStruct(norm.shape, F32)]
-        + [grad] * 3 + [swapped] * 3,
+        out_shape=[jax.ShapeDtypeStruct((t_here, D), F32)] + reduced + [jax.ShapeDtypeStruct(norm.shape, F32)]
+        + grads + swapped,
         in_specs=[ANY, VMEM, VMEM] + [ANY] * 4 + [VMEM, ANY, ANY, VMEM] + [ANY] * 6 + [VMEM],
-        out_specs=[ANY] + [VMEM] * 4 + [ANY] * 6,
+        out_specs=[ANY] + [VMEM] * 7 + [ANY] * 12,
         scratch_shapes=[
             pltpu.VMEM((8, t_here, 512), BF16),
             pltpu.VMEM((t_here, D), BF16),
@@ -1183,8 +1258,8 @@
             pltpu.VMEM((4 * nz,) + piece, BF16),
             pltpu.VMEM((4 * nz,) + piece, BF16),
             DMA((16,)),
-            DMA((24 * nz,)),
-            DMA((24 * nz,)),
+            DMA((48 * nz,)),
+            DMA((48 * nz,)),
             DMA((20,)),
             pltpu.VMEM((n_sum + 1,) + norm.shape, F32),
             pltpu.VMEM((n_sum,) + norm.shape, F32),
@@ -1197,7 +1272,7 @@
         name="backward",
     )(tokens_in, seg_col, seg_row, proj, out, up, down, norm, qkv, ctx, lse,
       resid, hidden, act, slope, dres, dffn, dnorm_two)
-    return results[:5]
+    return results[:8]
 
 
 def local_rows(
@@ -1235,13 +1310,13 @@
         tokens_in,
         cotangent,
         segments,
-        project_weight.astype(BF16),
-        output_weight.astype(BF16),
-        up_weight.astype(BF16),
-        down_weight.astype(BF16),
+        project_weight,
+        output_weight,
+        up_weight,
+        down_weight,
         norm_wide,
     )
-    input_grad, down_red, up_red, mix_red, norm_sum = run_backward(
+    input_grad, down_red, up_red, out_red, *proj_red, norm_sum = run_backward(
         nz,
         tokens_in,
         segments,
@@ -1261,8 +1336,7 @@
         d_ffn,
         d_norm_two,
     )
-    mix_red = mix_red.reshape(mix_red.shape[0], 4, -1).transpose(1, 0, 2)
-    proj_red, out_red = mix_red[:3], mix_red[3]
+    proj_red = jnp.stack(proj_red)
     norm_red = lax.dynamic_slice(norm_sum, (0, norm_start), (4, norm_cols))
     return (
         layer_out,

time: 432 us -> 344 us (0.80)
  Pallas kernels: 408 us -> 326 us
  other arithmetic: 13.2 us -> 8.54 us
    pallas_call x1, Pallas kernels: 193 us -> 152 us  [run_forward(): pl.pallas_call(functools.partial(forward_kernel, nz), out_shape=[jax.Shap...]
    pallas_call x1, Pallas kernels: 215 us -> 174 us  [run_backward(): pl.pallas_call(functools.partial(backward_kernel, nz), out_shape=[jax.Sha...]
    convert_element_type x4 -> x0, other arithmetic: 6.79 us -> none  [the longest x1 1.77 us: local_rows(): up_weight.astype(BF16)]
where the time goes in v4:
time: 344 us
  Pallas kernels  326 us (95%)
  local copies, waits for them, and re-layouts  8.65 us (3%)
  other arithmetic  8.54 us (2%)
    pallas_call x1, Pallas kernels, run_backward(): pl.pallas_call(functools.partial(backward_kernel, nz), out_shape=[jax.Sha...  174 us
    pallas_call x1, Pallas kernels, run_forward(): pl.pallas_call(functools.partial(forward_kernel, nz), out_shape=[jax.Shap...  152 us
    sub x4, other arithmetic, adam_step(): updated = weight - step_rate * (normed + DECAY_RATE * weight)  7.85 us

profile of v4, /device:TPU:0, one launch (start us, length us, event | category | flops | bytes accessed | tf_op | source)
XLA Modules:
  0.0 343.7 jit_solution(3384809904657601647)
XLA Ops:
  0.7 0.0 copy-start
  0.7 0.7 convert_convert_fusion
  1.4 0.0 copy-done
  1.4 0.6 reshape.63.seg_row
  2.0 0.2 dynamic_update_slice.3.norm
  2.3 0.0 copy-start.17
  2.3 1.0 broadcast_in_dim.14.seg_col
  3.3 0.0 copy-done.17
  3.3 151.8 %forward.1 = (bf16[3,4,2,2,64,1024]{5,4,3,2,1,0:T(8,128)(2,1)}, bf16[4,2,2,64,1024]{4,3,2,1,0:T(8,128)(2,1)}, bf16[4,2,2,64,4096]{4,3,2,1,0:T(8,128)(2,1)}, bf16...) custom-call(bf16[2048,1024]{1,0:T(8,128)(2,1)} %tokens.3, ...), custom_call_target="tpu_custom_call" | custom-call | tf_op jit(solution)/shard_map/forward/pallas_call | solution.py:718
  155.1 0.0 copy-start.19
  155.1 0.0 copy-start.20
  155.1 0.0 copy-start.21
  155.1 0.0 copy-start.14
  155.1 0.0 copy-start.18
  155.2 0.0 copy-start.8
  155.2 0.0 copy-start.15
  155.2 0.0 copy-start.16
  155.2 0.0 copy-start.12
  155.2 173.8 %backward.1 = (f32[1024,1024]{1,0:T(8,128)}, f32[64,2048]{1,0:T(8,128)}, f32[64,2048]{1,0:T(8,128)}, f32[64,512]{1,0:T(8,128)}, f32[64,512]{1,0:T(8,128)}, /*ind...) custom-call(bf16[2048,1024]{1,0:T(8,128)(2,1)} %tokens.3, ...), custom_call_target="tpu_custom_call" | custom-call | tf_op jit(solution)/shard_map/backward/pallas_call | solution.py:1235
  329.0 0.0 copy-start.3
  329.0 0.0 copy-start.4
  329.0 0.0 copy-start.6
  329.0 0.0 copy-start.7
  329.0 0.0 copy-start.9
  329.0 0.0 copy-start.10
  329.1 0.0 copy-start.11
  329.1 0.0 copy-done.19
  329.1 0.0 copy-done.20
  329.1 0.0 copy-done.21
  329.1 1.5 multiply_subtract_fusion.4
  330.6 0.0 copy-done.14
  330.6 0.0 copy-done.18
  330.6 1.8 multiply_subtract_fusion.3
  332.4 0.0 copy-done.8
  332.4 0.0 copy-done.15
  332.4 0.0 copy-done.16
  332.4 2.3 multiply_subtract_fusion.2
  334.7 0.0 copy-start.5
  334.7 0.0 copy-done.12
  334.7 0.0 copy-done.3
  334.7 0.0 copy-done.4
  334.7 0.0 copy-done.6
  334.8 0.0 copy-done.7
  334.8 0.0 copy-done.9
  334.8 0.0 copy-done.10
  334.8 0.0 copy-done.11
  334.8 0.0 copy-start.2
  334.8 2.2 multiply_subtract_fusion
  337.0 0.0 copy-done.5
  337.1 0.0 copy-start.1
  337.1 1.3 copy.47
  338.4 1.1 copy-done.2
  339.5 0.0 copy-start.13
  339.5 2.0 copy.48
  341.5 0.0 copy-done.13
  341.5 0.7 copy.49
  342.1 0.8 copy.50
  342.9 0.8 copy.51
  343.7 0.0 copy-done.1
  (4 shorter events, 0.0 us)
Async XLA Ops:
  0.7 0.7 copy-start
  2.3 1.0 copy-start.17
  155.1 174.0 %copy-start.19 = (f32[4,32]{1,0:T(4,128)S(1)}, f32[4,32]{1,0:T(4,128)}, u32[]{:S(2)}) copy-start(f32[4,32]{1,0:T(4,128)} %param.33) | copy-start | bytes 1540
  155.1 174.0 %copy-start.20 = (f32[4,32]{1,0:T(4,128)S(1)}, f32[4,32]{1,0:T(4,128)}, u32[]{:S(2)}) copy-start(f32[4,32]{1,0:T(4,128)} %param.35) | copy-start | bytes 1540
  155.1 174.0 %copy-start.21 = (f32[4,32]{1,0:T(4,128)S(1)}, f32[4,32]{1,0:T(4,128)}, u32[]{:S(2)}) copy-start(f32[4,32]{1,0:T(4,128)} %param.34) | copy-start | bytes 1540
  155.1 175.5 %copy-start.14 = (f32[64,512]{1,0:T(8,128)S(1)}, f32[64,512]{1,0:T(8,128)}, u32[]{:S(2)}) copy-start(f32[64,512]{1,0:T(8,128)} %out.1) | copy-start | bytes 393220
  155.1 175.5 %copy-start.18 = (f32[64,512]{1,0:T(8,128)S(1)}, f32[64,512]{1,0:T(8,128)}, u32[]{:S(2)}) copy-start(f32[64,512]{1,0:T(8,128)} %param.26) | copy-start | bytes 393220
  155.2 177.2 %copy-start.8 = (f32[3,64,512]{2,1,0:T(8,128)S(1)}, f32[3,64,512]{2,1,0:T(8,128)}, u32[]{:S(2)}) copy-start(f32[3,64,512]{2,1,0:T(8,128)} %proj.1) | copy-start | bytes 1179652
  155.2 177.2 %copy-start.15 = (f32[3,64,512]{2,1,0:T(8,128)S(1)}, f32[3,64,512]{2,1,0:T(8,128)}, u32[]{:S(2)}) copy-start(f32[3,64,512]{2,1,0:T(8,128)} %param.23) | copy-start | bytes 1179652
  155.2 177.2 %copy-start.16 = (f32[3,64,512]{2,1,0:T(8,128)S(1)}, f32[3,64,512]{2,1,0:T(8,128)}, u32[]{:S(2)}) copy-start(f32[3,64,512]{2,1,0:T(8,128)} %param.22) | copy-start | bytes 1179652
  155.2 179.5 %copy-start.12 = (f32[64,2048]{1,0:T(8,128)S(1)}, f32[64,2048]{1,0:T(8,128)}, u32[]{:S(2)}) copy-start(f32[64,2048]{1,0:T(8,128)} %param.28) | copy-start | bytes 1572868
  329.0 5.7 %copy-start.3 = (f32[64,2048]{1,0:T(8,128)S(1)}, f32[64,2048]{1,0:T(8,128)}, u32[]{:S(2)}) copy-start(f32[64,2048]{1,0:T(8,128)} %get-tuple-element.126) | copy-start | bytes 1572868
  329.0 5.7 %copy-start.4 = (f32[64,2048]{1,0:T(8,128)S(1)}, f32[64,2048]{1,0:T(8,128)}, u32[]{:S(2)}) copy-start(f32[64,2048]{1,0:T(8,128)} %get-tuple-element.122) | copy-start | bytes 1572868
  329.0 5.7 %copy-start.6 = (f32[64,2048]{1,0:T(8,128)S(1)}, f32[64,2048]{1,0:T(8,128)}, u32[]{:S(2)}) copy-start(f32[64,2048]{1,0:T(8,128)} %up.1) | copy-start | bytes 1572868
  329.0 5.7 %copy-start.7 = (f32[64,2048]{1,0:T(8,128)S(1)}, f32[64,2048]{1,0:T(8,128)}, u32[]{:S(2)}) copy-start(f32[64,2048]{1,0:T(8,128)} %down.1) | copy-start | bytes 1572868
  329.0 5.7 %copy-start.9 = (f32[64,2048]{1,0:T(8,128)S(1)}, f32[64,2048]{1,0:T(8,128)}, u32[]{:S(2)}) copy-start(f32[64,2048]{1,0:T(8,128)} %param.32) | copy-start | bytes 1572868
  329.0 5.7 %copy-start.10 = (f32[64,2048]{1,0:T(8,128)S(1)}, f32[64,2048]{1,0:T(8,128)}, u32[]{:S(2)}) copy-start(f32[64,2048]{1,0:T(8,128)} %param.31) | copy-start | bytes 1572868
  329.1 5.7 %copy-start.11 = (f32[64,2048]{1,0:T(8,128)S(1)}, f32[64,2048]{1,0:T(8,128)}, u32[]{:S(2)}) copy-start(f32[64,2048]{1,0:T(8,128)} %param.29) | copy-start | bytes 1572868
  334.7 2.3 copy-start.5
  334.8 4.7 %copy-start.2 = (f32[1024,1024]{1,0:T(8,128)S(1)}, f32[1024,1024]{1,0:T(8,128)}, u32[]{:S(2)}) copy-start(f32[1024,1024]{1,0:T(8,128)} %get-tuple-element.113) | copy-start | bytes 12582916
  337.1 6.7 %copy-start.1 = (s32[4,512]{1,0:T(4,128)S(1)}, s32[4,512]{1,0:T(4,128)}, u32[]{:S(2)}) copy-start(s32[4,512]{1,0:T(4,128)} %param.20) | copy-start | bytes 24580
  339.5 2.0 copy-start.13

commit v5 on v4

--- a/solution.py
+++ b/solution.py
@@ -915,8 +915,8 @@
                     input_grad, *refs):
     red, norm_sum, grads, swaps, refs = refs[:6], refs[6], refs[7:13], refs[13:19], refs[19:]
     down_grad, up_grad, out_grad = grads[:3]
-    (tiles, buf_a, buf_b, buf_c, total, dpre, stage, ctx, w_out, bias, dqkv, resid_tile, dq,
-     held, swap, came_down, came_up, came_mix,
+    (tiles, buf_a, buf_b, buf_c, total, dpre, stage, ctx, dqkv, resid_tile, dq,
+     held, held_mix, swap, came_down, came_up, came_mix,
      load_sem, send_sem, recv_sem, io_sem, parts, came, sum_send, sum_recv) = refs
     me = position()
     t_here, seq = total.shape[0], seg_row.shape[2]
@@ -963,9 +963,10 @@
     arrivals = (came_down, came_up) + (came_mix,) * 4
     scatters = {}
     for i, name in enumerate("duoqkv"):
-        before = {"u": "d", "o": "u"}.get(name)
+        before = {"u": "d"}.get(name)
         scatters[name] = Scatter(
-            me, nz, i, grads[i], swaps[i], cuts[i], held, swap, arrivals[i], red[i], sems, counter,
+            me, nz, i, grads[i], swaps[i], cuts[i], held if name in "du" else held_mix, swap, arrivals[i], red[i],
+            sems, counter,
             [scatters[before]] if before else [],
         )
     small = SmallSum(me, nz, parts, came, sum_send, sum_recv)
@@ -995,7 +996,8 @@
     copies["hidden"].wait()
     transpose_into(buf_c, ctx)
     begin("ctx", ctx_in, ctx, 11)
-    begin("w_out", out, w_out, 13)
+    for j in range(2):
+        begin(("w_out", j), out.at[:, pl.ds(j * 512, 512)], dqkv.at[j], 13 + 6 * j)
     flush_stage(down_grad)
     copies["dres"].wait()
 
@@ -1048,7 +1050,8 @@
     small.start(0)
     transpose_into(buf_a, buf_b)
     copies["ctx"].wait()
-    copies["w_out"].wait()
+    for j in range(2):
+        copies[("w_out", j)].wait()
 
     def out_grad_step(j):
         put_stage(j, dot_nn(buf_a[...], ctx[:, col512(j)]), out_grad, col512(j))
@@ -1057,15 +1060,18 @@
     flush_stage(out_grad)
 
     def ctx_step(j):
-        buf_a[:, col512(j)] = dot_nn(buf_b[...], w_out[:, col512(j)]).astype(BF16)
+        buf_a[:, col512(j)] = dot_nn(buf_b[...], dqkv[j]).astype(BF16)
 
     phase(2, [ctx_step], plans.get("ctx", {}))
     mine = pl.ds(pl.multiple_of(me[3] * t_here, t_here), t_here)
     begin("tok", tokens.at[mine, :], buf_b, 10)
 
+    bias = resid_tile
+
     def bias_step(r):
-        rows = pl.ds(pl.multiple_of(r * seq, seq), seq)
-        bias[r] = jnp.where(seg_col[rows, 0:1] == seg_row[r], 0.0, NEG_FILL)
+        for k in range(2):
+            rows = pl.ds(pl.multiple_of(r * seq + k * (seq // 2), seq // 2), seq // 2)
+            bias[r, :, k * seq : (k + 1) * seq] = jnp.where(seg_col[rows, 0:1] == seg_row[r], 0.0, NEG_FILL)
 
     phase(rows_here, [bias_step], {})
     for i in range(6):
@@ -1110,7 +1116,8 @@
                 waiting.append(products(kb + 1))
             keys, q, scores, d_probs = waiting.pop(0)
             low, high, k_rows, q_rows = block_of(kb)
-            block = bias[r, kb * 128 : kb * 128 + 128, low:high]
+            top, left = kb * 128 % (seq // 2), kb * 128 // (seq // 2) * seq
+            block = bias[r, top : top + 128, left + low : left + high]
             probs, d_scores = [], []
             for h in range(2):
                 part = slice(h * 128, h * 128 + 128)
@@ -1155,7 +1162,7 @@
     for m in range(n_m):
         in_copy(m).start()
     run_calls(plans, "end")
-    for name in "oqkv":
+    for name in "uoqkv":
         for a in range(nz):
             scatters[name].release(a)
     for m in range(n_m):
@@ -1165,57 +1172,57 @@
 
 BACKWARD_SCRIPT = (
     ("ffn", (
-        (0, (5062, 5061, 5060,)),
-        (4, (5072, 5063,)),
-        (6, (5082, 5071,)),
-        (7, (5070,)),
-        (8, (5081,)),
-        (9, (5080, 5073,)),
-        (11, (5083,)),
-        (13, (5090,)),
-        (14, (5101,)),
-        (17, (5092,)),
-        (21, (5103,)),
-        (23, (5032,)),
+        (0, (5061, 5062,)),
+        (4, (5071, 5063, 5060,)),
+        (6, (5081,)),
+        (7, (5073, 5072,)),
+        (9, (5083, 5082, 5070,)),
+        (11, (5080, 5090,)),
+        (14, (5092,)),
+        (15, (5103,)),
+        (23, (5030, 5032,)),
     )),
     ("ln", (
-        (1, (5030, 4063, 4061,)),
+        (1, (4063, 4061, 5101, 4062, 4060,)),
     )),
     ("out", (
-        (1, (4073, 4062, 4060, 5102,)),
+        (0, (4073,)),
+        (1, (5102,)),
     )),
     ("ctx", (
-        (1, (3063, 3060, 3061, 4071, 4083, 3062,)),
+        (1, (3061, 4071, 3062, 4083, 3060, 3063,)),
     )),
     ("attn", (
-        (0, (4072, 4081,)),
-        (4, (5100, 4082, 4103, 3073, 4070, 4092,)),
-        (5, (3083,)),
-        (6, (4080, 4101, 3071,)),
-        (7, (3081,)),
-        (8, (4090,)),
-        (12, (4032,)),
+        (0, (4081, 4072,)),
+        (2, (4082, 3071, 3072,)),
+        (3, (4103, 3081, 3082, 3070, 3073, 5100,)),
+        (4, (4092, 3080, 3083, 4070,)),
+        (6, (4080,)),
+        (9, (3101, 4090,)),
+        (10, (3090, 4101,)),
+        (13, (4032, 3092,)),
+        (14, (3103,)),
     )),
     ("pq", (
-        (0, (4030, 3103,)),
+        (0, (3032, 4030, 3030,)),
     )),
     ("pk", (
-        (0, (4102, 3101, 3072, 63, 61, 62, 60,)),
-        (1, (3082, 3092,)),
+        (0, (4102,)),
+        (1, (3102, 63, 61, 62, 60,)),
     )),
     ("pv", (
-        (0, (73, 72, 1061, 1063, 1060, 1062, 83, 82, 71,)),
-        (1, (3032, 81, 1073, 1071,)),
+        (0, (73,)),
+        (1, (83, 71, 1063, 72, 1062, 1061, 1060, 81, 82, 70,)),
     )),
     ("in", (
-        (0, (103, 4100, 92, 1083, 3102, 3070, 1081, 70, 2063, 101, 3080, 3090, 1072, 80, 90, 1070, 2061, 32,
-            1082, 2073, 1080, 2062, 1103, 1092, 2060, 2083,)),
-        (1, (3030, 2072, 2071,)),
-        (2, (30, 1032, 1090, 2082, 1101, 2092, 3100, 102, 2081, 2070,)),
-        (3, (2080, 2103,)),
+        (0, (103, 80, 1071, 92, 2063, 1072, 2061, 101, 1081, 4100, 1070, 1082, 1073, 2060, 90, 1080, 2073,
+            1083, 2071, 32, 2062, 2083,)),
+        (1, (1101, 30, 1090, 2081, 2072, 2070, 1092, 3100,)),
+        (2, (2082, 2092, 1103, 2080, 102,)),
+        (3, (1030, 1032, 2090, 2103,)),
     )),
     ("end", (
-        (-1, (100, 1030, 2032, 2101, 1102, 2090, 2102, 2030, 1100, 2100,)),
+        (-1, (2101, 2032, 1102, 2030, 100, 2102, 1100, 2100,)),
     )),
 )
 
@@ -1247,11 +1254,10 @@
             pltpu.VMEM((t_here, 512), BF16),
             pltpu.VMEM((2, t_here, 512), BF16),
             pltpu.VMEM((t_here, D), BF16),
-            pltpu.VMEM((D, D), BF16),
-            pltpu.VMEM((rows_here, seq, seq), F32),
             pltpu.VMEM((6, t_here, 512), BF16),
             pltpu.VMEM((2, 256, D), F32),
             pltpu.VMEM((128, seq), F32),
+            pltpu.VMEM((4 * nz,) + piece, BF16),
             pltpu.VMEM((4 * nz,) + piece, BF16),
             pltpu.VMEM((8,) + piece, BF16),
             pltpu.VMEM((4 * nz,) + piece, BF16),

time: 344 us -> 330 us (0.959)
  Pallas kernels: 326 us -> 311 us
    pallas_call x1, Pallas kernels: 174 us -> 159 us  [run_backward(): pl.pallas_call(functools.partial(backward_kernel, nz), out_shape=[jax.Sha...]
where the time goes in v5:
time: 330 us; the launch traced here: 329 us
  Pallas kernels  311 us (94%)
  local copies, waits for them, and re-layouts  8.65 us (3%)
  other arithmetic  8.54 us (3%)
    pallas_call x1, Pallas kernels, run_backward(): pl.pallas_call(functools.partial(backward_kernel, nz), out_shape=[jax.Sha...  159 us
    pallas_call x1, Pallas kernels, run_forward(): pl.pallas_call(functools.partial(forward_kernel, nz), out_shape=[jax.Shap...  152 us
    sub x4, other arithmetic, adam_step(): updated = weight - step_rate * (normed + DECAY_RATE * weight)  7.85 us
    unnamed x51, local copies, waits for them, and re-layouts  6.79 us

profile of v5, /device:TPU:0, one launch (start us, length us, event | category | flops | bytes accessed | tf_op | source)
XLA Modules:
  0.0 328.8 jit_solution(8672653633338411806)
XLA Ops:
  0.7 0.0 copy-start
  0.7 0.7 convert_convert_fusion
  1.4 0.0 copy-done
  1.4 0.6 reshape.63.seg_row
  2.0 0.2 dynamic_update_slice.3.norm
  2.3 0.0 copy-start.17
  2.3 1.0 broadcast_in_dim.14.seg_col
  3.3 0.0 copy-done.17
  3.3 151.8 %forward.1 = (bf16[3,4,2,2,64,1024]{5,4,3,2,1,0:T(8,128)(2,1)}, bf16[4,2,2,64,1024]{4,3,2,1,0:T(8,128)(2,1)}, bf16[4,2,2,64,4096]{4,3,2,1,0:T(8,128)(2,1)}, bf16...) custom-call(bf16[2048,1024]{1,0:T(8,128)(2,1)} %tokens.3, ...), custom_call_target="tpu_custom_call" | custom-call | tf_op jit(solution)/shard_map/forward/pallas_call | solution.py:718
  155.1 0.0 copy-start.19
  155.1 0.0 copy-start.20
  155.1 0.0 copy-start.21
  155.1 0.0 copy-start.14
  155.1 0.0 copy-start.18
  155.2 0.0 copy-start.8
  155.2 0.0 copy-start.15
  155.2 0.0 copy-start.16
  155.2 0.0 copy-start.12
  155.2 158.8 %backward.1 = (f32[1024,1024]{1,0:T(8,128)}, f32[64,2048]{1,0:T(8,128)}, f32[64,2048]{1,0:T(8,128)}, f32[64,512]{1,0:T(8,128)}, f32[64,512]{1,0:T(8,128)}, /*ind...) custom-call(bf16[2048,1024]{1,0:T(8,128)(2,1)} %tokens.3, ...), custom_call_target="tpu_custom_call" | custom-call | tf_op jit(solution)/shard_map/backward/pallas_call | solution.py:1242
  314.0 0.0 copy-start.3
  314.0 0.0 copy-start.4
  314.0 0.0 copy-start.6
  314.1 0.0 copy-start.7
  314.1 0.0 copy-start.9
  314.1 0.0 copy-start.10
  314.1 0.0 copy-start.11
  314.1 0.0 copy-done.19
  314.1 0.0 copy-done.20
  314.1 0.0 copy-done.21
  314.1 1.5 multiply_subtract_fusion.4
  315.6 0.0 copy-done.14
  315.6 0.0 copy-done.18
  315.6 1.8 multiply_subtract_fusion.3
  317.4 0.0 copy-done.8
  317.4 0.0 copy-done.15
  317.4 0.0 copy-done.16
  317.4 2.3 multiply_subtract_fusion.2
  319.8 0.0 copy-start.5
  319.8 0.0 copy-done.12
  319.8 0.0 copy-done.3
  319.8 0.0 copy-done.4
  319.8 0.0 copy-done.6
  319.8 0.0 copy-done.7
  319.8 0.0 copy-done.9
  319.8 0.0 copy-done.10
  319.8 0.0 copy-done.11
  319.8 0.0 copy-start.2
  319.8 2.2 multiply_subtract_fusion
  322.1 0.0 copy-done.5
  322.1 0.0 copy-start.1
  322.1 1.3 copy.47
  323.4 1.1 copy-done.2
  324.5 0.0 copy-start.13
  324.5 2.0 copy.48
  326.5 0.0 copy-done.13
  326.5 0.7 copy.49
  327.2 0.8 copy.50
  328.0 0.8 copy.51
  328.8 0.0 copy-done.1
  (4 shorter events, 0.0 us)
Async XLA Ops:
  0.7 0.7 copy-start
  2.3 1.0 copy-start.17
  155.1 159.0 %copy-start.19 = (f32[4,32]{1,0:T(4,128)S(1)}, f32[4,32]{1,0:T(4,128)}, u32[]{:S(2)}) copy-start(f32[4,32]{1,0:T(4,128)} %param.33) | copy-start | bytes 1540
  155.1 159.0 %copy-start.20 = (f32[4,32]{1,0:T(4,128)S(1)}, f32[4,32]{1,0:T(4,128)}, u32[]{:S(2)}) copy-start(f32[4,32]{1,0:T(4,128)} %param.35) | copy-start | bytes 1540
  155.1 159.0 %copy-start.21 = (f32[4,32]{1,0:T(4,128)S(1)}, f32[4,32]{1,0:T(4,128)}, u32[]{:S(2)}) copy-start(f32[4,32]{1,0:T(4,128)} %param.34) | copy-start | bytes 1540
  155.1 160.5 %copy-start.14 = (f32[64,512]{1,0:T(8,128)S(1)}, f32[64,512]{1,0:T(8,128)}, u32[]{:S(2)}) copy-start(f32[64,512]{1,0:T(8,128)} %out.1) | copy-start | bytes 393220
  155.1 160.5 %copy-start.18 = (f32[64,512]{1,0:T(8,128)S(1)}, f32[64,512]{1,0:T(8,128)}, u32[]{:S(2)}) copy-start(f32[64,512]{1,0:T(8,128)} %param.26) | copy-start | bytes 393220
  155.2 162.3 %copy-start.8 = (f32[3,64,512]{2,1,0:T(8,128)S(1)}, f32[3,64,512]{2,1,0:T(8,128)}, u32[]{:S(2)}) copy-start(f32[3,64,512]{2,1,0:T(8,128)} %proj.1) | copy-start | bytes 1179652
  155.2 162.3 %copy-start.15 = (f32[3,64,512]{2,1,0:T(8,128)S(1)}, f32[3,64,512]{2,1,0:T(8,128)}, u32[]{:S(2)}) copy-start(f32[3,64,512]{2,1,0:T(8,128)} %param.23) | copy-start | bytes 1179652
  155.2 162.3 %copy-start.16 = (f32[3,64,512]{2,1,0:T(8,128)S(1)}, f32[3,64,512]{2,1,0:T(8,128)}, u32[]{:S(2)}) copy-start(f32[3,64,512]{2,1,0:T(8,128)} %param.22) | copy-start | bytes 1179652
  155.2 164.6 %copy-start.12 = (f32[64,2048]{1,0:T(8,128)S(1)}, f32[64,2048]{1,0:T(8,128)}, u32[]{:S(2)}) copy-start(f32[64,2048]{1,0:T(8,128)} %param.28) | copy-start | bytes 1572868
  314.0 5.7 %copy-start.3 = (f32[64,2048]{1,0:T(8,128)S(1)}, f32[64,2048]{1,0:T(8,128)}, u32[]{:S(2)}) copy-start(f32[64,2048]{1,0:T(8,128)} %get-tuple-element.126) | copy-start | bytes 1572868
  314.0 5.7 %copy-start.4 = (f32[64,2048]{1,0:T(8,128)S(1)}, f32[64,2048]{1,0:T(8,128)}, u32[]{:S(2)}) copy-start(f32[64,2048]{1,0:T(8,128)} %get-tuple-element.122) | copy-start | bytes 1572868
  314.0 5.7 %copy-start.6 = (f32[64,2048]{1,0:T(8,128)S(1)}, f32[64,2048]{1,0:T(8,128)}, u32[]{:S(2)}) copy-start(f32[64,2048]{1,0:T(8,128)} %up.1) | copy-start | bytes 1572868
  314.1 5.7 %copy-start.7 = (f32[64,2048]{1,0:T(8,128)S(1)}, f32[64,2048]{1,0:T(8,128)}, u32[]{:S(2)}) copy-start(f32[64,2048]{1,0:T(8,128)} %down.1) | copy-start | bytes 1572868
  314.1 5.7 %copy-start.9 = (f32[64,2048]{1,0:T(8,128)S(1)}, f32[64,2048]{1,0:T(8,128)}, u32[]{:S(2)}) copy-start(f32[64,2048]{1,0:T(8,128)} %param.32) | copy-start | bytes 1572868
  314.1 5.7 %copy-start.10 = (f32[64,2048]{1,0:T(8,128)S(1)}, f32[64,2048]{1,0:T(8,128)}, u32[]{:S(2)}) copy-start(f32[64,2048]{1,0:T(8,128)} %param.31) | copy-start | bytes 1572868
  314.1 5.7 %copy-start.11 = (f32[64,2048]{1,0:T(8,128)S(1)}, f32[64,2048]{1,0:T(8,128)}, u32[]{:S(2)}) copy-start(f32[64,2048]{1,0:T(8,128)} %param.29) | copy-start | bytes 1572868
  319.8 2.3 copy-start.5
  319.8 4.7 %copy-start.2 = (f32[1024,1024]{1,0:T(8,128)S(1)}, f32[1024,1024]{1,0:T(8,128)}, u32[]{:S(2)}) copy-start(f32[1024,1024]{1,0:T(8,128)} %get-tuple-element.113) | copy-start | bytes 12582916
  322.1 6.7 %copy-start.1 = (s32[4,512]{1,0:T(4,128)S(1)}, s32[4,512]{1,0:T(4,128)}, u32[]{:S(2)}) copy-start(s32[4,512]{1,0:T(4,128)} %param.20) | copy-start | bytes 24580
  324.5 2.0 copy-start.13

commit v6 on v5

--- a/solution.py
+++ b/solution.py
@@ -1178,8 +1178,7 @@
         (7, (5073, 5072,)),
         (9, (5083, 5082, 5070,)),
         (11, (5080, 5090,)),
-        (14, (5092,)),
-        (15, (5103,)),
+        (14, (5092, 5103,)),
         (23, (5030, 5032,)),
     )),
     ("ln", (
@@ -1195,20 +1194,16 @@
     ("attn", (
         (0, (4081, 4072,)),
         (2, (4082, 3071, 3072,)),
-        (3, (4103, 3081, 3082, 3070, 3073, 5100,)),
-        (4, (4092, 3080, 3083, 4070,)),
-        (6, (4080,)),
-        (9, (3101, 4090,)),
-        (10, (3090, 4101,)),
-        (13, (4032, 3092,)),
-        (14, (3103,)),
+        (3, (4103, 3081, 3082, 3070, 3073, 5100, 4092, 3080, 3083, 4070,)),
+        (5, (4080,)),
+        (9, (3101, 4090, 3090, 4101,)),
+        (13, (4032, 3092, 3103,)),
     )),
     ("pq", (
         (0, (3032, 4030, 3030,)),
     )),
     ("pk", (
-        (0, (4102,)),
-        (1, (3102, 63, 61, 62, 60,)),
+        (0, (4102, 3102, 63, 61, 62, 60,)),
     )),
     ("pv", (
         (0, (73,)),
@@ -1219,10 +1214,10 @@
             1083, 2071, 32, 2062, 2083,)),
         (1, (1101, 30, 1090, 2081, 2072, 2070, 1092, 3100,)),
         (2, (2082, 2092, 1103, 2080, 102,)),
-        (3, (1030, 1032, 2090, 2103,)),
+        (3, (1030, 1032, 2090, 2103, 2101,)),
     )),
     ("end", (
-        (-1, (2101, 2032, 1102, 2030, 100, 2102, 1100, 2100,)),
+        (-1, (2032, 1102, 2030, 100, 2102, 1100, 2100,)),
     )),
 )
 

time: 330 us -> 325 us (0.985)
  Pallas kernels: 311 us -> 306 us
    pallas_call x1, Pallas kernels: 159 us -> 155 us  [run_backward(): pl.pallas_call(functools.partial(backward_kernel, nz), out_shape=[jax.Sha...]
where the time goes in v6:
time: 325 us
  Pallas kernels  306 us (94%)
  local copies, waits for them, and re-layouts  8.65 us (3%)
  other arithmetic  8.54 us (3%)
    pallas_call x1, Pallas kernels, run_backward(): pl.pallas_call(functools.partial(backward_kernel, nz), out_shape=[jax.Sha...  155 us
    pallas_call x1, Pallas kernels, run_forward(): pl.pallas_call(functools.partial(forward_kernel, nz), out_shape=[jax.Shap...  152 us
    sub x4, other arithmetic, adam_step(): updated = weight - step_rate * (normed + DECAY_RATE * weight)  7.85 us
    unnamed x51, local copies, waits for them, and re-layouts  6.79 us

profile of v6, /device:TPU:0, one launch (start us, length us, event | category | flops | bytes accessed | tf_op | source)
XLA Modules:
  0.0 324.5 jit_solution(9714887985017485871)
XLA Ops:
  0.7 0.0 copy-start
  0.7 0.7 convert_convert_fusion
  1.4 0.0 copy-done
  1.4 0.6 reshape.63.seg_row
  2.0 0.2 dynamic_update_slice.3.norm
  2.3 0.0 copy-start.17
  2.3 1.0 broadcast_in_dim.14.seg_col
  3.3 0.0 copy-done.17
  3.3 151.8 %forward.1 = (bf16[3,4,2,2,64,1024]{5,4,3,2,1,0:T(8,128)(2,1)}, bf16[4,2,2,64,1024]{4,3,2,1,0:T(8,128)(2,1)}, bf16[4,2,2,64,4096]{4,3,2,1,0:T(8,128)(2,1)}, bf16...) custom-call(bf16[2048,1024]{1,0:T(8,128)(2,1)} %tokens.3, ...), custom_call_target="tpu_custom_call" | custom-call | tf_op jit(solution)/shard_map/forward/pallas_call | solution.py:718
  155.1 0.0 copy-start.19
  155.1 0.0 copy-start.20
  155.1 0.0 copy-start.21
  155.1 0.0 copy-start.14
  155.1 0.0 copy-start.18
  155.2 0.0 copy-start.8
  155.2 0.0 copy-start.15
  155.2 0.0 copy-start.16
  155.2 0.0 copy-start.12
  155.2 154.6 %backward.1 = (f32[1024,1024]{1,0:T(8,128)}, f32[64,2048]{1,0:T(8,128)}, f32[64,2048]{1,0:T(8,128)}, f32[64,512]{1,0:T(8,128)}, f32[64,512]{1,0:T(8,128)}, /*ind...) custom-call(bf16[2048,1024]{1,0:T(8,128)(2,1)} %tokens.3, ...), custom_call_target="tpu_custom_call" | custom-call | tf_op jit(solution)/shard_map/backward/pallas_call | solution.py:1237
  309.8 0.0 copy-start.3
  309.8 0.0 copy-start.4
  309.8 0.0 copy-start.6
  309.8 0.0 copy-start.7
  309.8 0.0 copy-start.9
  309.9 0.0 copy-start.10
  309.9 0.0 copy-start.11
  309.9 0.0 copy-done.19
  309.9 0.0 copy-done.20
  309.9 0.0 copy-done.21
  309.9 1.5 multiply_subtract_fusion.4
  311.4 0.0 copy-done.14
  311.4 0.0 copy-done.18
  311.4 1.8 multiply_subtract_fusion.3
  313.2 0.0 copy-done.8
  313.2 0.0 copy-done.15
  313.2 0.0 copy-done.16
  313.2 2.3 multiply_subtract_fusion.2
  315.5 0.0 copy-start.5
  315.5 0.0 copy-done.12
  315.5 0.0 copy-done.3
  315.6 0.0 copy-done.4
  315.6 0.0 copy-done.6
  315.6 0.0 copy-done.7
  315.6 0.0 copy-done.9
  315.6 0.0 copy-done.10
  315.6 0.0 copy-done.11
  315.6 0.0 copy-start.2
  315.6 2.2 multiply_subtract_fusion
  317.9 0.0 copy-done.5
  317.9 0.0 copy-start.1
  317.9 1.3 copy.47
  319.2 1.1 copy-done.2
  320.3 0.0 copy-start.13
  320.3 2.0 copy.48
  322.3 0.0 copy-done.13
  322.3 0.7 copy.49
  322.9 0.8 copy.50
  323.7 0.8 copy.51
  324.5 0.0 copy-done.1
  (4 shorter events, 0.0 us)
Async XLA Ops:
  0.7 0.7 copy-start
  2.3 1.0 copy-start.17
  155.1 154.8 %copy-start.19 = (f32[4,32]{1,0:T(4,128)S(1)}, f32[4,32]{1,0:T(4,128)}, u32[]{:S(2)}) copy-start(f32[4,32]{1,0:T(4,128)} %param.33) | copy-start | bytes 1540
  155.1 154.8 %copy-start.20 = (f32[4,32]{1,0:T(4,128)S(1)}, f32[4,32]{1,0:T(4,128)}, u32[]{:S(2)}) copy-start(f32[4,32]{1,0:T(4,128)} %param.35) | copy-start | bytes 1540
  155.1 154.8 %copy-start.21 = (f32[4,32]{1,0:T(4,128)S(1)}, f32[4,32]{1,0:T(4,128)}, u32[]{:S(2)}) copy-start(f32[4,32]{1,0:T(4,128)} %param.34) | copy-start | bytes 1540
  155.1 156.3 %copy-start.14 = (f32[64,512]{1,0:T(8,128)S(1)}, f32[64,512]{1,0:T(8,128)}, u32[]{:S(2)}) copy-start(f32[64,512]{1,0:T(8,128)} %out.1) | copy-start | bytes 393220
  155.1 156.3 %copy-start.18 = (f32[64,512]{1,0:T(8,128)S(1)}, f32[64,512]{1,0:T(8,128)}, u32[]{:S(2)}) copy-start(f32[64,512]{1,0:T(8,128)} %param.26) | copy-start | bytes 393220
  155.2 158.0 %copy-start.8 = (f32[3,64,512]{2,1,0:T(8,128)S(1)}, f32[3,64,512]{2,1,0:T(8,128)}, u32[]{:S(2)}) copy-start(f32[3,64,512]{2,1,0:T(8,128)} %proj.1) | copy-start | bytes 1179652
  155.2 158.0 %copy-start.15 = (f32[3,64,512]{2,1,0:T(8,128)S(1)}, f32[3,64,512]{2,1,0:T(8,128)}, u32[]{:S(2)}) copy-start(f32[3,64,512]{2,1,0:T(8,128)} %param.23) | copy-start | bytes 1179652
  155.2 158.0 %copy-start.16 = (f32[3,64,512]{2,1,0:T(8,128)S(1)}, f32[3,64,512]{2,1,0:T(8,128)}, u32[]{:S(2)}) copy-start(f32[3,64,512]{2,1,0:T(8,128)} %param.22) | copy-start | bytes 1179652
  155.2 160.4 %copy-start.12 = (f32[64,2048]{1,0:T(8,128)S(1)}, f32[64,2048]{1,0:T(8,128)}, u32[]{:S(2)}) copy-start(f32[64,2048]{1,0:T(8,128)} %param.28) | copy-start | bytes 1572868
  309.8 5.7 %copy-start.3 = (f32[64,2048]{1,0:T(8,128)S(1)}, f32[64,2048]{1,0:T(8,128)}, u32[]{:S(2)}) copy-start(f32[64,2048]{1,0:T(8,128)} %get-tuple-element.126) | copy-start | bytes 1572868
  309.8 5.7 %copy-start.4 = (f32[64,2048]{1,0:T(8,128)S(1)}, f32[64,2048]{1,0:T(8,128)}, u32[]{:S(2)}) copy-start(f32[64,2048]{1,0:T(8,128)} %get-tuple-element.122) | copy-start | bytes 1572868
  309.8 5.7 %copy-start.6 = (f32[64,2048]{1,0:T(8,128)S(1)}, f32[64,2048]{1,0:T(8,128)}, u32[]{:S(2)}) copy-start(f32[64,2048]{1,0:T(8,128)} %up.1) | copy-start | bytes 1572868
  309.8 5.7 %copy-start.7 = (f32[64,2048]{1,0:T(8,128)S(1)}, f32[64,2048]{1,0:T(8,128)}, u32[]{:S(2)}) copy-start(f32[64,2048]{1,0:T(8,128)} %down.1) | copy-start | bytes 1572868
  309.8 5.7 %copy-start.9 = (f32[64,2048]{1,0:T(8,128)S(1)}, f32[64,2048]{1,0:T(8,128)}, u32[]{:S(2)}) copy-start(f32[64,2048]{1,0:T(8,128)} %param.32) | copy-start | bytes 1572868
  309.9 5.7 %copy-start.10 = (f32[64,2048]{1,0:T(8,128)S(1)}, f32[64,2048]{1,0:T(8,128)}, u32[]{:S(2)}) copy-start(f32[64,2048]{1,0:T(8,128)} %param.31) | copy-start | bytes 1572868
  309.9 5.7 %copy-start.11 = (f32[64,2048]{1,0:T(8,128)S(1)}, f32[64,2048]{1,0:T(8,128)}, u32[]{:S(2)}) copy-start(f32[64,2048]{1,0:T(8,128)} %param.29) | copy-start | bytes 1572868
  315.5 2.3 copy-start.5
  315.6 4.7 %copy-start.2 = (f32[1024,1024]{1,0:T(8,128)S(1)}, f32[1024,1024]{1,0:T(8,128)}, u32[]{:S(2)}) copy-start(f32[1024,1024]{1,0:T(8,128)} %get-tuple-element.113) | copy-start | bytes 12582916
  317.9 6.7 %copy-start.1 = (s32[4,512]{1,0:T(4,128)S(1)}, s32[4,512]{1,0:T(4,128)}, u32[]{:S(2)}) copy-start(s32[4,512]{1,0:T(4,128)} %param.20) | copy-start | bytes 24580
  320.3 2.0 copy-start.13
